TPU v7x, 256 devices: a whole 4x4x8 slice. The times are simulated.
256 devices in a mesh: gx: 32 (over z, x), gy: 8 (over y, core).
Axes of the slice: x: 4, y: 4, z: 8, core: 2. Of those that a mesh axis runs over, the one named last changes fastest.
Arguments:
- body_force: float32 [3, 512, 256, 128], P(None, 'gx', 'gy'), may hold values from -30 to 30, as said below
- fixed_dofs: int32 [3, 512, 256, 128], P(None, 'gx', 'gy'), may hold values 0 or 1
- load_nodes: int32 [512, 3], replicated, may hold values from 0 to 511, as said below
- load_forces: float32 [3, 512], replicated, may hold values from -32 to 32
- frequencies: float32 [3, 64], replicated, may hold values from -24 to 24
- hidden_weights: float32 [3, 128, 128], replicated, may hold values from -0.5 to 0.5
- hidden_biases: float32 [3, 128], replicated, may hold values from -6 to 6
- output_weights: float32 [128], replicated, may hold values from -3 to 3
- output_bias: float32 [1], replicated, may hold values from -3 to 3
Outputs:
- displacement: float32 [3, 512, 256, 128], P(None, 'gx', 'gy')
- density: float32 [512, 256, 128], P('gx', 'gy')
Inputs may be any that keep to these rules, and one draw needn't show every extreme that they name: `load_nodes`: row p gives the x, y and z index of point load p's node: column 0 below 512, column 1 below 256, column 2 below 128; several loads may share a node. `body_force`: finite values of order one to ten.
All inputs are finite; a program needn't handle non-finite values. No bound on the sum of `fixed_dofs` on one device may be relied on, other than what follows from the above.
Results may differ from a plain program's by a relative error of at most 0.00013.
Values sent between devices are 32-bit elements; how exact they have to be, the bound alone decides.
No kernel may reach another device: no remote copies, remote signals or barrier semaphores. Data moves between devices by JAX's collectives and lax.ppermute only.
A program may use at most 128 MiB of HBM per device.

v0:
```python
import math

import jax
import jax.numpy as jnp
import numpy as np
from jax import lax
from jax.sharding import PartitionSpec as P

CF = 4
ITERS = 2


full_turn = 2.0 * math.pi
highest = lax.Precision.HIGHEST


def extended(array, sides, width):
    for axis, dim in sides:
        count, length = (lax.axis_size(axis), array.shape[dim])
        up = [(i, (i + 1) % count) for i in range(count - 1)]
        down = [(j, i) for i, j in up]
        last = lax.slice_in_dim(array, length - width, length, axis=dim)
        leading = lax.slice_in_dim(array, 0, width, axis=dim)
        before = lax.ppermute(last, axis, up)
        after = lax.ppermute(leading, axis, down)
        array = jnp.concatenate([before, array, after], axis=dim)
    return array


def element_stiffness():
    poisson = 0.3
    lame_first = poisson / ((1.0 + poisson) * (1.0 - 2.0 * poisson))
    lame_second = 1.0 / (2.0 * (1.0 + poisson))
    elastic = np.zeros((6, 6))
    elastic[:3, :3] = lame_first
    elastic[np.arange(3), np.arange(3)] += 2.0 * lame_second
    elastic[np.arange(3, 6), np.arange(3, 6)] = lame_second
    gauss = 1.0 / math.sqrt(3.0)
    stiffness = np.zeros((24, 24))
    for point in range(8):
        where_at = [gauss * (2 * (point >> which & 1) - 1) for which in range(3)]
        strain = np.zeros((6, 24))
        for corner in range(8):
            signs = [2 * (corner >> which & 1) - 1 for which in range(3)]
            slopes = []
            for which in range(3):
                value = 0.25 * signs[which]
                for other in range(3):
                    if other != which:
                        value = value * (1.0 + signs[other] * where_at[other])
                slopes.append(value)
            column = 3 * corner
            strain[0, column] = slopes[0]
            strain[1, column + 1] = slopes[1]
            strain[2, column + 2] = slopes[2]
            strain[3, column] = slopes[1]
            strain[3, column + 1] = slopes[0]
            strain[4, column + 1] = slopes[2]
            strain[4, column + 2] = slopes[1]
            strain[5, column] = slopes[2]
            strain[5, column + 2] = slopes[0]
        stiffness = stiffness + strain.T @ elastic @ strain * 0.125
    return jnp.asarray(stiffness, dtype=jnp.float32)


def corner_offsets(corner):
    return (corner & 1, corner >> 1 & 1, corner >> 2 & 1)


def z_shift(values, offset):
    widths = [(0, 0)] * (values.ndim - 1)
    if offset > 0:
        return jnp.pad(values[..., 1:], widths + [(0, 1)])
    return jnp.pad(values[..., :-1], widths + [(1, 0)])


def coarse_density(
    begin_x,
    begin_y,
    count_x,
    count_y,
    count_z,
    total_x,
    total_y,
    total_z,
    frequencies,
    hidden_weights,
    hidden_biases,
    output_weights,
    output_bias,
):
    along_x = ((begin_x + jnp.arange(count_x, dtype=jnp.int32)).astype(jnp.float32) + 0.5) / float(
        total_x
    )
    along_y = ((begin_y + jnp.arange(count_y, dtype=jnp.int32)).astype(jnp.float32) + 0.5) / float(
        total_y
    )
    along_z = (jnp.arange(count_z, dtype=jnp.int32).astype(jnp.float32) + 0.5) / float(total_z)
    grid_shape = (count_x, count_y, count_z)
    centres = jnp.stack(
        [
            jnp.broadcast_to(along_x[:, None, None], grid_shape).reshape(-1),
            jnp.broadcast_to(along_y[None, :, None], grid_shape).reshape(-1),
            jnp.broadcast_to(along_z[None, None, :], grid_shape).reshape(-1),
        ],
        axis=0,
    )
    phases = (
        jnp.dot(frequencies.T, centres, precision=highest, preferred_element_type=jnp.float32)
        * full_turn
    )
    hidden = jnp.concatenate([jnp.sin(phases), jnp.cos(phases)], axis=0)
    for layer in range(hidden_weights.shape[0]):
        mixed = jnp.dot(
            hidden_weights[layer].T, hidden, precision=highest, preferred_element_type=jnp.float32
        )
        hidden = jax.nn.silu(mixed + hidden_biases[layer][:, None])
    logits = (
        jnp.dot(output_weights, hidden, precision=highest, preferred_element_type=jnp.float32)
        + output_bias[0]
    )
    return jax.nn.sigmoid(logits).reshape(grid_shape)


def upsample(coarse):
    across, along, height = coarse.shape
    spread = jnp.broadcast_to(
        coarse[:, None, :, None, :, None], (across, CF, along, CF, height, CF)
    )
    return spread.reshape(across * CF, along * CF, height * CF)


def inside_mask(begin_x, begin_y, count_x, count_y, height, total_x, total_y):
    index_x = begin_x + jnp.arange(count_x, dtype=jnp.int32)
    index_y = begin_y + jnp.arange(count_y, dtype=jnp.int32)
    valid_x = (index_x >= 0) & (index_x < total_x)
    valid_y = (index_y >= 0) & (index_y < total_y)
    inside = (valid_x[:, None, None] & valid_y[None, :, None]).astype(jnp.float32)
    return jnp.broadcast_to(inside, (count_x, count_y, height))


def cone_filter(padded, count_x, count_y):
    result = jnp.zeros((count_x, count_y, padded.shape[2]), jnp.float32)
    for shift_x in (-1, 0, 1):
        for shift_y in (-1, 0, 1):
            for shift_z in (-1, 0, 1):
                weight = 2.0 - math.sqrt(shift_x * shift_x + shift_y * shift_y + shift_z * shift_z)
                piece = padded[
                    1 + shift_x : 1 + shift_x + count_x, 1 + shift_y : 1 + shift_y + count_y
                ]
                if shift_z != 0:
                    piece = z_shift(piece, shift_z)
                result = result + weight * piece
    return result


def corner_products(nodes, young, stiffness):
    across, along, height = young.shape
    pieces = []
    for corner in range(8):
        off_x, off_y, off_z = corner_offsets(corner)
        piece = nodes[:, off_x : off_x + across, off_y : off_y + along]
        if off_z:
            piece = z_shift(piece, 1)
        pieces.append(piece)
    stacked = jnp.concatenate(pieces, axis=0).reshape(24, across * along * height)
    products = jnp.dot(stiffness, stacked, precision=highest, preferred_element_type=jnp.float32)
    return products.reshape(24, across, along, height) * young[None]


def interior_forces(products):
    across, along = (products.shape[1], products.shape[2])
    result = jnp.zeros((3, across - 1, along - 1, products.shape[3]), jnp.float32)
    for corner in range(8):
        off_x, off_y, off_z = corner_offsets(corner)
        piece = products[
            3 * corner : 3 * corner + 3, 1 - off_x : across - off_x, 1 - off_y : along - off_y
        ]
        if off_z:
            piece = z_shift(piece, -1)
        result = result + piece
    return result


def recompute_forces(nodes_ext, young_ext, stiffness):
    planes = nodes_ext.shape[1] - 2
    count = planes // CF

    def block(index):
        begin = index * CF
        nodes_block = lax.dynamic_slice_in_dim(nodes_ext, begin, CF + 2, 1)
        young_block = lax.dynamic_slice_in_dim(young_ext, begin, CF + 1, 0)
        return interior_forces(corner_products(nodes_block, young_block, stiffness))

    blocks = lax.map(block, jnp.arange(count, dtype=jnp.int32))
    return jnp.moveaxis(blocks, 0, 1).reshape(3, planes, nodes_ext.shape[2] - 2, nodes_ext.shape[3])


def stiffness_diagonal(young_ext, stiffness):
    across, along = (young_ext.shape[0] - 1, young_ext.shape[1] - 1)
    entries = jnp.diagonal(stiffness)
    result = jnp.zeros((3, across, along, young_ext.shape[2]), jnp.float32)
    for corner in range(8):
        off_x, off_y, off_z = corner_offsets(corner)
        piece = young_ext[1 - off_x : 1 - off_x + across, 1 - off_y : 1 - off_y + along]
        if off_z:
            piece = z_shift(piece, -1)
        result = result + entries[3 * corner : 3 * corner + 3][:, None, None, None] * piece[None]
    return result


def per_device(
    body_force,
    fixed_dofs,
    load_nodes,
    load_forces,
    frequencies,
    hidden_weights,
    hidden_biases,
    output_weights,
    output_bias,
):
    stiffness = element_stiffness()
    cells_x, cells_y, height = (body_force.shape[1], body_force.shape[2], body_force.shape[3])
    total_x = cells_x * lax.axis_size("gx")
    total_y = cells_y * lax.axis_size("gy")
    block_x = lax.axis_index("gx")
    block_y = lax.axis_index("gy")
    start_x = block_x * cells_x
    start_y = block_y * cells_y
    network = (frequencies, hidden_weights, hidden_biases, output_weights, output_bias)
    inside_raw = inside_mask(
        start_x - 2, start_y - 2, cells_x + 4, cells_y + 4, height, total_x, total_y
    )
    own_coarse = coarse_density(
        block_x * (cells_x // CF),
        block_y * (cells_y // CF),
        cells_x // CF,
        cells_y // CF,
        height // CF,
        total_x // CF,
        total_y // CF,
        height // CF,
        *network
    )
    raw_padded = extended(upsample(own_coarse), (("gx", 0), ("gy", 1)), 2)
    filtered = cone_filter(raw_padded, cells_x + 1, cells_y + 1) / cone_filter(
        inside_raw, cells_x + 1, cells_y + 1
    )
    density = filtered[1:, 1:]
    inside_elements = inside_raw[1 : cells_x + 2, 1 : cells_y + 2]
    young_ext = (0.02 + 0.98 * filtered**3) * inside_elements
    free_dofs = 1.0 - fixed_dofs.astype(jnp.float32)
    jacobi = free_dofs * stiffness_diagonal(young_ext, stiffness) + (1.0 - free_dofs)
    local_x = load_nodes[:, 0] - start_x
    local_y = load_nodes[:, 1] - start_y
    mine = (local_x >= 0) & (local_x < cells_x) & (local_y >= 0) & (local_y < cells_y)
    index_x = jnp.where(mine, local_x, cells_x)
    index_y = jnp.where(mine, local_y, 0)
    loaded = body_force.at[:, index_x, index_y, load_nodes[:, 2]].add(load_forces, mode="drop")
    rhs = free_dofs * loaded
    displacement = jnp.zeros_like(rhs)
    residual = rhs
    scaled = residual / jacobi

    def scaled_norm(residual_now, scaled_now):
        return lax.psum(jnp.sum(residual_now * scaled_now), ("gx", "gy"))

    direction = scaled
    norm_now = scaled_norm(residual, scaled)
    for iteration in range(ITERS):
        padded = extended(direction, (("gx", 1), ("gy", 2)), 1)
        forces = recompute_forces(padded, young_ext, stiffness)
        image = free_dofs * forces
        alpha = norm_now / lax.psum(jnp.sum(direction * image), ("gx", "gy"))
        displacement = displacement + alpha * direction
        residual = residual - alpha * image
        if iteration + 1 < ITERS:
            scaled = residual / jacobi
            norm_next = scaled_norm(residual, scaled)
            direction = scaled + norm_next / norm_now * direction
            norm_now = norm_next
    return (displacement, density)


def solution(mesh):
    return jax.shard_map(
        per_device,
        mesh=mesh,
        in_specs=(
            P(None, "gx", "gy", None),
            P(None, "gx", "gy", None),
            P(),
            P(),
            P(),
            P(),
            P(),
            P(),
            P(),
        ),
        out_specs=(P(None, "gx", "gy", None), P("gx", "gy", None)),
        check_vma=False,
    )
```

profile of v0, /device:TPU:1, one launch (start us, length us, event | category | flops | bytes accessed | tf_op | source)
XLA Modules:
  0.0 550.1 jit_solution(15720621203659905396)
XLA Ops:
  2.5 3.1 sine_bitcast_fusion
  5.6 1.8 fusion.14
  11.2 4.4 broadcast_in_dim.95
  15.6 8.2 %reshape.131 = f32[16,32,128]{2,1,0:T(8,128)S(1)} reshape(f32[4,4,8,4,32,4]{5,4,3,2,1,0:T(8,128)} %broadcast_in_dim.95) | data formatting | bytes 524288 | tf_op jit(solution)/shard_map/reshape | solution.py:130
  23.9 3.9 collective-permute-start
  30.2 2.3 collective-permute-done.1
  32.5 5.2 collective-permute-start.2
  37.8 16.6 %copy.50 = f32[3,16,32,128]{0,3,2,1:T(8,128)} copy(f32[3,16,32,128]{3,2,1,0:T(8,128)S(1)} %copy-done.17) | data formatting | bytes 1572864 | tf_op args[0]
  54.6 50.0 %scatter_fusion = f32[3,16,32,128]{0,3,2,1:T(8,128)} fusion(f32[3,16,32,128]{0,3,2,1:T(8,128)} %copy.50, s32[512]{0:T(512)S(1)} %bitcast.72, f32[512,3]{1,0:T(8,128)S(1)} %copy.51), kind=kCustom, calls=%fused_computation.1 | custom fusion | flops 1536 | bytes 24576 | tf_op jit(solution)/shard_map/scatter-add | solution.py:260
  104.6 19.5 %copy.52 = f32[3,16,32,128]{3,2,1,0:T(8,128)S(1)} copy(f32[3,16,32,128]{0,3,2,1:T(8,128)} %scatter_fusion) | data formatting | bytes 1572864 | tf_op jit(solution)/shard_map/scatter-add | solution.py:260
  124.1 2.1 collective-permute-start.3
  126.7 2.4 collective-permute-done.3
  131.0 4.2 fusion.38
  139.2 4.0 collective-permute-start.4
  144.4 1.9 collective-permute-start.7
  146.3 3.6 collective-permute-start.6
  152.1 63.0 %while.26 = (s32[]{:T(128)}, f32[4,3,4,32,128]{4,3,2,1,0:T(8,128)}, s32[4]{0:T(128)S(1)}, f32[3,18,34,128]{3,2,1,0:T(8,128)S(1)}, f32[17,33,128]{2,1,0:T(8,128)S...) while((s32[]{:T(128)}, f32[4,3,4,32,128]{4,3,2,1,0:T(8,128)}, ...), condition=%wide.region_4.5_spmd.clone, body=%wide.region_3.4_spmd.sunk.clone.sunk | while | flops 146832384 | bytes 33809276 | solution.py:195
  159.8 1.8 reshape.160
  161.6 3.1 fusion.152
  164.7 1.7 reshape.161
  175.6 1.8 reshape.160
  177.4 3.1 fusion.152
  180.4 1.7 reshape.161
  191.3 1.8 reshape.160
  193.1 3.1 fusion.152
  196.2 1.7 reshape.161
  207.0 1.8 reshape.160
  208.8 3.1 fusion.152
  211.9 1.7 reshape.161
  216.4 2.6 multiply_reduce_fusion.2
  219.0 87.5 %all-reduce.56 = (f32[]{:T(128)}, f32[]{:T(128)}) all-reduce(f32[]{:T(128)} %get-tuple-element.221, f32[]{:T(128)} %get-tuple-element.220), channel_id=1, replica_groups=mesh['gx'=32,'gy'=8] {'gx','gy'}, use_global_device_ids=true, to_apply=%region_2.3 | all-reduce | flops 2 | bytes 16 | tf_op jit(solution)/shard_map/psum | solution.py:267
  307.8 2.9 multiply_reduce_fusion.1
  310.7 74.6 %psum.30 = f32[]{:T(128)} all-reduce(f32[]{:T(128)} %get-tuple-element.244), channel_id=1, replica_groups=mesh['gx'=32,'gy'=8] {'gx','gy'}, use_global_device_ids=true, to_apply=%region_8.9 | all-reduce | flops 1 | bytes 8 | tf_op jit(solution)/shard_map/psum | solution.py:267
  389.2 4.0 collective-permute-start.8
  394.4 3.7 collective-permute-start.11
  398.1 2.6 collective-permute-start.10
  402.6 62.8 %while.27 = (s32[]{:T(128)}, f32[4,3,4,32,128]{4,3,2,1,0:T(8,128)}, s32[4]{0:T(128)S(1)}, f32[3,18,34,128]{3,2,1,0:T(8,128)S(1)}, f32[17,33,128]{2,1,0:T(8,128)S...) while((s32[]{:T(128)}, f32[4,3,4,32,128]{4,3,2,1,0:T(8,128)}, ...), condition=%wide.region_10.11_spmd.clone, body=%wide.region_9.10_spmd.sunk.clone.sunk | while | flops 146832384 | bytes 33809276 | solution.py:195
  410.3 1.8 reshape.162
  412.1 3.1 fusion.157
  415.2 1.7 reshape.163
  426.0 1.8 reshape.162
  427.8 3.1 fusion.157
  441.7 1.8 reshape.162
  443.5 3.1 fusion.157
  457.4 1.8 reshape.162
  459.2 3.1 fusion.157
  466.8 2.2 multiply_reduce_fusion
  469.8 77.9 %psum.31 = f32[]{:T(128)} all-reduce(f32[]{:T(128)} %multiply_reduce_fusion), channel_id=1, replica_groups=mesh['gx'=32,'gy'=8] {'gx','gy'}, use_global_device_ids=true, to_apply=%region_12.13 | all-reduce | flops 1 | bytes 8 | tf_op jit(solution)/shard_map/psum | solution.py:275
  (256 shorter events, 100.1 us)
Async XLA Ops:
  0.6 1.9 copy-start
  7.5 3.0 copy-start.20
  15.6 13.5 %copy-start.19 = (s32[512,3]{0,1:T(4,128)S(1)}, s32[512,3]{0,1:T(4,128)}, u32[]{:S(2)}) copy-start(s32[512,3]{0,1:T(4,128)} %param.16) | copy-start | bytes 18436
  15.6 13.8 %copy-start.6 = (f32[24,24]{1,0:T(8,128)S(1)}, f32[24,24]{1,0:T(8,128)}, u32[]{:S(2)}) copy-start(f32[24,24]{1,0:T(8,128)} %constant.148.clone) | copy-start | bytes 6916
  15.6 22.2 %copy-start.17 = (f32[3,16,32,128]{3,2,1,0:T(8,128)S(1)}, f32[3,16,32,128]{3,2,1,0:T(8,128)}, u32[]{:S(2)}) copy-start(f32[3,16,32,128]{3,2,1,0:T(8,128)} %param.14) | copy-start | bytes 2359300
  23.9 6.3 %collective-permute-start = (f32[2,32,128]{2,1,0:T(8,128)S(1)}, f32[2,32,128]{2,1,0:T(8,128)S(1)}, u32[]{:S(2)}, u32[]{:S(2)}) collective-permute-start(f32[2,32,128]{2,1,0:T(8,128)S(1)} %get-tuple-element.306), channel_id=1, source_target_pairs={{0,8},{8,16},{16,24},{24,32},{32,40},{40,48},{48,56},{56,64},{64,7... | collective-permute-start | bytes 98312 | tf_op jit(solution)/shard_map/ppermute | solution.py:24
  27.8 4.7 collective-permute-start.1
  32.5 93.7 %collective-permute-start.2 = (f32[20,2,128]{2,1,0:T(2,128)S(1)}, f32[20,2,128]{2,1,0:T(2,128)S(1)}, u32[]{:S(2)}, u32[]{:S(2)}) collective-permute-start(f32[20,2,128]{2,1,0:T(2,128)S(1)} %get-tuple-element.303), channel_id=1, source_target_pairs={{0,1},{1,2},{2,3},{3,4},{4,5},{5,6},{6,7},{8,9},{9,10},{10,11},{11... | collective-permute-start | bytes 61448 | tf_op jit(solution)/shard_map/ppermute | solution.py:24
  37.8 16.6 %copy-start.18 = (f32[3,512]{1,0:T(4,128)S(1)}, f32[3,512]{1,0:T(4,128)}, u32[]{:S(2)}) copy-start(f32[3,512]{1,0:T(4,128)} %param.17) | copy-start | bytes 18436
  124.1 11.8 %copy-start.14 = (f32[3,16,32,128]{3,2,1,0:T(8,128)}, f32[3,16,32,128]{3,2,1,0:T(8,128)S(1)}, u32[]{:S(2)}) copy-start(f32[3,16,32,128]{3,2,1,0:T(8,128)S(1)} %copy.52) | copy-start | bytes 2359300
  124.1 5.1 collective-permute-start.3
  135.2 1.1 copy-start.12
  137.9 14.2 %copy-start.7 = (f32[3,16,32,128]{3,2,1,0:T(8,128)}, f32[3,16,32,128]{3,2,1,0:T(8,128)S(1)}, u32[]{:S(2)}) copy-start(f32[3,16,32,128]{3,2,1,0:T(8,128)S(1)} %get-tuple-element.246) | copy-start | bytes 2359300
  137.9 5.3 collective-permute-start.5
  139.2 5.2 collective-permute-start.4
  144.4 5.6 %collective-permute-start.7 = (f32[3,18,1,128]{3,2,1,0:T(1,128)S(1)}, f32[3,18,1,128]{3,2,1,0:T(1,128)S(1)}, u32[]{:S(2)}, u32[]{:S(2)}) collective-permute-start(f32[3,18,1,128]{3,2,1,0:T(1,128)S(1)} %get-tuple-element.269), channel_id=1, source_target_pairs={{1,0},{2,1},{3,2},{4,3},{5,4},{6,5},{7,6},{9,8},{10,9},{11,10},{12... | collective-permute-start | bytes 82952 | tf_op jit(solution)/shard_map/ppermute | solution.py:25
  146.3 4.6 collective-permute-start.6
  152.1 4.7 copy-start.4
  166.6 1.2 copy-start.5
  167.8 4.7 copy-start.4
  182.3 1.2 copy-start.5
  183.6 4.7 copy-start.4
  198.1 1.2 copy-start.5
  199.3 4.7 copy-start.4
  213.8 1.2 copy-start.5
  215.1 92.7 %copy-start.13 = (s32[3,16,32,128]{3,2,1,0:T(8,128)S(1)}, s32[3,16,32,128]{3,2,1,0:T(8,128)}, u32[]{:S(2)}) copy-start(s32[3,16,32,128]{3,2,1,0:T(8,128)} %param.15) | copy-start | bytes 2359300
  215.1 92.7 %copy-start.15 = (f32[3,16,32,128]{3,2,1,0:T(8,128)S(1)}, f32[3,16,32,128]{3,2,1,0:T(8,128)}, u32[]{:S(2)}) copy-start(f32[3,16,32,128]{3,2,1,0:T(8,128)} %copy-done.14) | copy-start | bytes 2359300
  219.0 167.6 %copy-start.8 = (f32[3,16,32,128]{3,2,1,0:T(8,128)S(1)}, f32[3,16,32,128]{3,2,1,0:T(8,128)}, u32[]{:S(2)}) copy-start(f32[3,16,32,128]{3,2,1,0:T(8,128)} %copy-done.7) | copy-start | bytes 2359300
  387.9 14.7 %copy-start.10 = (f32[3,16,32,128]{3,2,1,0:T(8,128)}, f32[3,16,32,128]{3,2,1,0:T(8,128)S(1)}, u32[]{:S(2)}) copy-start(f32[3,16,32,128]{3,2,1,0:T(8,128)S(1)} %multiply_add_fusion.1) | copy-start | bytes 2359300
  387.9 5.3 collective-permute-start.9
  389.2 5.2 collective-permute-start.8
  394.4 6.3 %collective-permute-start.11 = (f32[3,18,1,128]{3,2,1,0:T(1,128)S(1)}, f32[3,18,1,128]{3,2,1,0:T(1,128)S(1)}, u32[]{:S(2)}, u32[]{:S(2)}) collective-permute-start(f32[3,18,1,128]{3,2,1,0:T(1,128)S(1)} %get-tuple-element.267), channel_id=1, source_target_pairs={{1,0},{2,1},{3,2},{4,3},{5,4},{6,5},{7,6},{9,8},{10,9},{11,10},{12... | collective-permute-start | bytes 82952 | tf_op jit(solution)/shard_map/ppermute | solution.py:25
  398.1 3.3 collective-permute-start.10
  402.6 4.7 copy-start.2
  417.1 1.2 copy-start.3
  418.3 4.7 copy-start.2
  432.8 1.2 copy-start.3
  434.0 4.7 copy-start.2
  448.5 1.2 copy-start.3
  449.7 4.7 copy-start.2
  464.2 1.2 copy-start.3
  465.5 3.6 copy-start.16
  465.5 83.6 %copy-start.9 = (f32[3,16,32,128]{3,2,1,0:T(8,128)S(1)}, f32[3,16,32,128]{3,2,1,0:T(8,128)}, u32[]{:S(2)}) copy-start(f32[3,16,32,128]{3,2,1,0:T(8,128)} %copy-done.7) | copy-start | bytes 2359300
  465.5 83.6 %copy-start.11 = (f32[3,16,32,128]{3,2,1,0:T(8,128)S(1)}, f32[3,16,32,128]{3,2,1,0:T(8,128)}, u32[]{:S(2)}) copy-start(f32[3,16,32,128]{3,2,1,0:T(8,128)} %copy-done.10) | copy-start | bytes 2359300
  466.8 83.3 %copy-start.1 = (f32[3,64]{1,0:T(4,128)S(1)}, f32[3,64]{1,0:T(4,128)}, u32[]{:S(2)}) copy-start(f32[3,64]{1,0:T(4,128)} %param.18) | copy-start | bytes 2308
where the time goes:
time: 554 us; the launch traced here: 550 us
  blocking collectives  240 us (43%)
  local copies, waits for them, and re-layouts  145 us (26%)
  other arithmetic  76.5 us (14%)
  starting transfers between devices  34.9 us (6%)
  matrix products  33.1 us (6%)
  waiting for transfers between devices  8.66 us (2%)
  between operations  5.87 us (1%)
  loops' own time  5.64 us (1%)
    psum x2, blocking collectives, scaled_norm(): return lax.psum(jnp.sum(residual_now * scaled_now), ('gx', 'gy'))  162 us
    psum x1, blocking collectives, per_device(): alpha = norm_now / lax.psum(jnp.sum(direction * image), ('gx', 'gy'))  77.9 us
    scatter-add x1, other arithmetic, per_device(): body_force.at[:, index_x, index_y, load_nodes[:, 2]]  50 us
    while x88, local copies, waits for them, and re-layouts  43.3 us
    dot_general x8, matrix products, corner_products(): jnp.dot(stiffness, stacked, precision=highest, preferred_element_type=jnp...  24.6 us
    ppermute x6, starting transfers between devices, extended(): before = lax.ppermute(last, axis, up)  23.3 us
    scatter-add x1, local copies, waits for them, and re-layouts, per_device(): body_force.at[:, index_x, index_y, load_nodes[:, 2]]  19.5 us
    unnamed x38, local copies, waits for them, and re-layouts  17.3 us
  transfers between devices with their start and end apart: 12, of which 6 were waited for; matrix products, arithmetic and copies ran while one was open for 16% of the time, Pallas kernels for 0%

commit v1 on v0

v1 whole, which is shorter than its diff:
```python
import functools
import math

import jax
import jax.numpy as jnp
from jax import lax
from jax.experimental import pallas as pl
from jax.experimental.pallas import tpu as pltpu
from jax.sharding import PartitionSpec as P

CF = 4
NX, NY, NZ = 16, 32, 128
TOTAL_X, TOTAL_Y = 512, 256
CX, CY, CZ = NX // CF, NY // CF, NZ // CF
GX, GY = CX + 2, CY + 2
EX, EY = GX * CF, GY * CF
SIZE = EX * EY
LOADS = 512
NU, MU = 0.3, 1.0 / 2.6
LAM = 0.3 / (1.3 * 0.4)
RATIO = LAM / MU
DIAG = (LAM + 4.0 * MU) / 9.0
VMEM = pltpu.VMEM
SMEM = pltpu.SMEM
highest = lax.Precision.HIGHEST
f32 = jnp.float32


def spec(space=VMEM):
    return pl.BlockSpec(memory_space=space)


def call(kernel, out_shape, in_spaces, args, scratch=(), cost=None):
    return pl.pallas_call(
        kernel,
        out_shape=out_shape,
        in_specs=[spec(s) for s in in_spaces],
        out_specs=jax.tree.map(lambda _: spec(), out_shape),
        scratch_shapes=list(scratch),
        compiler_params=pltpu.CompilerParams(vmem_limit_bytes=48 << 20),
        cost_estimate=cost,
    )(*args)


def shape(*dims):
    return jax.ShapeDtypeStruct(dims, f32)


def pack_kernel(ids, nodes_s, forces_s, body, fixed, nodes_v, r_out, lo_out, hi_out):
    start_x = ids[0] * NX
    start_y = ids[1] * NY
    r_out[...] = body[...]
    lx = nodes_v[0:1, :] - start_x
    ly = nodes_v[1:2, :] - start_y
    mine = (lx >= 0) & (lx < NX) & (ly >= 0) & (ly < NY)
    index = lax.broadcasted_iota(jnp.int32, (1, LOADS), 1)
    todo = jnp.where(mine, index, LOADS)
    lane = lax.broadcasted_iota(jnp.int32, (1, NZ), 1)

    def more(p):
        return p < LOADS

    def add_one(p):
        x = nodes_s[0, p] - start_x
        y = nodes_s[1, p] - start_y
        hit = lane == nodes_s[2, p]
        for c in range(3):
            row = pl.ds((c * NX + x) * NY + y, 1)
            r_out[row, :] = r_out[row, :] + jnp.where(hit, forces_s[c, p], 0.0)
        return jnp.min(jnp.where(todo > p, todo, LOADS))

    lax.while_loop(more, add_one, jnp.min(todo))

    def mask(i, carry):
        rows = pl.ds(pl.multiple_of(i * NY, NY), NY)
        r_out[rows, :] = jnp.where(fixed[rows, :] == 0, r_out[rows, :], 0.0)
        return carry

    lax.fori_loop(0, 3 * NX, mask, 0, unroll=4)
    for c in range(3):
        for j in range(2):
            lo_out[pl.ds((c * 2 + j) * NX, NX), :] = r_out[pl.ds(c * NX * NY + j, NX, stride=NY), :]
            hi_out[pl.ds((c * 2 + j) * NX, NX), :] = r_out[
                pl.ds(c * NX * NY + NY - 2 + j, NX, stride=NY), :
            ]
        free = fixed[pl.ds(c * NX * NY, NX, stride=NY), :] == 0
        lo_out[pl.ds((6 + c) * NX, NX), :] = jnp.where(free, 1.0, 0.0)
        free = fixed[pl.ds(c * NX * NY + NY - 1, NX, stride=NY), :] == 0
        hi_out[pl.ds((6 + c) * NX, NX), :] = jnp.where(free, 1.0, 0.0)


def planes_kernel(r, fixed, ylo, yhi, lo_out, hi_out):
    for out, first in ((lo_out, 0), (hi_out, NX - 2)):
        out[...] = jnp.zeros_like(out)
        for c in range(3):
            for j in range(2):
                x = first + j
                base = (c * 2 + j) * EY
                out[pl.ds(base + 4, NY), :] = r[pl.ds((c * NX + x) * NY, NY), :]
                for k in range(2):
                    out[pl.ds(base + 2 + k, 1), :] = ylo[pl.ds((c * 2 + k) * NX + x, 1), :]
                    out[pl.ds(base + 36 + k, 1), :] = yhi[pl.ds((c * 2 + k) * NX + x, 1), :]
            x = 0 if first == 0 else NX - 1
            base = (6 + c) * EY
            free = fixed[pl.ds((c * NX + x) * NY, NY), :] == 0
            out[pl.ds(base + 4, NY), :] = jnp.where(free, 1.0, 0.0)
            out[pl.ds(base + 3, 1), :] = ylo[pl.ds((6 + c) * NX + x, 1), :]
            out[pl.ds(base + 36, 1), :] = yhi[pl.ds((6 + c) * NX + x, 1), :]


def split2(v):
    hi = v.astype(jnp.bfloat16)
    return hi, (v - hi.astype(f32)).astype(jnp.bfloat16)


def sigmoid(v):
    return 1.0 / (1.0 + jnp.exp(-v))


def mlp_kernel(ids, freq, weights, biases, wout, bout, coarse, axy, bxy, w2):
    cx0 = ids[0] * CX - 1
    cy0 = ids[1] * CY - 1
    f = freq[...]
    ff = jnp.concatenate([f, f], axis=1)
    quarter = jnp.where(lax.broadcasted_iota(jnp.int32, (1, 128), 1) < 64, 0.0, 0.25)

    def waves(row, coords):
        turns = ff[row : row + 1, :] * coords
        turns = turns - jnp.round(turns)
        wave = jnp.sin((turns + quarter) * (2.0 * math.pi))
        other = jnp.sin((turns + (0.25 - quarter)) * (2.0 * math.pi))
        return wave, other

    def coords(start, rows, total):
        i = lax.broadcasted_iota(jnp.int32, (rows, 128), 0) + start
        return (i.astype(f32) + 0.5) * (1.0 / total)

    first = lax.broadcasted_iota(jnp.int32, (1, 128), 1) < 64
    wx, ox = waves(0, coords(cx0, 8, TOTAL_X // CF))
    wy, oy = waves(1, coords(cy0, 16, TOTAL_Y // CF))
    wz, oz = waves(2, coords(0, CZ, CZ))
    cosx, sinx = jnp.where(first, ox, wx), jnp.where(first, wx, ox)
    cosz, sinz = jnp.where(first, oz, wz), jnp.where(first, wz, oz)
    turnedy = jnp.where(first, oy, -oy)
    cosy, siny = jnp.where(first, oy, wy), jnp.where(first, wy, oy)
    for i in range(GX):
        both = wy * cosx[i : i + 1, :] + turnedy * sinx[i : i + 1, :]
        axy[pl.ds(16 * i, 16), :] = both
        c = cosy * cosx[i : i + 1, :] - siny * sinx[i : i + 1, :]
        s = siny * cosx[i : i + 1, :] + cosy * sinx[i : i + 1, :]
        bxy[pl.ds(16 * i, 16), :] = jnp.where(first, c, -s)

    for l in range(3):
        hi, lo = split2(weights[l])
        both = jnp.concatenate([hi, lo], axis=1)
        w2[l] = jnp.concatenate([both, both], axis=0)

    rows = GY * CZ
    wrow = jnp.broadcast_to(wout[...], (16, 128))
    ri = lax.broadcasted_iota(jnp.int32, (16, rows), 0)
    li = lax.broadcasted_iota(jnp.int32, (16, rows), 1)
    pick = (li // CZ) == ((ri + 1) & 15)
    ui = lax.broadcasted_iota(jnp.int32, (rows, 128), 0)
    uj = lax.broadcasted_iota(jnp.int32, (rows, 128), 1)
    up = jnp.where((ui & (CZ - 1)) == (uj // CF), 1.0, 0.0)

    def body(i, carry):
        parts = []
        for j in range(GY):
            a = axy[pl.ds(16 * i + j, 1), :]
            b = bxy[pl.ds(16 * i + j, 1), :]
            parts.append(a * cosz + b * sinz)
        h = jnp.concatenate(parts, axis=0)
        for l in range(3):
            hi, lo = split2(h)
            both = jnp.concatenate([hi, lo], axis=1)
            out = jnp.dot(both, w2[l], preferred_element_type=f32)
            v = out[:, :128] + out[:, 128:] + biases[l : l + 1, :]
            h = v * sigmoid(v)
        logits = lax.dot_general(
            wrow, h, (((1,), (1,)), ((), ())), precision=highest, preferred_element_type=f32
        )
        picked = jnp.where(pick, logits, 0.0)
        wide = jnp.dot(picked, up, precision=highest, preferred_element_type=f32)
        coarse[i] = sigmoid(wide + bout[0])
        return carry

    lax.fori_loop(0, GX, body, 0)


W0, W1, W2, W3 = 2.0, 1.0, 2.0 - math.sqrt(2.0), 2.0 - math.sqrt(3.0)


def density_kernel(ids, coarse, young, inverse, density):
    lane = lax.broadcasted_iota(jnp.int32, (16, NZ), 1)
    not_last, not_first = lane < NZ - 1, lane > 0
    y_cell = ids[1] * CY + jnp.where(
        lax.broadcasted_iota(jnp.int32, (16, NZ), 0) == 15,
        -1,
        lax.broadcasted_iota(jnp.int32, (16, NZ), 0),
    )
    inside_y = (y_cell >= 0) & (y_cell < TOTAL_Y // CF)

    def layers(v):
        side = jnp.where(not_last, pltpu.roll(v, NZ - 1, 1), 0.0) + jnp.where(
            not_first, pltpu.roll(v, 1, 1), 0.0
        )
        return W0 * v + W1 * side, W1 * v + W2 * side, W2 * v + W3 * side

    zero = jnp.zeros((16, NZ), f32)
    values, insides = [], []
    for i in range(GX):
        x_cell = ids[0] * CX - 1 + i
        ok = inside_y & (x_cell >= 0) & (x_cell < TOTAL_X // CF)
        insides.append(jnp.where(ok, 1.0, 0.0))
        values.append(jnp.where(ok, coarse[i], 0.0))
    stacks = [[layers(v) for v in group] for group in (values, insides)]

    for i in range(GX):
        for kind in range(3):
            low = max(i - 1, 0) if kind == 0 else i
            high = min(i + 1, GX - 1) if kind == 2 else i
            sums = []
            for stack in stacks:
                t0 = stack[i][0] + (stack[low][1] + stack[high][1])
                t1 = stack[i][1] + (stack[low][2] + stack[high][2])
                down = pltpu.roll(t1, 1, 0)
                above = pltpu.roll(t1, 15, 0)
                sums.append((t0 + (down + t1), t0 + (t1 + t1), t0 + (t1 + above)))
            planes = {0: (0,), 1: (1, 2), 2: (3,)}[kind]
            for row_kind in range(3):
                count = sums[1][row_kind]
                inside = insides[i] > 0.0
                rho = sums[0][row_kind] / jnp.where(inside, count, 1.0)
                modulus = jnp.where(inside, 0.02 + 0.98 * (rho * rho * rho), 0.0)
                for ox in planes:
                    x = i * CF + ox
                    for oy in {0: (0,), 1: (1, 2), 2: (3,)}[row_kind]:
                        young[pl.ds(x * EY + CF + oy, 8, stride=CF), :] = modulus[0:8, :]
                        young[pl.ds(x * EY + 36 + oy, 1), :] = modulus[8:9, :]
                        young[pl.ds(x * EY + oy, 1), :] = modulus[15:16, :]
                        if 1 <= i <= CX:
                            density[pl.ds((x - CF) * NY + oy, 8, stride=CF), :] = rho[0:8, :]

    lane8 = lax.broadcasted_iota(jnp.int32, (EY, NZ), 1) > 0
    inverse[pl.ds(0, EY), :] = jnp.zeros((EY, NZ), f32)

    def plane(x, carry):
        rows = pl.ds(pl.multiple_of(x * EY, 8), EY)
        before = pl.ds(pl.multiple_of((x - 1) * EY, 8), EY)
        total = young[rows, :] + young[before, :]
        total = total + pltpu.roll(total, 1, 0)
        total = total + jnp.where(lane8, pltpu.roll(total, 1, 1), 0.0)
        inverse[rows, :] = jnp.where(total > 0.0, 1.0 / (DIAG * jnp.where(total > 0.0, total, 1.0)), 0.0)
        return carry

    lax.fori_loop(1, EX, plane, 0, unroll=2)


QUANTITIES = 7


def operator_pass(field, young, yb, begin, end, finish, carry0, rows_above):
    lane = lax.broadcasted_iota(jnp.int32, (8, NZ), 1)
    not_last, not_first = lane < NZ - 1, lane > 0
    r0 = yb * 8

    def transform(x):
        out = []
        for c in range(3):
            at = c * SIZE + x * EY + r0
            v = field[pl.ds(at, 8), :]
            u = field[pl.ds(at + 1, 8), :]
            modes = []
            for t in (v + u, u - v):
                n = jnp.where(not_last, pltpu.roll(t, NZ - 1, 1), 0.0)
                modes += [t + n, n - t]
            out += modes
        return out

    def step(x, state):
        a, held, carry = state
        b = transform(x + 1)
        e1 = young[pl.ds(x * EY + r0, 8), :] * (MU / 16.0)
        e3 = e1 * (1.0 / 3.0)
        e31 = e1 * 0.5
        e9 = e1 * ((RATIO + 4.0) / 9.0)
        s = [p + q for p, q in zip(a, b)]
        d = [q - p for p, q in zip(a, b)]
        u = lambda c, p, q, r: (d if p else s)[4 * c + 2 * q + r]
        g = {}
        ux, uy, uz = u(0, 1, 0, 0), u(1, 0, 1, 0), u(2, 0, 0, 1)
        trace = RATIO * (ux + uy + uz)
        g[0, 1, 0, 0] = e1 * ((ux + ux) + trace)
        g[1, 0, 1, 0] = e1 * ((uy + uy) + trace)
        g[2, 0, 0, 1] = e1 * ((uz + uz) + trace)
        g[0, 0, 1, 0] = g[1, 1, 0, 0] = e1 * (u(0, 0, 1, 0) + u(1, 1, 0, 0))
        g[0, 0, 0, 1] = g[2, 1, 0, 0] = e1 * (u(0, 0, 0, 1) + u(2, 1, 0, 0))
        g[1, 0, 0, 1] = g[2, 0, 1, 0] = e1 * (u(1, 0, 0, 1) + u(2, 0, 1, 0))
        for one, two in (
            ((0, 1, 0, 1), (1, 0, 1, 1)),
            ((0, 1, 1, 0), (2, 0, 1, 1)),
            ((1, 1, 1, 0), (2, 1, 0, 1)),
        ):
            p, q = u(*one), u(*two)
            g[one] = e31 * (3.0 * p + q)
            g[two] = e31 * (3.0 * q + p)
        p, q, r = u(0, 0, 1, 1), u(1, 1, 0, 1), u(2, 1, 1, 0)
        total = p + q + r
        g[0, 0, 1, 1] = e3 * (p + total)
        g[1, 1, 0, 1] = e3 * (q + total)
        g[2, 1, 1, 0] = e3 * (r + total)
        for c in range(3):
            g[c, 1, 1, 1] = e9 * u(c, 1, 1, 1)
        forces, kept = [], []
        for c in range(3):
            f = []
            for q in range(2):
                for r in range(2):
                    one = g[c, 1, q, r]
                    h = held[4 * c + 2 * q + r]
                    if q == 0 and r == 0:
                        f.append(h - one)
                        kept.append(one)
                    else:
                        zero = g[c, 0, q, r]
                        f.append((zero - one) + h)
                        kept.append(zero + one)
            h = []
            for q in range(2):
                low, high = f[2 * q], f[2 * q + 1]
                h.append((low - high) + jnp.where(not_first, pltpu.roll(low + high, 1, 1), 0.0))
            at = (c * EX + x) * 48 + 8 + r0
            rows_above[pl.ds(at, 8), :] = h[0] + h[1]
            forces.append((h[0] - h[1]) + rows_above[pl.ds(at - 1, 8), :])
        return b, kept, finish(x, forces, carry)

    zeros = [jnp.zeros((8, NZ), f32)] * 12
    state = (transform(begin), zeros, carry0)
    return lax.fori_loop(begin, end, step, state)[2]


def main_kernel(
    r, fixed, ylo, yhi, xlo, xhi, young, inverse,
    z_out, y_out, dots_out,
    field, free, load, image, second, above,
):
    def clear(i, carry):
        rows = pl.ds(pl.multiple_of(i * EY, 8), EY)
        zero = jnp.zeros((EY, NZ), f32)
        load[rows, :] = zero
        free[rows, :] = zero
        second[rows, :] = zero
        return carry

    lax.fori_loop(0, 3 * EX, clear, 0)
    for ref in (field, second):
        ref[pl.ds(3 * SIZE, 8), :] = jnp.zeros((8, NZ), f32)

    def own(i, carry):
        c = i // NX
        x = i - c * NX
        src = pl.ds(pl.multiple_of(i * NY, NY), NY)
        dst = pl.ds(c * SIZE + (x + CF) * EY + CF, NY)
        load[dst, :] = r[src, :]
        free[dst, :] = jnp.where(fixed[src, :] == 0, 1.0, 0.0)
        return carry

    lax.fori_loop(0, 3 * NX, own, 0)
    for c in range(3):
        for k in range(2):
            for strip, row in ((ylo, 2 + k), (yhi, 36 + k)):
                load[pl.ds(c * SIZE + CF * EY + row, NX, stride=EY), :] = strip[
                    pl.ds((c * 2 + k) * NX, NX), :
                ]
            for plane, x in ((xlo, 2 + k), (xhi, 20 + k)):
                load[pl.ds(c * SIZE + x * EY, EY), :] = plane[pl.ds((c * 2 + k) * EY, EY), :]
        for strip, row in ((ylo, 3), (yhi, 36)):
            free[pl.ds(c * SIZE + CF * EY + row, NX, stride=EY), :] = strip[pl.ds((6 + c) * NX, NX), :]
        for plane, x in ((xlo, 3), (xhi, 20)):
            free[pl.ds(c * SIZE + x * EY, EY), :] = plane[pl.ds((6 + c) * EY, EY), :]

    def scale(i, carry):
        c = i // EX
        rows = pl.ds(pl.multiple_of(i * EY, 8), EY)
        field[rows, :] = load[rows, :] * inverse[pl.ds(pl.multiple_of((i - c * EX) * EY, 8), EY), :]
        return carry

    lax.fori_loop(0, 3 * EX, scale, 0)

    zero = jnp.zeros((8, NZ), f32)
    row = lax.broadcasted_iota(jnp.int32, (8, NZ), 0)

    def clear_above(i, carry):
        above[pl.ds(pl.multiple_of(i * 48, 8), 8), :] = zero
        return carry

    lax.fori_loop(0, 3 * EX, clear_above, 0)

    def block_one(yb, dots):
        r0 = yb * 8
        own_row = (row + r0 >= CF) & (row + r0 < CF + NY)

        def finish(x, forces, dots):
            keep = jnp.where(own_row & (x >= CF) & (x < CF + NX), 1.0, 0.0)
            inv = inverse[pl.ds(x * EY + r0, 8), :]
            sums = [zero] * 5
            for c in range(3):
                at = pl.ds(c * SIZE + x * EY + r0, 8)
                w = free[at, :] * forces[c]
                y = w * inv
                z = field[at, :]
                rr = load[at, :]
                zt = z - y
                rt = rr - w
                second[at, :] = zt
                image[at, :] = w
                for k, t in enumerate((z * rr, z * w, y * w, z * rt, zt * rt)):
                    sums[k] = sums[k] + t
            return [d + keep * s for d, s in zip(dots, sums)]

        return operator_pass(field, young, yb, 2, 21, finish, dots, above)

    dots = lax.fori_loop(0, 5, block_one, [zero] * 5)

    def block_two(yb, dots):
        r0 = yb * 8
        own_row = (row + r0 >= CF) & (row + r0 < CF + NY)

        def finish(x, forces, dots):
            keep = jnp.where(own_row & (x >= CF), 1.0, 0.0)
            sums = [zero] * 2
            for c in range(3):
                at = pl.ds(c * SIZE + x * EY + r0, 8)
                q = free[at, :] * forces[c]
                w = image[at, :]
                zt = second[at, :]
                z = field[at, :]
                sums[0] = sums[0] + zt * q
                sums[1] = sums[1] + (z - zt) * (w - q)
            return [d + keep * s for d, s in zip(dots, sums)]

        return operator_pass(second, young, yb, 3, 20, finish, dots, above)

    dots = dots + lax.fori_loop(0, 5, block_two, [zero] * 2)

    def copy_out(i, carry):
        c = i // NX
        x = i - c * NX
        src = pl.ds(c * SIZE + (x + CF) * EY + CF, NY)
        dst = pl.ds(pl.multiple_of(i * NY, NY), NY)
        z = field[src, :]
        z_out[dst, :] = z
        y_out[dst, :] = z - second[src, :]
        return carry

    lax.fori_loop(0, 3 * NX, copy_out, 0)
    lane = lax.broadcasted_iota(jnp.int32, (1, NZ), 1)
    line = jnp.zeros((1, NZ), f32)
    for k, d in enumerate(dots):
        line = jnp.where(lane == k, jnp.sum(d), line)
    dots_out[...] = line


def final_kernel(parts, z, y, out):
    total = jnp.sum(parts[...], axis=0, keepdims=True)
    lane = lax.broadcasted_iota(jnp.int32, (1, NZ), 1)
    rz, zw, yw, a, b, c, d = (
        jnp.sum(jnp.where(lane == k, total, 0.0), axis=1, keepdims=True) for k in range(QUANTITIES)
    )
    alpha = rz / zw
    far = zw < 0.5 * rz
    less = -(a / zw)
    rz1 = jnp.where(far, alpha * (alpha * yw) - rz, alpha * (alpha * b + less * a))
    energy = jnp.where(
        far,
        zw - 2.0 * alpha * yw + alpha * (alpha * d),
        less * (less * zw) + 2.0 * alpha * (less * (a - b)) + alpha * (alpha * c),
    )
    beta = rz1 / rz
    curve = energy - beta * (rz1 / alpha)
    alpha1 = rz1 / curve
    c1 = alpha + alpha1 * (1.0 + beta)
    c2 = -(alpha * alpha1)
    c1 = jnp.broadcast_to(c1, (8, NZ))[0:1, :]
    c2 = jnp.broadcast_to(c2, (8, NZ))[0:1, :]

    def body(i, carry):
        rows = pl.ds(pl.multiple_of(i * NY, NY), NY)
        out[rows, :] = c1 * z[rows, :] + c2 * y[rows, :]
        return carry

    lax.fori_loop(0, 3 * NX, body, 0, unroll=4)


def per_device(
    body_force, fixed_dofs, load_nodes, load_forces, frequencies,
    hidden_weights, hidden_biases, output_weights, output_bias,
):
    bx, by = lax.axis_index("gx"), lax.axis_index("gy")
    ids = jnp.stack([bx, by]).astype(jnp.int32)
    rows = 3 * NX * NY
    body = body_force.reshape(rows, NZ)
    fixed = fixed_dofs.reshape(rows, NZ)
    nodes = load_nodes.T
    strip = shape(9 * NX, NZ)
    r, ylo_send, yhi_send = call(
        pack_kernel, (shape(rows, NZ), strip, strip),
        [SMEM, SMEM, SMEM, VMEM, VMEM, VMEM],
        (ids, nodes, load_forces, body, fixed, nodes),
        cost=pl.CostEstimate(flops=400000, transcendentals=0, bytes_accessed=2400000),
    )
    ny, nx = lax.axis_size("gy"), lax.axis_size("gx")
    up_y = [(i, i + 1) for i in range(ny - 1)]
    down_y = [(i + 1, i) for i in range(ny - 1)]
    up_x = [(i, i + 1) for i in range(nx - 1)]
    down_x = [(i + 1, i) for i in range(nx - 1)]
    ylo = lax.ppermute(yhi_send, "gy", up_y)
    yhi = lax.ppermute(ylo_send, "gy", down_y)

    coarse = call(
        mlp_kernel, shape(GX, 16, 128),
        [SMEM, VMEM, VMEM, VMEM, VMEM, SMEM],
        (ids, frequencies, hidden_weights, hidden_biases, output_weights.reshape(1, 128), output_bias),
        scratch=[VMEM((16 * GX, 128), f32), VMEM((16 * GX, 128), f32), VMEM((3, 256, 256), jnp.bfloat16)],
        cost=pl.CostEstimate(flops=1500000000, transcendentals=800000, bytes_accessed=300000),
    )
    plane = shape(9 * EY, NZ)
    xlo_send, xhi_send = call(
        planes_kernel, (plane, plane), [VMEM] * 4, (r, fixed, ylo, yhi),
    )
    xlo = lax.ppermute(xhi_send, "gx", up_x)
    xhi = lax.ppermute(xlo_send, "gx", down_x)
    young, inverse, density = call(
        density_kernel, (shape(SIZE, NZ), shape(SIZE, NZ), shape(NX * NY, NZ)),
        [SMEM, VMEM], (ids, coarse),
        cost=pl.CostEstimate(flops=8000000, transcendentals=0, bytes_accessed=1300000),
    )
    z, y, dots = call(
        main_kernel, (shape(rows, NZ), shape(rows, NZ), shape(1, NZ)),
        [VMEM] * 8, (r, fixed, ylo, yhi, xlo, xhi, young, inverse),
        scratch=[VMEM((3 * SIZE + 8, NZ), f32), VMEM((3 * SIZE, NZ), f32), VMEM((3 * SIZE, NZ), f32),
                 VMEM((3 * SIZE, NZ), f32), VMEM((3 * SIZE + 8, NZ), f32), VMEM((3 * EX * 48, NZ), f32)],
    )
    parts = lax.all_to_all(
        jnp.broadcast_to(dots, (nx * ny, NZ)), ("gx", "gy"), 0, 0, tiled=True
    )
    out = call(final_kernel, shape(rows, NZ), [VMEM] * 3, (parts, z, y))
    return out.reshape(3, NX, NY, NZ), density.reshape(NX, NY, NZ)


def solution(mesh):
    return jax.shard_map(
        per_device,
        mesh=mesh,
        in_specs=(P(None, "gx", "gy", None), P(None, "gx", "gy", None)) + (P(),) * 7,
        out_specs=(P(None, "gx", "gy", None), P("gx", "gy", None)),
        check_vma=False,
    )
```

time: 554 us -> 99.1 us (0.18)
  blocking collectives: 240 us -> 28.6 us
  local copies, waits for them, and re-layouts: 145 us -> 3.6 us
  other arithmetic: 76.5 us -> 0.08 us
  Pallas kernels: 0 us -> 49.8 us
  matrix products: 33.1 us -> 0 us
  starting transfers between devices: 34.9 us -> 11.1 us
  loops' own time: 5.64 us -> 0 us
    psum x3 -> x0, blocking collectives: 240 us -> none  [the longest x2 162 us: scaled_norm(): return lax.psum(jnp.sum(residual_now * scaled_now), ('gx', 'gy'))]
    scatter-add x1 -> x0, other arithmetic: 50 us -> none  [per_device(): body_force.at[:, index_x, index_y, load_nodes[:, 2]]]
    pallas_call x0 -> x6, Pallas kernels: none -> 49.8 us  [call(): pl.pallas_call(kernel, out_shape=out_shape, in_specs=[spec(s) for s in in...]
    while x88 -> x0, local copies, waits for them, and re-layouts: 43.3 us -> none
    reshape x17 -> x0, local copies, waits for them, and re-layouts: 35.9 us -> none  [the longest x8 14.3 us: corner_products(): jnp.concatenate(pieces, axis=0).reshape(24, across * along * height)]
    dot_general x13 -> x0, matrix products: 33.1 us -> none  [the longest x8 24.6 us: corner_products(): jnp.dot(stiffness, stacked, precision=highest, preferred_element_type=jnp...]
    all_to_all x0 -> x1, blocking collectives: none -> 28.6 us  [per_device(): lax.all_to_all(jnp.broadcast_to(dots, (nx * ny, NZ)), ('gx', 'gy'), 0, 0,...]
    ppermute x12 -> x4, starting transfers between devices: 34.9 us -> 11.1 us  [the longest x1 4.79 us: per_device(): ylo = lax.ppermute(yhi_send, 'gy', up_y)]
  transfers between devices with their start and end apart: 12 -> 4, of which waited for: 6 -> 1; matrix products, arithmetic and copies ran while one was open for 16% -> 0% of each run, Pallas kernels for 0% -> 10%
where the time goes in v1:
time: 99.1 us; the launch traced here: 98.4 us
  Pallas kernels  49.8 us (50%)
  blocking collectives  28.6 us (29%)
  starting transfers between devices  11.1 us (11%)
  waiting for transfers between devices  3.74 us (4%)
  local copies, waits for them, and re-layouts  3.6 us (4%)
  between operations  1.43 us (1%)
    pallas_call x6, Pallas kernels, call(): pl.pallas_call(kernel, out_shape=out_shape, in_specs=[spec(s) for s in in...  49.8 us
    all_to_all x1, blocking collectives, per_device(): lax.all_to_all(jnp.broadcast_to(dots, (nx * ny, NZ)), ('gx', 'gy'), 0, 0,...  28.6 us
    ppermute x1, starting transfers between devices, per_device(): ylo = lax.ppermute(yhi_send, 'gy', up_y)  4.79 us
    ppermute x1, waiting for transfers between devices, per_device(): yhi = lax.ppermute(ylo_send, 'gy', down_y)  3.73 us
    unnamed x18, local copies, waits for them, and re-layouts  3.53 us
    ppermute x1, starting transfers between devices, per_device(): xlo = lax.ppermute(xhi_send, 'gx', up_x)  3.05 us
  transfers between devices with their start and end apart: 4, of which 1 were waited for; matrix products, arithmetic and copies ran while one was open for 0% of the time, Pallas kernels for 10%

profile of v1, /device:TPU:1, one launch (start us, length us, event | category | flops | bytes accessed | tf_op | source)
XLA Modules:
  0.0 98.4 jit_solution(13295510170415850818)
XLA Ops:
  0.6 0.0 copy-start.4
  0.6 0.0 copy-start.3
  0.7 0.1 pad_add_fusion.ids
  0.7 0.6 copy-done.4
  1.3 0.0 copy-done.3
  1.3 0.0 copy-start
  1.4 1.1 %copy-done = s32[3,16,32,128]{3,2,1,0:T(8,128)S(1)} copy-done((s32[3,16,32,128]{3,2,1,0:T(8,128)S(1)}, s32[3,16,32,128]{3,2,1,0:T(8,128)}, u32[]{:S(2)}) %copy-start) | copy-done | bytes 786456
  2.5 0.0 copy-start.2
  2.5 1.1 %copy-done.2 = f32[3,16,32,128]{3,2,1,0:T(8,128)S(1)} copy-done((f32[3,16,32,128]{3,2,1,0:T(8,128)S(1)}, f32[3,16,32,128]{3,2,1,0:T(8,128)}, u32[]{:S(2)}) %copy-start.2) | copy-done | bytes 786456
  3.6 0.0 copy-start.1
  3.6 1.7 %shard_map.104 = (f32[1536,128]{1,0:T(8,128)S(1)}, f32[144,128]{1,0:T(8,128)S(1)}, f32[144,128]{1,0:T(8,128)S(1)}) custom-call(s32[2]{0:T(128)S(1)} %pad_add_fusion.ids, s32[3,512]{1,0:T(4,128)S(1)} %bitcast.15, f32[3,512]{1,0:T(4,128)S(1)} %copy-done.4, f32[1536,128]{1,0:T(8,128)S(1)} %bitcast.13, s32[1536,128]{1,0:T(8,128)S(1)} %bitcast.10, ...), custom_call_target="tpu_custom_call" | custom-call | flops 400000 | bytes 2400000 | tf_op jit(solution)/shard_map/pallas_call | solution.py:34
  5.3 4.8 %collective-permute-start = (f32[144,128]{1,0:T(8,128)S(1)}, f32[144,128]{1,0:T(8,128)S(1)}, u32[]{:S(2)}, u32[]{:S(2)}) collective-permute-start(f32[144,128]{1,0:T(8,128)S(1)} %get-tuple-element.14), channel_id=1, source_target_pairs={{0,1},{1,2},{2,3},{3,4},{4,5},{5,6},{6,7},{8,9},{9,10},{10,11},{11... | collective-permute-start | bytes 221192 | tf_op jit(solution)/shard_map/ppermute | solution.py:518
  10.1 1.9 %collective-permute-start.1 = (f32[144,128]{1,0:T(8,128)S(1)}, f32[144,128]{1,0:T(8,128)S(1)}, u32[]{:S(2)}, u32[]{:S(2)}) collective-permute-start(f32[144,128]{1,0:T(8,128)S(1)} %get-tuple-element.15), channel_id=1, source_target_pairs={{1,0},{2,1},{3,2},{4,3},{5,4},{6,5},{7,6},{9,8},{10,9},{11,10},{12... | collective-permute-start | bytes 221192 | tf_op jit(solution)/shard_map/ppermute | solution.py:519
  12.0 0.0 collective-permute-done.ylo
  12.0 3.7 %collective-permute-done.1.yhi = f32[144,128]{1,0:T(8,128)S(1)} collective-permute-done((f32[144,128]{1,0:T(8,128)S(1)}, f32[144,128]{1,0:T(8,128)S(1)}, u32[]{:S(2)}, u32[]{:S(2)}) %collective-permute-start.1) | collective-permute-done | bytes 73760 | tf_op jit(solution)/shard_map/ppermute | solution.py:519
  15.7 0.0 copy-done.1
  15.7 0.0 copy-start.5
  15.7 0.1 shard_map.105
  15.8 3.1 %collective-permute-start.2 = (f32[360,128]{1,0:T(8,128)S(1)}, f32[360,128]{1,0:T(8,128)S(1)}, u32[]{:S(2)}, u32[]{:S(2)}) collective-permute-start(f32[360,128]{1,0:T(8,128)S(1)} %get-tuple-element.16), channel_id=1, source_target_pairs={{0,8},{8,16},{16,24},{24,32},{32,40},{40,48},{48,56},{56,64},{64,7... | collective-permute-start | bytes 552968 | tf_op jit(solution)/shard_map/ppermute | solution.py:532
  18.9 0.0 copy-start.7
  18.9 0.0 copy-start.6
  18.9 1.3 %collective-permute-start.3 = (f32[360,128]{1,0:T(8,128)S(1)}, f32[360,128]{1,0:T(8,128)S(1)}, u32[]{:S(2)}, u32[]{:S(2)}) collective-permute-start(f32[360,128]{1,0:T(8,128)S(1)} %get-tuple-element.17), channel_id=1, source_target_pairs={{8,0},{16,8},{24,16},{32,24},{40,32},{48,40},{56,48},{64,56},{72,6... | collective-permute-start | bytes 552968 | tf_op jit(solution)/shard_map/ppermute | solution.py:533
  20.8 0.0 copy-start.8
  20.9 0.0 copy-done.5
  20.9 0.0 copy-done.7
  20.9 0.0 copy-done.6
  20.9 0.6 copy-done.8
  21.5 7.0 %shard_map.106.coarse = f32[6,16,128]{2,1,0:T(8,128)S(1)} custom-call(s32[2]{0:T(128)S(1)} %pad_add_fusion.ids, f32[3,64]{1,0:T(4,128)S(1)} %copy-done.6, f32[3,128,128]{2,1,0:T(8,128)S(1)} %copy-done.5, f32[3,128]{1,0:T(4,128)S(1)} %copy-done.7, f32[1,128]{1,0:T(1,128)S(1)} %bitcast.18, f32[1]{0:T(128)S(6)} %copy.11.bout), custom_call_target="tpu_custom_call" | custom-call | flops 1500000000 | bytes 300000 | tf_op jit(solution)/shard_map/pallas_call | solution.py:34
  28.5 2.6 %shard_map.107 = (f32[960,128]{1,0:T(8,128)S(1)}, f32[960,128]{1,0:T(8,128)S(1)}, f32[512,128]{1,0:T(8,128)}) custom-call(s32[2]{0:T(128)S(1)} %pad_add_fusion.ids, f32[6,16,128]{2,1,0:T(8,128)S(1)} %shard_map.106.coarse), custom_call_target="tpu_custom_call" | custom-call | flops 8000000 | bytes 1300000 | tf_op jit(solution)/shard_map/pallas_call | solution.py:34
  31.1 0.0 collective-permute-done.2.xlo
  31.1 0.0 collective-permute-done.3.xhi
  31.1 37.4 %shard_map.108 = (f32[1536,128]{1,0:T(8,128)S(1)}, f32[1536,128]{1,0:T(8,128)S(1)}, f32[1,128]{1,0:T(1,128)S(1)}) custom-call(f32[1536,128]{1,0:T(8,128)S(1)} %get-tuple-element.13.r, s32[1536,128]{1,0:T(8,128)S(1)} %bitcast.12, f32[144,128]{1,0:T(8,128)S(1)} %collective-permute-done.ylo, f32[144,128]{1,0:T(8,128)S(1)} %collective-permute-done.1.yhi, ...), custom_call_target="tpu_custom_call" | custom-call | tf_op jit(solution)/shard_map/pallas_call | solution.py:34
  68.5 0.1 broadcast_in_dim.2
  68.6 28.6 %all_to_all.8 = f32[256,1,128]{2,1,0:T(1,128)S(1)} all-to-all(f32[256,1,128]{2,1,0:T(1,128)S(1)} %broadcast_in_dim.2), channel_id=1, replica_groups=mesh['gx'=32,'gy'=8] {'gx','gy'}, dimensions={0} | all-to-all | bytes 262144 | tf_op jit(solution)/shard_map/all_to_all | solution.py:545
  97.2 1.1 %shard_map.109 = f32[1536,128]{1,0:T(8,128)} custom-call(f32[256,128]{1,0:T(8,128)S(1)} %bitcast.14, f32[1536,128]{1,0:T(8,128)S(1)} %get-tuple-element.21.z, f32[1536,128]{1,0:T(8,128)S(1)} %get-tuple-element.22.y), custom_call_target="tpu_custom_call" | custom-call | tf_op jit(solution)/shard_map/pallas_call | solution.py:34
Async XLA Ops:
  0.6 0.7 copy-start.4
  0.6 0.7 copy-start.3
  1.3 1.1 %copy-start = (s32[3,16,32,128]{3,2,1,0:T(8,128)S(1)}, s32[3,16,32,128]{3,2,1,0:T(8,128)}, u32[]{:S(2)}) copy-start(s32[3,16,32,128]{3,2,1,0:T(8,128)} %param.10) | copy-start | bytes 2359300
  2.5 1.1 %copy-start.2 = (f32[3,16,32,128]{3,2,1,0:T(8,128)S(1)}, f32[3,16,32,128]{3,2,1,0:T(8,128)}, u32[]{:S(2)}) copy-start(f32[3,16,32,128]{3,2,1,0:T(8,128)} %param.9) | copy-start | bytes 2359300
  3.6 12.1 %copy-start.1 = (s32[3,16,32,128]{3,2,1,0:T(8,128)S(1)}, s32[3,16,32,128]{3,2,1,0:T(8,128)}, u32[]{:S(2)}) copy-start(s32[3,16,32,128]{3,2,1,0:T(8,128)} %param.10) | copy-start | bytes 2359300
  5.3 6.7 %collective-permute-start = (f32[144,128]{1,0:T(8,128)S(1)}, f32[144,128]{1,0:T(8,128)S(1)}, u32[]{:S(2)}, u32[]{:S(2)}) collective-permute-start(f32[144,128]{1,0:T(8,128)S(1)} %get-tuple-element.14), channel_id=1, source_target_pairs={{0,1},{1,2},{2,3},{3,4},{4,5},{5,6},{6,7},{8,9},{9,10},{10,11},{11... | collective-permute-start | bytes 221192 | tf_op jit(solution)/shard_map/ppermute | solution.py:518
  10.1 5.7 %collective-permute-start.1 = (f32[144,128]{1,0:T(8,128)S(1)}, f32[144,128]{1,0:T(8,128)S(1)}, u32[]{:S(2)}, u32[]{:S(2)}) collective-permute-start(f32[144,128]{1,0:T(8,128)S(1)} %get-tuple-element.15), channel_id=1, source_target_pairs={{1,0},{2,1},{3,2},{4,3},{5,4},{6,5},{7,6},{9,8},{10,9},{11,10},{12... | collective-permute-start | bytes 221192 | tf_op jit(solution)/shard_map/ppermute | solution.py:519
  15.7 5.1 %copy-start.5 = (f32[3,128,128]{2,1,0:T(8,128)S(1)}, f32[3,128,128]{2,1,0:T(8,128)}, u32[]{:S(2)}) copy-start(f32[3,128,128]{2,1,0:T(8,128)} %weights.1) | copy-start | bytes 589828
  15.8 15.3 %collective-permute-start.2 = (f32[360,128]{1,0:T(8,128)S(1)}, f32[360,128]{1,0:T(8,128)S(1)}, u32[]{:S(2)}, u32[]{:S(2)}) collective-permute-start(f32[360,128]{1,0:T(8,128)S(1)} %get-tuple-element.16), channel_id=1, source_target_pairs={{0,8},{8,16},{16,24},{24,32},{32,40},{40,48},{48,56},{56,64},{64,7... | collective-permute-start | bytes 552968 | tf_op jit(solution)/shard_map/ppermute | solution.py:532
  18.9 2.0 %copy-start.7 = (f32[3,128]{1,0:T(4,128)S(1)}, f32[3,128]{1,0:T(4,128)}, u32[]{:S(2)}) copy-start(f32[3,128]{1,0:T(4,128)} %biases.1) | copy-start | bytes 4612
  18.9 2.0 %copy-start.6 = (f32[3,64]{1,0:T(4,128)S(1)}, f32[3,64]{1,0:T(4,128)}, u32[]{:S(2)}) copy-start(f32[3,64]{1,0:T(4,128)} %freq.1) | copy-start | bytes 2308
  18.9 12.2 %collective-permute-start.3 = (f32[360,128]{1,0:T(8,128)S(1)}, f32[360,128]{1,0:T(8,128)S(1)}, u32[]{:S(2)}, u32[]{:S(2)}) collective-permute-start(f32[360,128]{1,0:T(8,128)S(1)} %get-tuple-element.17), channel_id=1, source_target_pairs={{8,0},{16,8},{24,16},{32,24},{40,32},{48,40},{56,48},{64,56},{72,6... | collective-permute-start | bytes 552968 | tf_op jit(solution)/shard_map/ppermute | solution.py:533
  20.8 0.7 copy-start.8

commit v2 on v1

--- a/solution.py
+++ b/solution.py
@@ -258,115 +258,112 @@
 
 
 QUANTITIES = 7
-
-
-def operator_pass(field, young, yb, begin, end, finish, carry0, rows_above):
+BLOCKS = EY // 8
+TALL = EY + 8
+
+
+def operator_pass(zsum, zdiff, young, above, minus, plus, begin, end, unroll):
+    def block(yb, carry):
+        r0 = yb * 8
+
+        def transform(x):
+            out = []
+            for c in range(3):
+                at = c * SIZE + x * EY + r0
+                pairs = [(t[pl.ds(at, 8), :], t[pl.ds(at + 1, 8), :]) for t in (zsum, zdiff)]
+                out += [v + u for v, u in pairs] + [u - v for v, u in pairs]
+            return out
+
+        def modal(x, a, b):
+            e1 = young[pl.ds(x * EY + r0, 8), :] * (MU / 16.0)
+            e3 = e1 * (1.0 / 3.0)
+            e31 = e1 * 0.5
+            e9 = e1 * ((RATIO + 4.0) / 9.0)
+            s = [p + q for p, q in zip(a, b)]
+            d = [q - p for p, q in zip(a, b)]
+            u = lambda c, p, q, r: (d if p else s)[4 * c + 2 * q + r]
+            g = {}
+            ux, uy, uz = u(0, 1, 0, 0), u(1, 0, 1, 0), u(2, 0, 0, 1)
+            trace = RATIO * (ux + uy + uz)
+            g[0, 1, 0, 0] = e1 * ((ux + ux) + trace)
+            g[1, 0, 1, 0] = e1 * ((uy + uy) + trace)
+            g[2, 0, 0, 1] = e1 * ((uz + uz) + trace)
+            g[0, 0, 1, 0] = g[1, 1, 0, 0] = e1 * (u(0, 0, 1, 0) + u(1, 1, 0, 0))
+            g[0, 0, 0, 1] = g[2, 1, 0, 0] = e1 * (u(0, 0, 0, 1) + u(2, 1, 0, 0))
+            g[1, 0, 0, 1] = g[2, 0, 1, 0] = e1 * (u(1, 0, 0, 1) + u(2, 0, 1, 0))
+            for one, two in (
+                ((0, 1, 0, 1), (1, 0, 1, 1)),
+                ((0, 1, 1, 0), (2, 0, 1, 1)),
+                ((1, 1, 1, 0), (2, 1, 0, 1)),
+            ):
+                p, q = u(*one), u(*two)
+                g[one] = e31 * (3.0 * p + q)
+                g[two] = e31 * (3.0 * q + p)
+            p, q, r = u(0, 0, 1, 1), u(1, 1, 0, 1), u(2, 1, 1, 0)
+            total = p + q + r
+            g[0, 0, 1, 1] = e3 * (p + total)
+            g[1, 1, 0, 1] = e3 * (q + total)
+            g[2, 1, 1, 0] = e3 * (r + total)
+            for c in range(3):
+                g[c, 1, 1, 1] = e9 * u(c, 1, 1, 1)
+            return g
+
+        def keep(g):
+            out = []
+            for c in range(3):
+                out.append(g[c, 1, 0, 0])
+                for q, r in ((0, 1), (1, 0), (1, 1)):
+                    out.append(g[c, 0, q, r] + g[c, 1, q, r])
+            return out
+
+        def step(x, state):
+            a, held = state
+            b = transform(x + 1)
+            g = modal(x, a, b)
+            for c in range(3):
+                f = [held[4 * c] - g[c, 1, 0, 0]]
+                for k, (q, r) in enumerate(((0, 1), (1, 0), (1, 1))):
+                    f.append((g[c, 0, q, r] - g[c, 1, q, r]) + held[4 * c + 1 + k])
+                h = []
+                for r in range(2):
+                    at = ((2 * c + r) * EX + x) * TALL + 8 + r0
+                    above[pl.ds(at, 8), :] = f[r] + f[2 + r]
+                    h.append((f[r] - f[2 + r]) + above[pl.ds(at - 1, 8), :])
+                rows = pl.ds(pl.multiple_of(c * SIZE + x * EY + r0, 8), 8)
+                minus[rows, :] = h[0] - h[1]
+                plus[rows, :] = h[0] + h[1]
+            return b, keep(g)
+
+        a = transform(begin)
+        b = transform(begin + 1)
+        lax.fori_loop(begin + 1, end, step, (b, keep(modal(begin, a, b))), unroll=unroll)
+        return carry
+
+    lax.fori_loop(0, BLOCKS, block, 0)
+
+
+def main_kernel(
+    r, fixed, ylo, yhi, xlo, xhi, young, inverse,
+    field, scaled, dots_out,
+    free, load, image, zsum, zdiff, above, minus, plus,
+):
+    zero = jnp.zeros((8, NZ), f32)
     lane = lax.broadcasted_iota(jnp.int32, (8, NZ), 1)
     not_last, not_first = lane < NZ - 1, lane > 0
-    r0 = yb * 8
-
-    def transform(x):
-        out = []
-        for c in range(3):
-            at = c * SIZE + x * EY + r0
-            v = field[pl.ds(at, 8), :]
-            u = field[pl.ds(at + 1, 8), :]
-            modes = []
-            for t in (v + u, u - v):
-                n = jnp.where(not_last, pltpu.roll(t, NZ - 1, 1), 0.0)
-                modes += [t + n, n - t]
-            out += modes
-        return out
-
-    def step(x, state):
-        a, held, carry = state
-        b = transform(x + 1)
-        e1 = young[pl.ds(x * EY + r0, 8), :] * (MU / 16.0)
-        e3 = e1 * (1.0 / 3.0)
-        e31 = e1 * 0.5
-        e9 = e1 * ((RATIO + 4.0) / 9.0)
-        s = [p + q for p, q in zip(a, b)]
-        d = [q - p for p, q in zip(a, b)]
-        u = lambda c, p, q, r: (d if p else s)[4 * c + 2 * q + r]
-        g = {}
-        ux, uy, uz = u(0, 1, 0, 0), u(1, 0, 1, 0), u(2, 0, 0, 1)
-        trace = RATIO * (ux + uy + uz)
-        g[0, 1, 0, 0] = e1 * ((ux + ux) + trace)
-        g[1, 0, 1, 0] = e1 * ((uy + uy) + trace)
-        g[2, 0, 0, 1] = e1 * ((uz + uz) + trace)
-        g[0, 0, 1, 0] = g[1, 1, 0, 0] = e1 * (u(0, 0, 1, 0) + u(1, 1, 0, 0))
-        g[0, 0, 0, 1] = g[2, 1, 0, 0] = e1 * (u(0, 0, 0, 1) + u(2, 1, 0, 0))
-        g[1, 0, 0, 1] = g[2, 0, 1, 0] = e1 * (u(1, 0, 0, 1) + u(2, 0, 1, 0))
-        for one, two in (
-            ((0, 1, 0, 1), (1, 0, 1, 1)),
-            ((0, 1, 1, 0), (2, 0, 1, 1)),
-            ((1, 1, 1, 0), (2, 1, 0, 1)),
-        ):
-            p, q = u(*one), u(*two)
-            g[one] = e31 * (3.0 * p + q)
-            g[two] = e31 * (3.0 * q + p)
-        p, q, r = u(0, 0, 1, 1), u(1, 1, 0, 1), u(2, 1, 1, 0)
-        total = p + q + r
-        g[0, 0, 1, 1] = e3 * (p + total)
-        g[1, 1, 0, 1] = e3 * (q + total)
-        g[2, 1, 1, 0] = e3 * (r + total)
-        for c in range(3):
-            g[c, 1, 1, 1] = e9 * u(c, 1, 1, 1)
-        forces, kept = [], []
-        for c in range(3):
-            f = []
-            for q in range(2):
-                for r in range(2):
-                    one = g[c, 1, q, r]
-                    h = held[4 * c + 2 * q + r]
-                    if q == 0 and r == 0:
-                        f.append(h - one)
-                        kept.append(one)
-                    else:
-                        zero = g[c, 0, q, r]
-                        f.append((zero - one) + h)
-                        kept.append(zero + one)
-            h = []
-            for q in range(2):
-                low, high = f[2 * q], f[2 * q + 1]
-                h.append((low - high) + jnp.where(not_first, pltpu.roll(low + high, 1, 1), 0.0))
-            at = (c * EX + x) * 48 + 8 + r0
-            rows_above[pl.ds(at, 8), :] = h[0] + h[1]
-            forces.append((h[0] - h[1]) + rows_above[pl.ds(at - 1, 8), :])
-        return b, kept, finish(x, forces, carry)
-
-    zeros = [jnp.zeros((8, NZ), f32)] * 12
-    state = (transform(begin), zeros, carry0)
-    return lax.fori_loop(begin, end, step, state)[2]
-
-
-def main_kernel(
-    r, fixed, ylo, yhi, xlo, xhi, young, inverse,
-    z_out, y_out, dots_out,
-    field, free, load, image, second, above,
-):
-    def clear(i, carry):
-        rows = pl.ds(pl.multiple_of(i * EY, 8), EY)
-        zero = jnp.zeros((EY, NZ), f32)
-        load[rows, :] = zero
-        free[rows, :] = zero
-        second[rows, :] = zero
-        return carry
-
-    lax.fori_loop(0, 3 * EX, clear, 0)
-    for ref in (field, second):
-        ref[pl.ds(3 * SIZE, 8), :] = jnp.zeros((8, NZ), f32)
 
     def own(i, carry):
         c = i // NX
         x = i - c * NX
         src = pl.ds(pl.multiple_of(i * NY, NY), NY)
-        dst = pl.ds(c * SIZE + (x + CF) * EY + CF, NY)
-        load[dst, :] = r[src, :]
-        free[dst, :] = jnp.where(fixed[src, :] == 0, 1.0, 0.0)
-        return carry
-
-    lax.fori_loop(0, 3 * NX, own, 0)
+        base = pl.multiple_of(c * SIZE + (x + CF) * EY, 8)
+        for ref in (load, free):
+            ref[pl.ds(base, 8), :] = zero
+            ref[pl.ds(base + EY - 8, 8), :] = zero
+        load[pl.ds(base + CF, NY), :] = r[src, :]
+        free[pl.ds(base + CF, NY), :] = jnp.where(fixed[src, :] == 0, 1.0, 0.0)
+        return carry
+
+    lax.fori_loop(0, 3 * NX, own, 0, unroll=2)
     for c in range(3):
         for k in range(2):
             for strip, row in ((ylo, 2 + k), (yhi, 36 + k)):
@@ -379,86 +376,103 @@
             free[pl.ds(c * SIZE + CF * EY + row, NX, stride=EY), :] = strip[pl.ds((6 + c) * NX, NX), :]
         for plane, x in ((xlo, 3), (xhi, 20)):
             free[pl.ds(c * SIZE + x * EY, EY), :] = plane[pl.ds((6 + c) * EY, EY), :]
-
-    def scale(i, carry):
-        c = i // EX
-        rows = pl.ds(pl.multiple_of(i * EY, 8), EY)
-        field[rows, :] = load[rows, :] * inverse[pl.ds(pl.multiple_of((i - c * EX) * EY, 8), EY), :]
-        return carry
-
-    lax.fori_loop(0, 3 * EX, scale, 0)
-
-    zero = jnp.zeros((8, NZ), f32)
+    for ref in (zsum, zdiff):
+        ref[pl.ds(3 * SIZE, 8), :] = zero
+
+    def z_stage(at, v):
+        n = jnp.where(not_last, pltpu.roll(v, NZ - 1, 1), 0.0)
+        zsum[at, :] = v + n
+        zdiff[at, :] = n - v
+
+    def prepare(x, carry):
+        for j in range(BLOCKS):
+            base = pl.multiple_of(x * EY, 8) + 8 * j
+            inv = inverse[pl.ds(base, 8), :]
+            for c in range(3):
+                at = pl.ds(base + c * SIZE, 8)
+                v = load[at, :] * inv
+                field[at, :] = v
+                z_stage(at, v)
+        return carry
+
+    lax.fori_loop(2, 22, prepare, 0)
+
+    for c in range(3):
+        for ref in (zsum, zdiff):
+            ref[pl.ds(c * SIZE + 22 * EY, 8), :] = zero
+
+    def clear_above(i, carry):
+        above[pl.ds(pl.multiple_of(i * TALL, 8), 8), :] = zero
+        return carry
+
+    lax.fori_loop(0, 6 * EX, clear_above, 0, unroll=8)
+
+    operator_pass(zsum, zdiff, young, above, minus, plus, 2, 21, 3)
+
     row = lax.broadcasted_iota(jnp.int32, (8, NZ), 0)
-
-    def clear_above(i, carry):
-        above[pl.ds(pl.multiple_of(i * 48, 8), 8), :] = zero
-        return carry
-
-    lax.fori_loop(0, 3 * EX, clear_above, 0)
-
-    def block_one(yb, dots):
-        r0 = yb * 8
-        own_row = (row + r0 >= CF) & (row + r0 < CF + NY)
-
-        def finish(x, forces, dots):
-            keep = jnp.where(own_row & (x >= CF) & (x < CF + NX), 1.0, 0.0)
-            inv = inverse[pl.ds(x * EY + r0, 8), :]
-            sums = [zero] * 5
-            for c in range(3):
-                at = pl.ds(c * SIZE + x * EY + r0, 8)
-                w = free[at, :] * forces[c]
+    first_rows = jnp.where(row >= CF, 1.0, 0.0)
+    last_rows = jnp.where(row < CF, 1.0, 0.0)
+
+    def gather(totals, j, terms):
+        for k, t in enumerate(terms):
+            if j == 0:
+                t = t * first_rows
+            if j == BLOCKS - 1:
+                t = t * last_rows
+            totals[k] = t if totals[k] is None else totals[k] + t
+
+    def force(at):
+        return minus[at, :] + jnp.where(not_first, pltpu.roll(plus[at, :], 1, 1), 0.0)
+
+    def finish_one(x, dots):
+        totals = [None] * 5
+        for j in range(BLOCKS):
+            base = pl.multiple_of(x * EY, 8) + 8 * j
+            inv = inverse[pl.ds(base, 8), :]
+            sums = None
+            for c in range(3):
+                at = pl.ds(base + c * SIZE, 8)
+                w = free[at, :] * force(at)
                 y = w * inv
                 z = field[at, :]
-                rr = load[at, :]
                 zt = z - y
-                rt = rr - w
-                second[at, :] = zt
+                scaled[at, :] = y
                 image[at, :] = w
-                for k, t in enumerate((z * rr, z * w, y * w, z * rt, zt * rt)):
-                    sums[k] = sums[k] + t
-            return [d + keep * s for d, s in zip(dots, sums)]
-
-        return operator_pass(field, young, yb, 2, 21, finish, dots, above)
-
-    dots = lax.fori_loop(0, 5, block_one, [zero] * 5)
-
-    def block_two(yb, dots):
-        r0 = yb * 8
-        own_row = (row + r0 >= CF) & (row + r0 < CF + NY)
-
-        def finish(x, forces, dots):
-            keep = jnp.where(own_row & (x >= CF), 1.0, 0.0)
-            sums = [zero] * 2
-            for c in range(3):
-                at = pl.ds(c * SIZE + x * EY + r0, 8)
-                q = free[at, :] * forces[c]
-                w = image[at, :]
-                zt = second[at, :]
-                z = field[at, :]
-                sums[0] = sums[0] + zt * q
-                sums[1] = sums[1] + (z - zt) * (w - q)
-            return [d + keep * s for d, s in zip(dots, sums)]
-
-        return operator_pass(second, young, yb, 3, 20, finish, dots, above)
-
-    dots = dots + lax.fori_loop(0, 5, block_two, [zero] * 2)
-
-    def copy_out(i, carry):
-        c = i // NX
-        x = i - c * NX
-        src = pl.ds(c * SIZE + (x + CF) * EY + CF, NY)
-        dst = pl.ds(pl.multiple_of(i * NY, NY), NY)
-        z = field[src, :]
-        z_out[dst, :] = z
-        y_out[dst, :] = z - second[src, :]
-        return carry
-
-    lax.fori_loop(0, 3 * NX, copy_out, 0)
-    lane = lax.broadcasted_iota(jnp.int32, (1, NZ), 1)
+                z_stage(at, zt)
+                if dots is not None:
+                    rr = load[at, :]
+                    rt = rr - w
+                    terms = (z * rr, z * w, y * w, z * rt, zt * rt)
+                    sums = terms if sums is None else [p + q for p, q in zip(sums, terms)]
+            if dots is not None:
+                gather(totals, j, sums)
+        return dots if dots is None else [p + q for p, q in zip(dots, totals)]
+
+    finish_one(CF - 1, None)
+    finish_one(CF + NX, None)
+    dots = lax.fori_loop(CF, CF + NX, finish_one, [zero] * 5)
+
+    operator_pass(zsum, zdiff, young, above, minus, plus, 3, 20, 4)
+
+    def finish_two(x, dots):
+        totals = [None] * 2
+        for j in range(BLOCKS):
+            base = pl.multiple_of(x * EY, 8) + 8 * j
+            sums = None
+            for c in range(3):
+                at = pl.ds(base + c * SIZE, 8)
+                q = free[at, :] * force(at)
+                y = scaled[at, :]
+                terms = ((field[at, :] - y) * q, y * (image[at, :] - q))
+                sums = terms if sums is None else [a + b for a, b in zip(sums, terms)]
+            gather(totals, j, sums)
+        return [p + q for p, q in zip(dots, totals)]
+
+    dots = dots + lax.fori_loop(CF, CF + NX, finish_two, [zero] * 2)
+    one = lax.broadcasted_iota(jnp.int32, (1, NZ), 1)
     line = jnp.zeros((1, NZ), f32)
     for k, d in enumerate(dots):
-        line = jnp.where(lane == k, jnp.sum(d), line)
+        line = jnp.where(one == k, jnp.sum(d), line)
     dots_out[...] = line
 
 
@@ -486,8 +500,9 @@
     c2 = jnp.broadcast_to(c2, (8, NZ))[0:1, :]
 
     def body(i, carry):
-        rows = pl.ds(pl.multiple_of(i * NY, NY), NY)
-        out[rows, :] = c1 * z[rows, :] + c2 * y[rows, :]
+        c = i // NX
+        src = pl.ds(c * SIZE + (i - c * NX + CF) * EY + CF, NY)
+        out[pl.ds(pl.multiple_of(i * NY, NY), NY), :] = c1 * z[src, :] + c2 * y[src, :]
         return carry
 
     lax.fori_loop(0, 3 * NX, body, 0, unroll=4)
@@ -536,11 +551,12 @@
         [SMEM, VMEM], (ids, coarse),
         cost=pl.CostEstimate(flops=8000000, transcendentals=0, bytes_accessed=1300000),
     )
+    ext = VMEM((3 * SIZE, NZ), f32)
+    tail = VMEM((3 * SIZE + 8, NZ), f32)
     z, y, dots = call(
-        main_kernel, (shape(rows, NZ), shape(rows, NZ), shape(1, NZ)),
+        main_kernel, (shape(3 * SIZE, NZ), shape(3 * SIZE, NZ), shape(1, NZ)),
         [VMEM] * 8, (r, fixed, ylo, yhi, xlo, xhi, young, inverse),
-        scratch=[VMEM((3 * SIZE + 8, NZ), f32), VMEM((3 * SIZE, NZ), f32), VMEM((3 * SIZE, NZ), f32),
-                 VMEM((3 * SIZE, NZ), f32), VMEM((3 * SIZE + 8, NZ), f32), VMEM((3 * EX * 48, NZ), f32)],
+        scratch=[ext, ext, ext, tail, tail, VMEM((6 * EX * TALL, NZ), f32), ext, ext],
     )
     parts = lax.all_to_all(
         jnp.broadcast_to(dots, (nx * ny, NZ)), ("gx", "gy"), 0, 0, tiled=True

time: 99.1 us -> 75.7 us (0.76)
  Pallas kernels: 49.8 us -> 26.8 us
    pallas_call x6, Pallas kernels: 49.8 us -> 26.8 us  [call(): pl.pallas_call(kernel, out_shape=out_shape, in_specs=[spec(s) for s in in...]
  transfers between devices with their start and end apart: 4 -> 4, of which waited for: 1 -> 1; matrix products, arithmetic and copies ran while one was open for 0% -> 0% of each run, Pallas kernels for 10% -> 13%
where the time goes in v2:
time: 75.7 us; the launch traced here: 75.8 us
  blocking collectives  28.9 us (38%)
  Pallas kernels  26.8 us (35%)
  starting transfers between devices  11.1 us (15%)
  local copies, waits for them, and re-layouts  3.75 us (5%)
  waiting for transfers between devices  3.74 us (5%)
  between operations  1.41 us (2%)
    all_to_all x1, blocking collectives, per_device(): lax.all_to_all(jnp.broadcast_to(dots, (nx * ny, NZ)), ('gx', 'gy'), 0, 0,...  28.9 us
    pallas_call x6, Pallas kernels, call(): pl.pallas_call(kernel, out_shape=out_shape, in_specs=[spec(s) for s in in...  26.8 us
    ppermute x1, starting transfers between devices, per_device(): ylo = lax.ppermute(yhi_send, 'gy', up_y)  4.38 us
    ppermute x1, waiting for transfers between devices, per_device(): yhi = lax.ppermute(ylo_send, 'gy', down_y)  3.73 us
    unnamed x18, local copies, waits for them, and re-layouts  3.68 us
    ppermute x1, starting transfers between devices, per_device(): xlo = lax.ppermute(xhi_send, 'gx', up_x)  3.54 us
    ppermute x1, starting transfers between devices, per_device(): yhi = lax.ppermute(ylo_send, 'gy', down_y)  1.92 us
  transfers between devices with their start and end apart: 4, of which 1 were waited for; matrix products, arithmetic and copies ran while one was open for 0% of the time, Pallas kernels for 13%

profile of v2, /device:TPU:1, one launch (start us, length us, event | category | flops | bytes accessed | tf_op | source)
XLA Modules:
  0.0 75.8 jit_solution(14691783600254906665)
XLA Ops:
  0.6 0.1 pad_add_fusion.ids
  0.7 0.0 copy-start
  0.7 1.1 %copy-done = s32[3,16,32,128]{3,2,1,0:T(8,128)S(1)} copy-done((s32[3,16,32,128]{3,2,1,0:T(8,128)S(1)}, s32[3,16,32,128]{3,2,1,0:T(8,128)}, u32[]{:S(2)}) %copy-start) | copy-done | bytes 786456
  1.8 0.0 copy-start.2
  1.8 1.1 %copy-done.2 = f32[3,16,32,128]{3,2,1,0:T(8,128)S(1)} copy-done((f32[3,16,32,128]{3,2,1,0:T(8,128)S(1)}, f32[3,16,32,128]{3,2,1,0:T(8,128)}, u32[]{:S(2)}) %copy-start.2) | copy-done | bytes 786456
  3.0 0.0 copy-start.3
  3.0 0.7 copy-done.3
  3.7 0.0 copy-start.4
  3.7 0.7 copy-done.4
  4.4 0.0 copy-start.1
  4.4 0.0 copy-start.5
  4.4 0.0 copy-start.6
  4.4 0.0 copy-start.7
  4.4 0.0 copy-start.8
  4.4 1.7 %shard_map.104 = (f32[1536,128]{1,0:T(8,128)S(1)}, f32[144,128]{1,0:T(8,128)S(1)}, f32[144,128]{1,0:T(8,128)S(1)}) custom-call(s32[2]{0:T(128)S(1)} %pad_add_fusion.ids, s32[3,512]{1,0:T(4,128)S(1)} %bitcast.15, f32[3,512]{1,0:T(4,128)S(1)} %copy-done.4, f32[1536,128]{1,0:T(8,128)S(1)} %bitcast.13, s32[1536,128]{1,0:T(8,128)S(1)} %bitcast.10, ...), custom_call_target="tpu_custom_call" | custom-call | flops 400000 | bytes 2400000 | tf_op jit(solution)/shard_map/pallas_call | solution.py:34
  6.1 4.4 %collective-permute-start = (f32[144,128]{1,0:T(8,128)S(1)}, f32[144,128]{1,0:T(8,128)S(1)}, u32[]{:S(2)}, u32[]{:S(2)}) collective-permute-start(f32[144,128]{1,0:T(8,128)S(1)} %get-tuple-element.14), channel_id=1, source_target_pairs={{0,1},{1,2},{2,3},{3,4},{4,5},{5,6},{6,7},{8,9},{9,10},{10,11},{11... | collective-permute-start | bytes 221192 | tf_op jit(solution)/shard_map/ppermute | solution.py:533
  10.4 1.9 %collective-permute-start.1 = (f32[144,128]{1,0:T(8,128)S(1)}, f32[144,128]{1,0:T(8,128)S(1)}, u32[]{:S(2)}, u32[]{:S(2)}) collective-permute-start(f32[144,128]{1,0:T(8,128)S(1)} %get-tuple-element.15), channel_id=1, source_target_pairs={{1,0},{2,1},{3,2},{4,3},{5,4},{6,5},{7,6},{9,8},{10,9},{11,10},{12... | collective-permute-start | bytes 221192 | tf_op jit(solution)/shard_map/ppermute | solution.py:534
  12.4 0.0 collective-permute-done.ylo
  12.4 3.7 %collective-permute-done.1.yhi = f32[144,128]{1,0:T(8,128)S(1)} collective-permute-done((f32[144,128]{1,0:T(8,128)S(1)}, f32[144,128]{1,0:T(8,128)S(1)}, u32[]{:S(2)}, u32[]{:S(2)}) %collective-permute-start.1) | collective-permute-done | bytes 73760 | tf_op jit(solution)/shard_map/ppermute | solution.py:534
  16.1 0.0 copy-done.1
  16.1 0.1 shard_map.105
  16.2 3.5 %collective-permute-start.2 = (f32[360,128]{1,0:T(8,128)S(1)}, f32[360,128]{1,0:T(8,128)S(1)}, u32[]{:S(2)}, u32[]{:S(2)}) collective-permute-start(f32[360,128]{1,0:T(8,128)S(1)} %get-tuple-element.16), channel_id=1, source_target_pairs={{0,8},{8,16},{16,24},{24,32},{32,40},{40,48},{48,56},{56,64},{64,7... | collective-permute-start | bytes 552968 | tf_op jit(solution)/shard_map/ppermute | solution.py:547
  19.7 1.3 %collective-permute-start.3 = (f32[360,128]{1,0:T(8,128)S(1)}, f32[360,128]{1,0:T(8,128)S(1)}, u32[]{:S(2)}, u32[]{:S(2)}) collective-permute-start(f32[360,128]{1,0:T(8,128)S(1)} %get-tuple-element.17), channel_id=1, source_target_pairs={{8,0},{16,8},{24,16},{32,24},{40,32},{48,40},{56,48},{64,56},{72,6... | collective-permute-start | bytes 552968 | tf_op jit(solution)/shard_map/ppermute | solution.py:548
  21.7 0.0 copy-done.5
  21.7 0.0 copy-done.6
  21.7 0.0 copy-done.7
  21.7 0.0 copy-done.8
  21.7 7.0 %shard_map.106.coarse = f32[6,16,128]{2,1,0:T(8,128)S(1)} custom-call(s32[2]{0:T(128)S(1)} %pad_add_fusion.ids, f32[3,64]{1,0:T(4,128)S(1)} %copy-done.6, f32[3,128,128]{2,1,0:T(8,128)S(1)} %copy-done.5, f32[3,128]{1,0:T(4,128)S(1)} %copy-done.7, f32[1,128]{1,0:T(1,128)S(1)} %bitcast.18, f32[1]{0:T(128)S(6)} %copy.11.bout), custom_call_target="tpu_custom_call" | custom-call | flops 1500000000 | bytes 300000 | tf_op jit(solution)/shard_map/pallas_call | solution.py:34
  28.7 2.6 %shard_map.107 = (f32[960,128]{1,0:T(8,128)S(1)}, f32[960,128]{1,0:T(8,128)S(1)}, f32[512,128]{1,0:T(8,128)}) custom-call(s32[2]{0:T(128)S(1)} %pad_add_fusion.ids, f32[6,16,128]{2,1,0:T(8,128)S(1)} %shard_map.106.coarse), custom_call_target="tpu_custom_call" | custom-call | flops 8000000 | bytes 1300000 | tf_op jit(solution)/shard_map/pallas_call | solution.py:34
  31.3 0.0 collective-permute-done.2.xlo
  31.3 0.0 collective-permute-done.3.xhi
  31.3 14.1 %shard_map.108 = (f32[2880,128]{1,0:T(8,128)S(1)}, f32[2880,128]{1,0:T(8,128)S(1)}, f32[1,128]{1,0:T(1,128)S(1)}) custom-call(f32[1536,128]{1,0:T(8,128)S(1)} %get-tuple-element.13.r, s32[1536,128]{1,0:T(8,128)S(1)} %bitcast.12, f32[144,128]{1,0:T(8,128)S(1)} %collective-permute-done.ylo, f32[144,128]{1,0:T(8,128)S(1)} %collective-permute-done.1.yhi, ...), custom_call_target="tpu_custom_call" | custom-call | tf_op jit(solution)/shard_map/pallas_call | solution.py:34
  45.4 0.1 broadcast_in_dim.2
  45.5 28.9 %all_to_all.8 = f32[256,1,128]{2,1,0:T(1,128)S(1)} all-to-all(f32[256,1,128]{2,1,0:T(1,128)S(1)} %broadcast_in_dim.2), channel_id=1, replica_groups=mesh['gx'=32,'gy'=8] {'gx','gy'}, dimensions={0} | all-to-all | bytes 262144 | tf_op jit(solution)/shard_map/all_to_all | solution.py:561
  74.4 1.4 %shard_map.109 = f32[1536,128]{1,0:T(8,128)} custom-call(f32[256,128]{1,0:T(8,128)S(1)} %bitcast.14, f32[2880,128]{1,0:T(8,128)S(1)} %get-tuple-element.21.z, f32[2880,128]{1,0:T(8,128)S(1)} %get-tuple-element.22.y), custom_call_target="tpu_custom_call" | custom-call | tf_op jit(solution)/shard_map/pallas_call | solution.py:34
Async XLA Ops:
  0.7 1.1 %copy-start = (s32[3,16,32,128]{3,2,1,0:T(8,128)S(1)}, s32[3,16,32,128]{3,2,1,0:T(8,128)}, u32[]{:S(2)}) copy-start(s32[3,16,32,128]{3,2,1,0:T(8,128)} %param.10) | copy-start | bytes 2359300
  1.8 1.1 %copy-start.2 = (f32[3,16,32,128]{3,2,1,0:T(8,128)S(1)}, f32[3,16,32,128]{3,2,1,0:T(8,128)}, u32[]{:S(2)}) copy-start(f32[3,16,32,128]{3,2,1,0:T(8,128)} %param.9) | copy-start | bytes 2359300
  3.0 0.7 copy-start.3
  3.7 0.7 copy-start.4
  4.4 11.7 %copy-start.1 = (s32[3,16,32,128]{3,2,1,0:T(8,128)S(1)}, s32[3,16,32,128]{3,2,1,0:T(8,128)}, u32[]{:S(2)}) copy-start(s32[3,16,32,128]{3,2,1,0:T(8,128)} %param.10) | copy-start | bytes 2359300
  4.4 17.3 %copy-start.5 = (f32[3,128,128]{2,1,0:T(8,128)S(1)}, f32[3,128,128]{2,1,0:T(8,128)}, u32[]{:S(2)}) copy-start(f32[3,128,128]{2,1,0:T(8,128)} %weights.1) | copy-start | bytes 589828
  4.4 17.3 %copy-start.6 = (f32[3,64]{1,0:T(4,128)S(1)}, f32[3,64]{1,0:T(4,128)}, u32[]{:S(2)}) copy-start(f32[3,64]{1,0:T(4,128)} %freq.1) | copy-start | bytes 2308
  4.4 17.3 %copy-start.7 = (f32[3,128]{1,0:T(4,128)S(1)}, f32[3,128]{1,0:T(4,128)}, u32[]{:S(2)}) copy-start(f32[3,128]{1,0:T(4,128)} %biases.1) | copy-start | bytes 4612
  4.4 17.3 %copy-start.8 = (f32[128]{0:T(128)S(1)}, f32[128]{0:T(128)}, u32[]{:S(2)}) copy-start(f32[128]{0:T(128)} %param.16) | copy-start | bytes 1540
  6.1 6.3 %collective-permute-start = (f32[144,128]{1,0:T(8,128)S(1)}, f32[144,128]{1,0:T(8,128)S(1)}, u32[]{:S(2)}, u32[]{:S(2)}) collective-permute-start(f32[144,128]{1,0:T(8,128)S(1)} %get-tuple-element.14), channel_id=1, source_target_pairs={{0,1},{1,2},{2,3},{3,4},{4,5},{5,6},{6,7},{8,9},{9,10},{10,11},{11... | collective-permute-start | bytes 221192 | tf_op jit(solution)/shard_map/ppermute | solution.py:533
  10.4 5.7 %collective-permute-start.1 = (f32[144,128]{1,0:T(8,128)S(1)}, f32[144,128]{1,0:T(8,128)S(1)}, u32[]{:S(2)}, u32[]{:S(2)}) collective-permute-start(f32[144,128]{1,0:T(8,128)S(1)} %get-tuple-element.15), channel_id=1, source_target_pairs={{1,0},{2,1},{3,2},{4,3},{5,4},{6,5},{7,6},{9,8},{10,9},{11,10},{12... | collective-permute-start | bytes 221192 | tf_op jit(solution)/shard_map/ppermute | solution.py:534
  16.2 15.1 %collective-permute-start.2 = (f32[360,128]{1,0:T(8,128)S(1)}, f32[360,128]{1,0:T(8,128)S(1)}, u32[]{:S(2)}, u32[]{:S(2)}) collective-permute-start(f32[360,128]{1,0:T(8,128)S(1)} %get-tuple-element.16), channel_id=1, source_target_pairs={{0,8},{8,16},{16,24},{24,32},{32,40},{40,48},{48,56},{56,64},{64,7... | collective-permute-start | bytes 552968 | tf_op jit(solution)/shard_map/ppermute | solution.py:547
  19.7 11.6 %collective-permute-start.3 = (f32[360,128]{1,0:T(8,128)S(1)}, f32[360,128]{1,0:T(8,128)S(1)}, u32[]{:S(2)}, u32[]{:S(2)}) collective-permute-start(f32[360,128]{1,0:T(8,128)S(1)} %get-tuple-element.17), channel_id=1, source_target_pairs={{8,0},{16,8},{24,16},{32,24},{40,32},{48,40},{56,48},{64,56},{72,6... | collective-permute-start | bytes 552968 | tf_op jit(solution)/shard_map/ppermute | solution.py:548

commit v3 on v2

v3 whole, which is shorter than its diff:
```python
import functools
import math

import jax
import jax.numpy as jnp
from jax import lax
from jax.experimental import pallas as pl
from jax.experimental.pallas import tpu as pltpu
from jax.sharding import PartitionSpec as P

CF = 4
NX, NY, NZ = 16, 32, 128
TOTAL_X, TOTAL_Y = 512, 256
CX, CY, CZ = NX // CF, NY // CF, NZ // CF
GX, GY = CX + 2, CY + 2
EX, EY = GX * CF, GY * CF
SIZE = EX * EY
LOADS = 512
NU, MU = 0.3, 1.0 / 2.6
LAM = 0.3 / (1.3 * 0.4)
RATIO = LAM / MU
DIAG = (LAM + 4.0 * MU) / 9.0
VMEM = pltpu.VMEM
SMEM = pltpu.SMEM
highest = lax.Precision.HIGHEST
f32 = jnp.float32


def spec(space=VMEM):
    return pl.BlockSpec(memory_space=space)


def call(kernel, out_shape, in_spaces, args, scratch=(), cost=None, out_spaces=None, aliases=None, limit=16):
    out_specs = jax.tree.map(lambda _: spec(), out_shape)
    if out_spaces is not None:
        out_specs = jax.tree.map(lambda _, space: spec(space), out_shape, out_spaces)
    args = [
        pltpu.with_memory_space_constraint(a, space) if space is pltpu.HBM else a
        for a, space in zip(args, in_spaces)
    ]
    if out_spaces is not None:
        out_shape = jax.tree.map(
            lambda a, space: pltpu.HBM(a.shape, a.dtype) if space is pltpu.HBM else a, out_shape, out_spaces
        )
    return pl.pallas_call(
        kernel,
        out_shape=out_shape,
        in_specs=[spec(s) for s in in_spaces],
        out_specs=out_specs,
        scratch_shapes=list(scratch),
        input_output_aliases=aliases or {},
        compiler_params=pltpu.CompilerParams(vmem_limit_bytes=limit << 20),
        cost_estimate=cost,
    )(*args)


def shape(*dims):
    return jax.ShapeDtypeStruct(dims, f32)


def pack_kernel(
    ids, nodes, forces, body, fixed,
    load, free, lo_out, hi_out,
    body_v, fixed_v, nodes_v, nodes_s, forces_s, sem,
):
    part = NX * NY
    copies = [
        pltpu.make_async_copy(nodes, nodes_v, sem.at[0]),
        pltpu.make_async_copy(nodes, nodes_s, sem.at[1]),
        pltpu.make_async_copy(forces, forces_s, sem.at[2]),
    ]
    for c in range(3):
        for k, (src, dst) in enumerate(((body, body_v), (fixed, fixed_v))):
            rows = pl.ds(c * part, part)
            copies.append(pltpu.make_async_copy(src.at[rows, :], dst.at[rows, :], sem.at[3 + 2 * c + k]))
    for copy in copies:
        copy.start()

    zero = jnp.zeros((8, NZ), f32)

    def clear(x, carry):
        for c in range(3):
            base = pl.multiple_of(c * SIZE + x * EY, 8)
            for ref in (load, free):
                ref[pl.ds(base, 8), :] = zero
                ref[pl.ds(base + EY - 8, 8), :] = zero
        return carry

    lax.fori_loop(CF, CF + NX, clear, 0, unroll=2)

    start_x = ids[0] * NX
    start_y = ids[1] * NY
    for copy in copies[:3]:
        copy.wait()
    lx = nodes_v[0:1, :] - start_x
    ly = nodes_v[1:2, :] - start_y
    mine = (lx >= 0) & (lx < NX) & (ly >= 0) & (ly < NY)
    index = lax.broadcasted_iota(jnp.int32, (1, LOADS), 1)
    todo = jnp.where(mine, index, LOADS)
    lane = lax.broadcasted_iota(jnp.int32, (1, NZ), 1)
    first = jnp.min(todo)
    for copy in copies[3:]:
        copy.wait()

    def more(p):
        return p < LOADS

    def add_one(p):
        x = nodes_s[0, p] - start_x
        y = nodes_s[1, p] - start_y
        hit = lane == nodes_s[2, p]
        for c in range(3):
            row = pl.ds((c * NX + x) * NY + y, 1)
            body_v[row, :] = body_v[row, :] + jnp.where(hit, forces_s[c, p], 0.0)
        return jnp.min(jnp.where(todo > p, todo, LOADS))

    lax.while_loop(more, add_one, first)

    def mask(x, carry):
        for c in range(3):
            src = pl.ds(pl.multiple_of((c * NX + x) * NY, NY), NY)
            dst = pl.ds(c * SIZE + (x + CF) * EY + CF, NY)
            ok = fixed_v[src, :] == 0
            load[dst, :] = jnp.where(ok, body_v[src, :], 0.0)
            free[dst, :] = jnp.where(ok, 1.0, 0.0)
        return carry

    lax.fori_loop(0, NX, mask, 0, unroll=2)
    for c in range(3):
        base = c * SIZE + CF * EY + CF
        for j in range(2):
            to = pl.ds((c * 2 + j) * NX, NX)
            lo_out[to, :] = load[pl.ds(base + j, NX, stride=EY), :]
            hi_out[to, :] = load[pl.ds(base + NY - 2 + j, NX, stride=EY), :]
        to = pl.ds((6 + c) * NX, NX)
        lo_out[to, :] = free[pl.ds(base, NX, stride=EY), :]
        hi_out[to, :] = free[pl.ds(base + NY - 1, NX, stride=EY), :]


def planes_kernel(load, free, ylo, yhi, coarse, lo_out, hi_out):
    del coarse
    for out, first in ((lo_out, CF), (hi_out, CF + NX - 2)):
        for c in range(3):
            for j in range(2):
                x = first + j
                base = (c * 2 + j) * EY
                out[pl.ds(base, EY), :] = load[pl.ds(c * SIZE + x * EY, EY), :]
                for k in range(2):
                    at = pl.ds((c * 2 + k) * NX + x - CF, 1)
                    out[pl.ds(base + 2 + k, 1), :] = ylo[at, :]
                    out[pl.ds(base + 36 + k, 1), :] = yhi[at, :]
            x = CF if first == CF else CF + NX - 1
            base = (6 + c) * EY
            out[pl.ds(base, EY), :] = free[pl.ds(c * SIZE + x * EY, EY), :]
            at = pl.ds((6 + c) * NX + x - CF, 1)
            out[pl.ds(base + 3, 1), :] = ylo[at, :]
            out[pl.ds(base + 36, 1), :] = yhi[at, :]


def split2(v):
    hi = v.astype(jnp.bfloat16)
    return hi, (v - hi.astype(f32)).astype(jnp.bfloat16)


def doubled(w):
    hi, lo = split2(w)
    both = jnp.concatenate([hi, lo], axis=1)
    return jnp.concatenate([both, both], axis=0)


def sine_of_turns(t):
    t = t - jnp.round(t)
    a = jnp.abs(t)
    x = jnp.minimum(a, 0.5 - a) * (2.0 * math.pi)
    x2 = x * x
    p = 1.0 / 6227020800.0
    for k in (39916800.0, 362880.0, 5040.0, 120.0, 6.0, 1.0):
        p = 1.0 / k - x2 * p
    p = x * p
    return jnp.where(t < 0.0, -p, p)


GROUP = 3


def mlp_kernel(ids, freq, weights, biases, wout, bout, coarse, axy, bxy, w2):
    cx0 = ids[0] * CX - 1
    cy0 = ids[1] * CY - 1
    f = freq[...]
    ff = jnp.concatenate([f, f], axis=1)
    first = lax.broadcasted_iota(jnp.int32, (1, 128), 1) < 64
    quarter = jnp.where(first, 0.0, 0.25)

    def waves(row, start, rows, total):
        i = lax.broadcasted_iota(jnp.int32, (rows, 128), 0) + start
        turns = ff[row : row + 1, :] * ((i.astype(f32) + 0.5) * (1.0 / total))
        turns = turns - jnp.round(turns)
        wave = sine_of_turns(turns + quarter)
        return wave, pltpu.roll(wave, 64, 1)

    wx, ox = waves(0, cx0, 8, TOTAL_X // CF)
    wy, oy = waves(1, cy0, 16, TOTAL_Y // CF)
    wz, oz = waves(2, 0, CZ, CZ)
    cosx, sinx = jnp.where(first, ox, wx), jnp.where(first, wx, ox)
    cosz, sinz = jnp.where(first, oz, wz), jnp.where(first, wz, oz)
    turnedy = jnp.where(first, oy, -oy)
    for i in range(GX):
        c, s = cosx[i : i + 1, :], sinx[i : i + 1, :]
        axy[pl.ds(16 * i, 16), :] = wy * c + turnedy * s
        bxy[pl.ds(16 * i, 16), :] = turnedy * c - wy * s

    for l in range(3):
        w2[l] = doubled(weights[l] * 0.5)
    w2[3] = doubled(jnp.broadcast_to(wout[...], (128, 128)).T)
    pick = lax.broadcasted_iota(jnp.int32, (CZ, 128), 0) == (
        lax.broadcasted_iota(jnp.int32, (CZ, 128), 1) // CF
    )
    row16 = lax.broadcasted_iota(jnp.int32, (16, 128), 0)

    def body(i, carry):
        parts = []
        for k in range(GROUP):
            for j in range(GY):
                at = pl.ds(16 * (GROUP * i + k) + j, 1)
                parts.append(axy[at, :] * cosz + bxy[at, :] * sinz)
        h = jnp.concatenate(parts, axis=0)
        for l in range(4):
            hi, lo = split2(h)
            both = jnp.concatenate([hi, lo], axis=1)
            out = jnp.dot(both, w2[l], preferred_element_type=f32)
            h = out[:, :128] + out[:, 128:]
            if l < 3:
                h = h + biases[l : l + 1, :] * 0.5
                h = h + h * jnp.tanh(h)
        for k in range(GROUP):
            logits = jnp.zeros((16, 128), f32)
            for j in range(GY):
                cell = (k * GY + j) * CZ
                line = jnp.sum(jnp.where(pick, h[cell : cell + CZ, :], 0.0), axis=0, keepdims=True)
                logits = jnp.where(row16 == (j + 15) % 16, line, logits)
            coarse[GROUP * i + k] = 1.0 / (1.0 + jnp.exp(-(logits + bout[0])))
        return carry

    lax.fori_loop(0, GX // GROUP, body, 0)


W0, W1, W2, W3 = 2.0, 1.0, 2.0 - math.sqrt(2.0), 2.0 - math.sqrt(3.0)
SCALE = MU / 16.0


def density_kernel(ids, coarse, young, inverse, density, density_v, sem):
    lane = lax.broadcasted_iota(jnp.int32, (16, NZ), 1)
    not_last, not_first = lane < NZ - 1, lane > 0
    row16 = lax.broadcasted_iota(jnp.int32, (16, NZ), 0)
    y_cell = ids[1] * CY + jnp.where(row16 == 15, -1, row16)
    inside_y = (y_cell >= 0) & (y_cell < TOTAL_Y // CF)

    ri = lax.broadcasted_iota(jnp.int32, (EY + NY, 144), 0)
    ci = lax.broadcasted_iota(jnp.int32, (EY + NY, 144), 1)
    r = jnp.where(ri < EY, ri, ri - EY + CF)
    oy = r & 3
    kind = jnp.where(oy == 0, 0, jnp.where(oy == 3, 2, 1))
    want = kind * 16 + (((r >> 2) + 15) & 15)
    spread = jnp.where(
        (ci == want) | (ci == want + 48) | (ci == want + 96), 1.0, 0.0
    ).astype(jnp.bfloat16)
    y_fine = ids[1] * NY - CF + lax.broadcasted_iota(jnp.int32, (EY, NZ), 0)
    inside_rows = jnp.where((y_fine >= 0) & (y_fine < TOTAL_Y), SCALE, 0.0)

    def layers(v):
        side = jnp.where(not_last, pltpu.roll(v, NZ - 1, 1), 0.0) + jnp.where(
            not_first, pltpu.roll(v, 1, 1), 0.0
        )
        return W0 * v + W1 * side, W1 * v + W2 * side, W2 * v + W3 * side

    side = jnp.where(not_last, 1.0, 0.0) + jnp.where(not_first, 1.0, 0.0)
    ones = (W0 + W1 * side, W1 + W2 * side, W2 + W3 * side)
    rows_in = jnp.where(inside_y, 1.0, 0.0)
    stacks = []
    for i in range(GX):
        x_cell = ids[0] * CX - 1 + i
        ok_x = (x_cell >= 0) & (x_cell < TOTAL_X // CF)
        inside = jnp.where(inside_y & ok_x, 1.0, 0.0)
        stacks.append((
            layers(jnp.where(inside > 0.0, coarse[i], 0.0)),
            [inside * w for w in ones],
            inside > 0.0,
            jnp.where(ok_x, 1.0, 0.0),
        ))

    for i in range(GX):
        for plane_kind in range(3):
            low = max(i - 1, 0) if plane_kind == 0 else i
            high = min(i + 1, GX - 1) if plane_kind == 2 else i
            sums = []
            for which in range(2):
                here, below, over = stacks[i][which], stacks[low][which], stacks[high][which]
                t0 = here[0] + (below[1] + over[1])
                t1 = here[1] + (below[2] + over[2])
                down = pltpu.roll(t1, 1, 0)
                above = pltpu.roll(t1, 15, 0)
                sums.append((t0 + (down + t1), t0 + (t1 + t1), t0 + (t1 + above)))
            rho = jnp.concatenate(
                [a / jnp.where(stacks[i][2], b, 1.0) for a, b in zip(*sums)], axis=0
            )
            hi = rho.astype(jnp.bfloat16)
            rest = rho - hi.astype(f32)
            mid = rest.astype(jnp.bfloat16)
            lo = (rest - mid.astype(f32)).astype(jnp.bfloat16)
            fine = jnp.dot(spread, jnp.concatenate([hi, mid, lo], axis=0), preferred_element_type=f32)
            ext = fine[:EY, :]
            modulus = (0.02 + 0.98 * (ext * ext * ext)) * (inside_rows * stacks[i][3])
            for ox in {0: (0,), 1: (1, 2), 2: (3,)}[plane_kind]:
                x = i * CF + ox
                young[pl.ds(x * EY, EY), :] = modulus
                if 1 <= i <= CX:
                    density_v[pl.ds((x - CF) * NY, NY), :] = fine[EY:, :]

    copy = pltpu.make_async_copy(density_v, density, sem)
    copy.start()
    lane8 = lax.broadcasted_iota(jnp.int32, (8, NZ), 1) > 0

    def plane(x, carry):
        for j in range(EY // 8):
            at = x * EY + 8 * j
            if j == 0:
                at = pl.multiple_of(at, 8)
            total = (young[pl.ds(at, 8), :] + young[pl.ds(at - 1, 8), :]) + (
                young[pl.ds(at - EY, 8), :] + young[pl.ds(at - EY - 1, 8), :]
            )
            total = total + jnp.where(lane8, pltpu.roll(total, 1, 1), 0.0)
            inverse[pl.ds(at, 8), :] = 1.0 / (DIAG / SCALE * total + 1e-30)
        return carry

    lax.fori_loop(2, 22, plane, 0, unroll=2)
    copy.wait()


QUANTITIES = 4
BLOCKS = EY // 8
TALL = EY + 8


def operator_pass(zsum, zdiff, young, above, minus, plus, begin, end, unroll):
    def block(yb, carry):
        r0 = yb * 8

        def transform(x):
            out = []
            for c in range(3):
                at = c * SIZE + x * EY + r0
                pairs = [(t[pl.ds(at, 8), :], t[pl.ds(at + 1, 8), :]) for t in (zsum, zdiff)]
                out += [v + u for v, u in pairs] + [u - v for v, u in pairs]
            return out

        def modal(x, a, b):
            e1 = young[pl.ds(pl.multiple_of(x * EY + r0, 8), 8), :]
            e3 = e1 * (1.0 / 3.0)
            e31 = e1 * 0.5
            e9 = e1 * ((RATIO + 4.0) / 9.0)
            s = [p + q for p, q in zip(a, b)]
            d = [q - p for p, q in zip(a, b)]
            u = lambda c, p, q, r: (d if p else s)[4 * c + 2 * q + r]
            g = {}
            ux, uy, uz = u(0, 1, 0, 0), u(1, 0, 1, 0), u(2, 0, 0, 1)
            trace = RATIO * (ux + uy + uz)
            g[0, 1, 0, 0] = e1 * ((ux + ux) + trace)
            g[1, 0, 1, 0] = e1 * ((uy + uy) + trace)
            g[2, 0, 0, 1] = e1 * ((uz + uz) + trace)
            g[0, 0, 1, 0] = g[1, 1, 0, 0] = e1 * (u(0, 0, 1, 0) + u(1, 1, 0, 0))
            g[0, 0, 0, 1] = g[2, 1, 0, 0] = e1 * (u(0, 0, 0, 1) + u(2, 1, 0, 0))
            g[1, 0, 0, 1] = g[2, 0, 1, 0] = e1 * (u(1, 0, 0, 1) + u(2, 0, 1, 0))
            for one, two in (
                ((0, 1, 0, 1), (1, 0, 1, 1)),
                ((0, 1, 1, 0), (2, 0, 1, 1)),
                ((1, 1, 1, 0), (2, 1, 0, 1)),
            ):
                p, q = u(*one), u(*two)
                g[one] = e31 * (3.0 * p + q)
                g[two] = e31 * (3.0 * q + p)
            p, q, r = u(0, 0, 1, 1), u(1, 1, 0, 1), u(2, 1, 1, 0)
            total = p + q + r
            g[0, 0, 1, 1] = e3 * (p + total)
            g[1, 1, 0, 1] = e3 * (q + total)
            g[2, 1, 1, 0] = e3 * (r + total)
            for c in range(3):
                g[c, 1, 1, 1] = e9 * u(c, 1, 1, 1)
            return g

        def keep(g):
            out = []
            for c in range(3):
                out.append(g[c, 1, 0, 0])
                for q, r in ((0, 1), (1, 0), (1, 1)):
                    out.append(g[c, 0, q, r] + g[c, 1, q, r])
            return out

        def step(x, state):
            a, held = state
            b = transform(x + 1)
            g = modal(x, a, b)
            for c in range(3):
                f = [held[4 * c] - g[c, 1, 0, 0]]
                for k, (q, r) in enumerate(((0, 1), (1, 0), (1, 1))):
                    f.append((g[c, 0, q, r] - g[c, 1, q, r]) + held[4 * c + 1 + k])
                h = []
                for r in range(2):
                    at = ((2 * c + r) * EX + x) * TALL + 8 + r0
                    above[pl.ds(at, 8), :] = f[r] + f[2 + r]
                    h.append((f[r] - f[2 + r]) + above[pl.ds(at - 1, 8), :])
                rows = pl.ds(pl.multiple_of(c * SIZE + x * EY + r0, 8), 8)
                minus[rows, :] = h[0] - h[1]
                plus[rows, :] = h[0] + h[1]
            return b, keep(g)

        a = transform(begin)
        b = transform(begin + 1)
        lax.fori_loop(begin + 1, end, step, (b, keep(modal(begin, a, b))), unroll=unroll)
        return carry

    lax.fori_loop(0, BLOCKS, block, 0)


def main_kernel(
    load_in, free_in, ylo, yhi, xlo, xhi, young, inverse,
    load, free, field, scaled, dots_out,
    zsum, zdiff, above, minus, plus,
):
    del load_in, free_in
    zero = jnp.zeros((8, NZ), f32)
    lane = lax.broadcasted_iota(jnp.int32, (8, NZ), 1)
    not_last, not_first = lane < NZ - 1, lane > 0

    for c in range(3):
        for k in range(2):
            for strip, row in ((ylo, 2 + k), (yhi, 36 + k)):
                load[pl.ds(c * SIZE + CF * EY + row, NX, stride=EY), :] = strip[
                    pl.ds((c * 2 + k) * NX, NX), :
                ]
            for plane, x in ((xlo, 2 + k), (xhi, 20 + k)):
                load[pl.ds(c * SIZE + x * EY, EY), :] = plane[pl.ds((c * 2 + k) * EY, EY), :]
        for strip, row in ((ylo, 3), (yhi, 36)):
            free[pl.ds(c * SIZE + CF * EY + row, NX, stride=EY), :] = strip[pl.ds((6 + c) * NX, NX), :]
        for plane, x in ((xlo, 3), (xhi, 20)):
            free[pl.ds(c * SIZE + x * EY, EY), :] = plane[pl.ds((6 + c) * EY, EY), :]
    for ref in (zsum, zdiff):
        ref[pl.ds(3 * SIZE, 8), :] = zero

    def z_stage(at, v):
        n = jnp.where(not_last, pltpu.roll(v, NZ - 1, 1), 0.0)
        zsum[at, :] = v + n
        zdiff[at, :] = n - v

    def prepare(x, carry):
        for j in range(BLOCKS):
            base = pl.multiple_of(x * EY, 8) + 8 * j
            inv = inverse[pl.ds(base, 8), :]
            for c in range(3):
                at = pl.ds(base + c * SIZE, 8)
                v = load[at, :] * inv
                field[at, :] = v
                z_stage(at, v)
        return carry

    lax.fori_loop(2, 22, prepare, 0, unroll=2)

    for c in range(3):
        for ref in (zsum, zdiff):
            ref[pl.ds(c * SIZE + 22 * EY, 8), :] = zero

    def clear_above(i, carry):
        above[pl.ds(pl.multiple_of(i * TALL, 8), 8), :] = zero
        return carry

    lax.fori_loop(0, 6 * EX, clear_above, 0, unroll=8)

    operator_pass(zsum, zdiff, young, above, minus, plus, 2, 21, 3)

    row = lax.broadcasted_iota(jnp.int32, (8, NZ), 0)
    first_rows = jnp.where(row >= CF, 1.0, 0.0)
    last_rows = jnp.where(row < CF, 1.0, 0.0)

    def gather(totals, j, terms):
        for k, t in enumerate(terms):
            if j == 0:
                t = t * first_rows
            if j == BLOCKS - 1:
                t = t * last_rows
            totals[k] = t if totals[k] is None else totals[k] + t

    def force(at):
        return minus[at, :] + jnp.where(not_first, pltpu.roll(plus[at, :], 1, 1), 0.0)

    def finish_one(x, dots):
        totals = [None] * 3
        for j in range(BLOCKS):
            base = pl.multiple_of(x * EY, 8) + 8 * j
            inv = inverse[pl.ds(base, 8), :]
            sums = None
            for c in range(3):
                at = pl.ds(base + c * SIZE, 8)
                w = free[at, :] * force(at)
                y = w * inv
                z = field[at, :]
                zt = z - y
                scaled[at, :] = y
                z_stage(at, zt)
                if dots is not None:
                    rt = load[at, :] - w
                    terms = (z * w, z * rt, zt * rt)
                    sums = terms if sums is None else [p + q for p, q in zip(sums, terms)]
            if dots is not None:
                gather(totals, j, sums)
        return dots if dots is None else [p + q for p, q in zip(dots, totals)]

    finish_one(CF - 1, None)
    finish_one(CF + NX, None)
    dots = lax.fori_loop(CF, CF + NX, finish_one, [zero] * 3, unroll=2)

    operator_pass(zsum, zdiff, young, above, minus, plus, 3, 20, 4)

    def finish_two(x, dots):
        totals = [None] * 1
        for j in range(BLOCKS):
            base = pl.multiple_of(x * EY, 8) + 8 * j
            sums = None
            for c in range(3):
                at = pl.ds(base + c * SIZE, 8)
                q = free[at, :] * force(at)
                terms = ((field[at, :] - scaled[at, :]) * q,)
                sums = terms if sums is None else [a + b for a, b in zip(sums, terms)]
            gather(totals, j, sums)
        return [p + q for p, q in zip(dots, totals)]

    dots = dots + lax.fori_loop(CF, CF + NX, finish_two, [zero], unroll=2)
    one = lax.broadcasted_iota(jnp.int32, (1, NZ), 1)
    line = jnp.zeros((1, NZ), f32)
    for k, d in enumerate(dots):
        line = jnp.where(one == k, jnp.sum(d), line)
    dots_out[...] = line


def final_kernel(parts, z, y, out, out_v, sem):
    total = jnp.sum(parts[...], axis=0, keepdims=True)
    lane = lax.broadcasted_iota(jnp.int32, (1, NZ), 1)
    zw, a, b, c = (
        jnp.sum(jnp.where(lane == k, total, 0.0), axis=1, keepdims=True) for k in range(QUANTITIES)
    )
    rz = zw + a
    alpha = rz / zw
    less = -(a / zw)
    rz1 = alpha * (alpha * b + less * a)
    energy = less * (less * zw) + 2.0 * alpha * (less * (a - b)) + alpha * (alpha * c)
    beta = rz1 / rz
    alpha1 = rz1 / (energy - beta * (rz1 / alpha))
    c1 = jnp.broadcast_to(alpha + alpha1 * (1.0 + beta), (8, NZ))[0:1, :]
    c2 = jnp.broadcast_to(-(alpha * alpha1), (8, NZ))[0:1, :]
    copies = []
    for c in range(3):
        def body(x, carry, c=c):
            src = pl.ds(c * SIZE + (x + CF) * EY + CF, NY)
            to = pl.ds(pl.multiple_of((c * NX + x) * NY, NY), NY)
            out_v[to, :] = c1 * z[src, :] + c2 * y[src, :]
            return carry

        lax.fori_loop(0, NX, body, 0, unroll=4)
        rows = pl.ds(c * NX * NY, NX * NY)
        copy = pltpu.make_async_copy(out_v.at[rows, :], out.at[rows, :], sem.at[c])
        copy.start()
        copies.append(copy)
    for copy in copies:
        copy.wait()


def per_device(
    body_force, fixed_dofs, load_nodes, load_forces, frequencies,
    hidden_weights, hidden_biases, output_weights, output_bias,
):
    bx, by = lax.axis_index("gx"), lax.axis_index("gy")
    ids = jnp.stack([bx, by]).astype(jnp.int32)
    rows = 3 * NX * NY
    body = body_force.reshape(rows, NZ)
    fixed = fixed_dofs.reshape(rows, NZ)
    nodes = load_nodes.T
    strip = shape(9 * NX, NZ)
    ext = shape(3 * SIZE, NZ)
    load, free, ylo_send, yhi_send = call(
        pack_kernel, (ext, ext, strip, strip),
        [SMEM] + [pltpu.HBM] * 4, (ids, nodes, load_forces, body, fixed),
        scratch=[VMEM((rows, NZ), f32), VMEM((rows, NZ), jnp.int32), VMEM((3, LOADS), jnp.int32),
                 SMEM((3, LOADS), jnp.int32), SMEM((3, LOADS), f32), pltpu.SemaphoreType.DMA((9,))],
        cost=pl.CostEstimate(flops=400000, transcendentals=0, bytes_accessed=2400000),
    )
    ny, nx = lax.axis_size("gy"), lax.axis_size("gx")
    up_y = [(i, i + 1) for i in range(ny - 1)]
    down_y = [(i + 1, i) for i in range(ny - 1)]
    up_x = [(i, i + 1) for i in range(nx - 1)]
    down_x = [(i + 1, i) for i in range(nx - 1)]
    ylo = lax.ppermute(yhi_send, "gy", up_y)
    yhi = lax.ppermute(ylo_send, "gy", down_y)

    coarse = call(
        mlp_kernel, shape(GX, 16, 128),
        [SMEM, VMEM, VMEM, VMEM, VMEM, SMEM],
        (ids, frequencies, hidden_weights, hidden_biases, output_weights.reshape(1, 128), output_bias),
        scratch=[VMEM((16 * GX, 128), f32), VMEM((16 * GX, 128), f32), VMEM((4, 256, 256), jnp.bfloat16)],
        cost=pl.CostEstimate(flops=1500000000, transcendentals=800000, bytes_accessed=300000),
    )
    plane = shape(9 * EY, NZ)
    xlo_send, xhi_send = call(
        planes_kernel, (plane, plane), [VMEM] * 5, (load, free, ylo, yhi, coarse),
    )
    xlo = lax.ppermute(xhi_send, "gx", up_x)
    xhi = lax.ppermute(xlo_send, "gx", down_x)
    young, inverse, density = call(
        density_kernel, (shape(SIZE, NZ), shape(SIZE, NZ), shape(NX * NY, NZ)),
        [SMEM, VMEM], (ids, coarse),
        scratch=[VMEM((NX * NY, NZ), f32), pltpu.SemaphoreType.DMA],
        out_spaces=(VMEM, VMEM, pltpu.HBM),
        cost=pl.CostEstimate(flops=8000000, transcendentals=0, bytes_accessed=1300000),
    )
    tail = VMEM((3 * SIZE + 8, NZ), f32)
    work = VMEM((3 * SIZE, NZ), f32)
    _, _, z, y, dots = call(
        main_kernel, (ext, ext, ext, ext, shape(1, NZ)),
        [VMEM] * 8, (load, free, ylo, yhi, xlo, xhi, young, inverse),
        scratch=[tail, tail, VMEM((6 * EX * TALL, NZ), f32), work, work],
        aliases={0: 0, 1: 1}, limit=20,
    )
    parts = lax.all_to_all(
        jnp.broadcast_to(dots, (nx * ny, NZ)), ("gx", "gy"), 0, 0, tiled=True
    )
    out = call(
        final_kernel, shape(rows, NZ), [VMEM] * 3, (parts, z, y),
        scratch=[VMEM((rows, NZ), f32), pltpu.SemaphoreType.DMA((3,))], out_spaces=pltpu.HBM,
    )
    return out.reshape(3, NX, NY, NZ), density.reshape(NX, NY, NZ)


def solution(mesh):
    return jax.shard_map(
        per_device,
        mesh=mesh,
        in_specs=(P(None, "gx", "gy", None), P(None, "gx", "gy", None)) + (P(),) * 7,
        out_specs=(P(None, "gx", "gy", None), P("gx", "gy", None)),
        check_vma=False,
    )
```

time: 75.7 us -> 67.1 us (0.89)
  Pallas kernels: 26.8 us -> 19.2 us
  local copies, waits for them, and re-layouts: 3.75 us -> 0.09 us
  blocking collectives: 28.9 us -> 31.4 us
    pallas_call x6, Pallas kernels: 26.8 us -> 19.2 us  [call(): pl.pallas_call(kernel, out_shape=out_shape, in_specs=[spec(s) for s in in...]
    unnamed x18 -> x8, local copies, waits for them, and re-layouts: 3.68 us -> 0.02 us
    ppermute x1, waiting for transfers between devices: 0.01 us -> 3.16 us  [per_device(): xhi = lax.ppermute(xlo_send, 'gx', down_x)]
    ppermute x1, waiting for transfers between devices: 3.73 us -> 0.68 us  [per_device(): yhi = lax.ppermute(ylo_send, 'gy', down_y)]
    all_to_all x1, blocking collectives: 28.9 us -> 31.4 us  [per_device(): lax.all_to_all(jnp.broadcast_to(dots, (nx * ny, NZ)), ('gx', 'gy'), 0, 0,...]
    ppermute x1, starting transfers between devices: 3.54 us -> 2.51 us  [per_device(): xlo = lax.ppermute(xhi_send, 'gx', up_x)]
  transfers between devices with their start and end apart: 4 -> 4, of which waited for: 1 -> 2; matrix products, arithmetic and copies ran while one was open for 0% -> 0% of each run, Pallas kernels for 13% -> 7%
where the time goes in v3:
time: 67.1 us; the launch traced here: 66.5 us
  blocking collectives  31.4 us (47%)
  Pallas kernels  19.2 us (29%)
  starting transfers between devices  10.5 us (16%)
  waiting for transfers between devices  3.85 us (6%)
  between operations  1.44 us (2%)
    all_to_all x1, blocking collectives, per_device(): lax.all_to_all(jnp.broadcast_to(dots, (nx * ny, NZ)), ('gx', 'gy'), 0, 0,...  31.4 us
    pallas_call x6, Pallas kernels, call(): pl.pallas_call(kernel, out_shape=out_shape, in_specs=[spec(s) for s in in...  19.2 us
    ppermute x1, starting transfers between devices, per_device(): ylo = lax.ppermute(yhi_send, 'gy', up_y)  4.79 us
    ppermute x1, waiting for transfers between devices, per_device(): xhi = lax.ppermute(xlo_send, 'gx', down_x)  3.16 us
    ppermute x1, starting transfers between devices, per_device(): xlo = lax.ppermute(xhi_send, 'gx', up_x)  2.51 us
    ppermute x1, starting transfers between devices, per_device(): yhi = lax.ppermute(ylo_send, 'gy', down_y)  1.92 us
  transfers between devices with their start and end apart: 4, of which 2 were waited for; matrix products, arithmetic and copies ran while one was open for 0% of the time, Pallas kernels for 7%

profile of v3, /device:TPU:1, one launch (start us, length us, event | category | flops | bytes accessed | tf_op | source)
XLA Modules:
  0.0 66.5 jit_solution(14897530009397519172)
XLA Ops:
  0.6 0.0 copy-start.3
  0.6 0.0 copy-start.2
  0.7 0.0 copy-start
  0.7 0.0 copy-start.1
  0.7 0.1 pad_add_fusion.ids
  0.8 2.6 %shard_map.104 = (f32[2880,128]{1,0:T(8,128)S(1)}, f32[2880,128]{1,0:T(8,128)S(1)}, f32[144,128]{1,0:T(8,128)S(1)}, f32[144,128]{1,0:T(8,128)S(1)}) custom-call(s32[2]{0:T(128)S(1)} %pad_add_fusion.ids, s32[3,512]{1,0:T(4,128)} %bitcast.16, f32[3,512]{1,0:T(4,128)} %forces.1, f32[1536,128]{1,0:T(8,128)} %bitcast.13, s32[1536,128]{1,0:T(8,128)} %bitcast.14), custom_call_target="tpu_custom_call" | custom-call | flops 400000 | bytes 2400000 | tf_op jit(solution)/shard_map/pallas_call | solution.py:45
  3.3 4.8 %collective-permute-start = (f32[144,128]{1,0:T(8,128)S(1)}, f32[144,128]{1,0:T(8,128)S(1)}, u32[]{:S(2)}, u32[]{:S(2)}) collective-permute-start(f32[144,128]{1,0:T(8,128)S(1)} %get-tuple-element.16), channel_id=1, source_target_pairs={{0,1},{1,2},{2,3},{3,4},{4,5},{5,6},{6,7},{8,9},{9,10},{10,11},{11... | collective-permute-start | bytes 221192 | tf_op jit(solution)/shard_map/ppermute | solution.py:599
  8.1 1.9 %collective-permute-start.1 = (f32[144,128]{1,0:T(8,128)S(1)}, f32[144,128]{1,0:T(8,128)S(1)}, u32[]{:S(2)}, u32[]{:S(2)}) collective-permute-start(f32[144,128]{1,0:T(8,128)S(1)} %get-tuple-element.17), channel_id=1, source_target_pairs={{1,0},{2,1},{3,2},{4,3},{5,4},{6,5},{7,6},{9,8},{10,9},{11,10},{12... | collective-permute-start | bytes 221192 | tf_op jit(solution)/shard_map/ppermute | solution.py:600
  10.7 0.0 copy-done.3
  10.7 0.0 copy-done.2
  10.7 0.0 copy-done
  10.7 0.0 copy-done.1
  10.7 2.4 %shard_map.105.coarse = f32[6,16,128]{2,1,0:T(8,128)S(1)} custom-call(s32[2]{0:T(128)S(1)} %pad_add_fusion.ids, f32[3,64]{1,0:T(4,128)S(1)} %copy-done.1, f32[3,128,128]{2,1,0:T(8,128)S(1)} %copy-done, f32[3,128]{1,0:T(4,128)S(1)} %copy-done.2, f32[1,128]{1,0:T(1,128)S(1)} %bitcast.12, f32[1]{0:T(128)S(6)} %copy.15.bout), custom_call_target="tpu_custom_call" | custom-call | flops 1500000000 | bytes 300000 | tf_op jit(solution)/shard_map/pallas_call | solution.py:45
  13.1 0.0 collective-permute-done.ylo
  13.1 0.7 %collective-permute-done.1.yhi = f32[144,128]{1,0:T(8,128)S(1)} collective-permute-done((f32[144,128]{1,0:T(8,128)S(1)}, f32[144,128]{1,0:T(8,128)S(1)}, u32[]{:S(2)}, u32[]{:S(2)}) %collective-permute-start.1) | collective-permute-done | bytes 73760 | tf_op jit(solution)/shard_map/ppermute | solution.py:600
  13.8 0.1 shard_map.106
  13.9 2.5 %collective-permute-start.2 = (f32[360,128]{1,0:T(8,128)S(1)}, f32[360,128]{1,0:T(8,128)S(1)}, u32[]{:S(2)}, u32[]{:S(2)}) collective-permute-start(f32[360,128]{1,0:T(8,128)S(1)} %get-tuple-element.18), channel_id=1, source_target_pairs={{0,8},{8,16},{16,24},{24,32},{32,40},{40,48},{48,56},{56,64},{64,7... | collective-permute-start | bytes 552968 | tf_op jit(solution)/shard_map/ppermute | solution.py:613
  16.4 1.3 %collective-permute-start.3 = (f32[360,128]{1,0:T(8,128)S(1)}, f32[360,128]{1,0:T(8,128)S(1)}, u32[]{:S(2)}, u32[]{:S(2)}) collective-permute-start(f32[360,128]{1,0:T(8,128)S(1)} %get-tuple-element.19), channel_id=1, source_target_pairs={{8,0},{16,8},{24,16},{32,24},{40,32},{48,40},{56,48},{64,56},{72,6... | collective-permute-start | bytes 552968 | tf_op jit(solution)/shard_map/ppermute | solution.py:614
  17.7 2.0 %shard_map.107 = (f32[960,128]{1,0:T(8,128)S(1)}, f32[960,128]{1,0:T(8,128)S(1)}, f32[512,128]{1,0:T(8,128)}) custom-call(s32[2]{0:T(128)S(1)} %pad_add_fusion.ids, f32[6,16,128]{2,1,0:T(8,128)S(1)} %shard_map.105.coarse), custom_call_target="tpu_custom_call" | custom-call | flops 8000000 | bytes 1300000 | tf_op jit(solution)/shard_map/pallas_call | solution.py:45
  19.7 0.0 collective-permute-done.2.xlo
  19.7 3.2 %collective-permute-done.3.xhi = f32[360,128]{1,0:T(8,128)S(1)} collective-permute-done((f32[360,128]{1,0:T(8,128)S(1)}, f32[360,128]{1,0:T(8,128)S(1)}, u32[]{:S(2)}, u32[]{:S(2)}) %collective-permute-start.3) | collective-permute-done | bytes 184352 | tf_op jit(solution)/shard_map/ppermute | solution.py:614
  22.9 11.1 %shard_map.108 = (f32[2880,128]{1,0:T(8,128)S(1)}, f32[2880,128]{1,0:T(8,128)S(1)}, f32[2880,128]{1,0:T(8,128)S(1)}, f32[2880,128]{1,0:T(8,128)S(1)}, f32[1,128]{1,0:T(1,128)S(1)}) custom-call(f32[2880,128]{1,0:T(8,128)S(1)} %get-tuple-element.14.load.load_in, ...), custom_call_target="tpu_custom_call", output_to_operand_aliasing={{0}: (0, {}), {1}: (1, {})} | custom-call | tf_op jit(solution)/shard_map/pallas_call | solution.py:45
  34.0 0.1 broadcast_in_dim.2
  34.1 31.4 %all_to_all.8 = f32[256,1,128]{2,1,0:T(1,128)S(1)} all-to-all(f32[256,1,128]{2,1,0:T(1,128)S(1)} %broadcast_in_dim.2), channel_id=1, replica_groups=mesh['gx'=32,'gy'=8] {'gx','gy'}, dimensions={0} | all-to-all | bytes 262144 | tf_op jit(solution)/shard_map/all_to_all | solution.py:630
  65.5 1.1 %shard_map.109 = f32[1536,128]{1,0:T(8,128)} custom-call(f32[256,128]{1,0:T(8,128)S(1)} %bitcast.10, f32[2880,128]{1,0:T(8,128)S(1)} %get-tuple-element.23.z, f32[2880,128]{1,0:T(8,128)S(1)} %get-tuple-element.24.y), custom_call_target="tpu_custom_call" | custom-call | tf_op jit(solution)/shard_map/pallas_call | solution.py:45
Async XLA Ops:
  0.6 10.1 %copy-start.3 = (f32[128]{0:T(128)S(1)}, f32[128]{0:T(128)}, u32[]{:S(2)}) copy-start(f32[128]{0:T(128)} %param.16) | copy-start | bytes 1540
  0.6 10.1 %copy-start.2 = (f32[3,128]{1,0:T(4,128)S(1)}, f32[3,128]{1,0:T(4,128)}, u32[]{:S(2)}) copy-start(f32[3,128]{1,0:T(4,128)} %biases.1) | copy-start | bytes 4612
  0.7 10.1 %copy-start = (f32[3,128,128]{2,1,0:T(8,128)S(1)}, f32[3,128,128]{2,1,0:T(8,128)}, u32[]{:S(2)}) copy-start(f32[3,128,128]{2,1,0:T(8,128)} %weights.1) | copy-start | bytes 589828
  0.7 10.1 %copy-start.1 = (f32[3,64]{1,0:T(4,128)S(1)}, f32[3,64]{1,0:T(4,128)}, u32[]{:S(2)}) copy-start(f32[3,64]{1,0:T(4,128)} %freq.1) | copy-start | bytes 2308
  3.3 9.8 %collective-permute-start = (f32[144,128]{1,0:T(8,128)S(1)}, f32[144,128]{1,0:T(8,128)S(1)}, u32[]{:S(2)}, u32[]{:S(2)}) collective-permute-start(f32[144,128]{1,0:T(8,128)S(1)} %get-tuple-element.16), channel_id=1, source_target_pairs={{0,1},{1,2},{2,3},{3,4},{4,5},{5,6},{6,7},{8,9},{9,10},{10,11},{11... | collective-permute-start | bytes 221192 | tf_op jit(solution)/shard_map/ppermute | solution.py:599
  8.1 5.7 %collective-permute-start.1 = (f32[144,128]{1,0:T(8,128)S(1)}, f32[144,128]{1,0:T(8,128)S(1)}, u32[]{:S(2)}, u32[]{:S(2)}) collective-permute-start(f32[144,128]{1,0:T(8,128)S(1)} %get-tuple-element.17), channel_id=1, source_target_pairs={{1,0},{2,1},{3,2},{4,3},{5,4},{6,5},{7,6},{9,8},{10,9},{11,10},{12... | collective-permute-start | bytes 221192 | tf_op jit(solution)/shard_map/ppermute | solution.py:600
  13.9 5.8 %collective-permute-start.2 = (f32[360,128]{1,0:T(8,128)S(1)}, f32[360,128]{1,0:T(8,128)S(1)}, u32[]{:S(2)}, u32[]{:S(2)}) collective-permute-start(f32[360,128]{1,0:T(8,128)S(1)} %get-tuple-element.18), channel_id=1, source_target_pairs={{0,8},{8,16},{16,24},{24,32},{32,40},{40,48},{48,56},{56,64},{64,7... | collective-permute-start | bytes 552968 | tf_op jit(solution)/shard_map/ppermute | solution.py:613
  16.4 6.5 %collective-permute-start.3 = (f32[360,128]{1,0:T(8,128)S(1)}, f32[360,128]{1,0:T(8,128)S(1)}, u32[]{:S(2)}, u32[]{:S(2)}) collective-permute-start(f32[360,128]{1,0:T(8,128)S(1)} %get-tuple-element.19), channel_id=1, source_target_pairs={{8,0},{16,8},{24,16},{32,24},{40,32},{48,40},{56,48},{64,56},{72,6... | collective-permute-start | bytes 552968 | tf_op jit(solution)/shard_map/ppermute | solution.py:614

commit v4 on v3

--- a/solution.py
+++ b/solution.py
@@ -421,118 +421,159 @@
     lax.fori_loop(0, BLOCKS, block, 0)
 
 
-def main_kernel(
-    load_in, free_in, ylo, yhi, xlo, xhi, young, inverse,
-    load, free, field, scaled, dots_out,
-    zsum, zdiff, above, minus, plus,
-):
-    del load_in, free_in
-    zero = jnp.zeros((8, NZ), f32)
-    lane = lax.broadcasted_iota(jnp.int32, (8, NZ), 1)
-    not_last, not_first = lane < NZ - 1, lane > 0
-
-    for c in range(3):
-        for k in range(2):
-            for strip, row in ((ylo, 2 + k), (yhi, 36 + k)):
-                load[pl.ds(c * SIZE + CF * EY + row, NX, stride=EY), :] = strip[
-                    pl.ds((c * 2 + k) * NX, NX), :
-                ]
-            for plane, x in ((xlo, 2 + k), (xhi, 20 + k)):
-                load[pl.ds(c * SIZE + x * EY, EY), :] = plane[pl.ds((c * 2 + k) * EY, EY), :]
-        for strip, row in ((ylo, 3), (yhi, 36)):
-            free[pl.ds(c * SIZE + CF * EY + row, NX, stride=EY), :] = strip[pl.ds((6 + c) * NX, NX), :]
-        for plane, x in ((xlo, 3), (xhi, 20)):
-            free[pl.ds(c * SIZE + x * EY, EY), :] = plane[pl.ds((6 + c) * EY, EY), :]
-    for ref in (zsum, zdiff):
-        ref[pl.ds(3 * SIZE, 8), :] = zero
-
-    def z_stage(at, v):
-        n = jnp.where(not_last, pltpu.roll(v, NZ - 1, 1), 0.0)
-        zsum[at, :] = v + n
-        zdiff[at, :] = n - v
-
-    def prepare(x, carry):
+class Stages:
+    def __init__(self, load, free, inverse, field, scaled, minus, plus):
+        self.load, self.free, self.inverse = load, free, inverse
+        self.field, self.scaled, self.minus, self.plus = field, scaled, minus, plus
+        lane = lax.broadcasted_iota(jnp.int32, (8, NZ), 1)
+        row = lax.broadcasted_iota(jnp.int32, (8, NZ), 0)
+        self.not_last, self.not_first = lane < NZ - 1, lane > 0
+        self.first_rows = jnp.where(row >= CF, 1.0, 0.0)
+        self.last_rows = jnp.where(row < CF, 1.0, 0.0)
+
+    def z_stage(self, out, at, v):
+        n = jnp.where(self.not_last, pltpu.roll(v, NZ - 1, 1), 0.0)
+        out[0][at, :] = v + n
+        out[1][at, :] = n - v
+
+    def prepare(self, out, x):
         for j in range(BLOCKS):
             base = pl.multiple_of(x * EY, 8) + 8 * j
-            inv = inverse[pl.ds(base, 8), :]
+            inv = self.inverse[pl.ds(base, 8), :]
             for c in range(3):
                 at = pl.ds(base + c * SIZE, 8)
-                v = load[at, :] * inv
-                field[at, :] = v
-                z_stage(at, v)
-        return carry
-
-    lax.fori_loop(2, 22, prepare, 0, unroll=2)
-
-    for c in range(3):
-        for ref in (zsum, zdiff):
-            ref[pl.ds(c * SIZE + 22 * EY, 8), :] = zero
-
-    def clear_above(i, carry):
-        above[pl.ds(pl.multiple_of(i * TALL, 8), 8), :] = zero
-        return carry
-
-    lax.fori_loop(0, 6 * EX, clear_above, 0, unroll=8)
-
-    operator_pass(zsum, zdiff, young, above, minus, plus, 2, 21, 3)
-
-    row = lax.broadcasted_iota(jnp.int32, (8, NZ), 0)
-    first_rows = jnp.where(row >= CF, 1.0, 0.0)
-    last_rows = jnp.where(row < CF, 1.0, 0.0)
-
-    def gather(totals, j, terms):
+                v = self.load[at, :] * inv
+                self.field[at, :] = v
+                self.z_stage(out, at, v)
+
+    def gather(self, totals, j, terms):
         for k, t in enumerate(terms):
             if j == 0:
-                t = t * first_rows
+                t = t * self.first_rows
             if j == BLOCKS - 1:
-                t = t * last_rows
+                t = t * self.last_rows
             totals[k] = t if totals[k] is None else totals[k] + t
 
-    def force(at):
-        return minus[at, :] + jnp.where(not_first, pltpu.roll(plus[at, :], 1, 1), 0.0)
-
-    def finish_one(x, dots):
+    def force(self, at):
+        return self.minus[at, :] + jnp.where(self.not_first, pltpu.roll(self.plus[at, :], 1, 1), 0.0)
+
+    def finish_one(self, out, x, dots):
         totals = [None] * 3
         for j in range(BLOCKS):
             base = pl.multiple_of(x * EY, 8) + 8 * j
-            inv = inverse[pl.ds(base, 8), :]
+            inv = self.inverse[pl.ds(base, 8), :]
             sums = None
             for c in range(3):
                 at = pl.ds(base + c * SIZE, 8)
-                w = free[at, :] * force(at)
+                w = self.free[at, :] * self.force(at)
                 y = w * inv
-                z = field[at, :]
+                z = self.field[at, :]
                 zt = z - y
-                scaled[at, :] = y
-                z_stage(at, zt)
+                self.scaled[at, :] = y
+                self.z_stage(out, at, zt)
                 if dots is not None:
-                    rt = load[at, :] - w
+                    rt = self.load[at, :] - w
                     terms = (z * w, z * rt, zt * rt)
                     sums = terms if sums is None else [p + q for p, q in zip(sums, terms)]
             if dots is not None:
-                gather(totals, j, sums)
+                self.gather(totals, j, sums)
         return dots if dots is None else [p + q for p, q in zip(dots, totals)]
 
-    finish_one(CF - 1, None)
-    finish_one(CF + NX, None)
-    dots = lax.fori_loop(CF, CF + NX, finish_one, [zero] * 3, unroll=2)
-
-    operator_pass(zsum, zdiff, young, above, minus, plus, 3, 20, 4)
-
-    def finish_two(x, dots):
-        totals = [None] * 1
+    def finish_two(self, x, dots):
+        totals = [None]
         for j in range(BLOCKS):
             base = pl.multiple_of(x * EY, 8) + 8 * j
             sums = None
             for c in range(3):
                 at = pl.ds(base + c * SIZE, 8)
-                q = free[at, :] * force(at)
-                terms = ((field[at, :] - scaled[at, :]) * q,)
-                sums = terms if sums is None else [a + b for a, b in zip(sums, terms)]
-            gather(totals, j, sums)
+                q = self.free[at, :] * self.force(at)
+                terms = ((self.field[at, :] - self.scaled[at, :]) * q,)
+                sums = terms if sums is None else [p + r for p, r in zip(sums, terms)]
+            self.gather(totals, j, sums)
         return [p + q for p, q in zip(dots, totals)]
 
-    dots = dots + lax.fori_loop(CF, CF + NX, finish_two, [zero], unroll=2)
+
+def clear_edges(above):
+    zero = jnp.zeros((8, NZ), f32)
+
+    def body(i, carry):
+        above[pl.ds(pl.multiple_of(i * TALL, 8), 8), :] = zero
+        return carry
+
+    lax.fori_loop(0, 6 * EX, body, 0, unroll=8)
+
+
+def clear_row_past(refs, x):
+    for ref in refs:
+        for c in range(3):
+            ref[pl.ds(c * SIZE + x * EY, 8), :] = jnp.zeros((8, NZ), f32)
+
+
+LAST = CF + NX - 1
+
+
+def inner_kernel(
+    load_in, free_in, ylo, yhi, young, inverse,
+    load, free, field, scaled, zsum, zdiff, zsum2, zdiff2, dots_out,
+    above, minus, plus,
+):
+    del load_in, free_in
+    for c in range(3):
+        base = c * SIZE + CF * EY
+        for k in range(2):
+            for strip, row in ((ylo, 2 + k), (yhi, 36 + k)):
+                load[pl.ds(base + row, NX, stride=EY), :] = strip[pl.ds((c * 2 + k) * NX, NX), :]
+        for strip, row in ((ylo, 3), (yhi, 36)):
+            free[pl.ds(base + row, NX, stride=EY), :] = strip[pl.ds((6 + c) * NX, NX), :]
+    stages = Stages(load, free, inverse, field, scaled, minus, plus)
+    first, second = (zsum, zdiff), (zsum2, zdiff2)
+
+    def prepare(x, carry):
+        stages.prepare(first, x)
+        return carry
+
+    lax.fori_loop(CF, LAST + 1, prepare, 0, unroll=2)
+    clear_row_past(first, LAST + 1)
+    clear_edges(above)
+    operator_pass(zsum, zdiff, young, above, minus, plus, CF, LAST, 7)
+    dots = lax.fori_loop(
+        CF + 1, LAST, lambda x, d: stages.finish_one(second, x, d), [jnp.zeros((8, NZ), f32)] * 3, unroll=2
+    )
+    for k, d in enumerate(dots):
+        dots_out[k] = d
+
+
+def outer_kernel(
+    load_in, free_in, field_in, scaled_in, zsum_in, zdiff_in, zsum2_in, zdiff2_in,
+    xlo, xhi, young, inverse, dots_in,
+    load, free, field, scaled, zsum, zdiff, zsum2, zdiff2, dots_out,
+    above, minus, plus,
+):
+    del load_in, free_in, field_in, scaled_in, zsum_in, zdiff_in, zsum2_in, zdiff2_in
+    for c in range(3):
+        for k in range(2):
+            for plane, x in ((xlo, 2 + k), (xhi, LAST + 1 + k)):
+                load[pl.ds(c * SIZE + x * EY, EY), :] = plane[pl.ds((c * 2 + k) * EY, EY), :]
+        for plane, x in ((xlo, 3), (xhi, LAST + 1)):
+            free[pl.ds(c * SIZE + x * EY, EY), :] = plane[pl.ds((6 + c) * EY, EY), :]
+    stages = Stages(load, free, inverse, field, scaled, minus, plus)
+    first, second = (zsum, zdiff), (zsum2, zdiff2)
+    for start in (2, LAST + 1):
+        stages.prepare(first, start)
+        stages.prepare(first, start + 1)
+    clear_row_past(first, LAST + 3)
+    clear_row_past(second, LAST + 2)
+    clear_edges(above)
+    operator_pass(zsum, zdiff, young, above, minus, plus, 2, CF + 1, 2)
+    operator_pass(zsum, zdiff, young, above, minus, plus, LAST - 1, LAST + 2, 2)
+    stages.finish_one(second, CF - 1, None)
+    stages.finish_one(second, LAST + 1, None)
+    dots = [dots_in[k] for k in range(3)]
+    for x in (CF, LAST):
+        dots = stages.finish_one(second, x, dots)
+
+    operator_pass(zsum2, zdiff2, young, above, minus, plus, CF - 1, LAST + 1, 8)
+    dots = dots + lax.fori_loop(CF, LAST + 1, stages.finish_two, [jnp.zeros((8, NZ), f32)], unroll=2)
     one = lax.broadcasted_iota(jnp.int32, (1, NZ), 1)
     line = jnp.zeros((1, NZ), f32)
     for k, d in enumerate(dots):
@@ -619,14 +660,19 @@
         out_spaces=(VMEM, VMEM, pltpu.HBM),
         cost=pl.CostEstimate(flops=8000000, transcendentals=0, bytes_accessed=1300000),
     )
-    tail = VMEM((3 * SIZE + 8, NZ), f32)
-    work = VMEM((3 * SIZE, NZ), f32)
-    _, _, z, y, dots = call(
-        main_kernel, (ext, ext, ext, ext, shape(1, NZ)),
-        [VMEM] * 8, (load, free, ylo, yhi, xlo, xhi, young, inverse),
-        scratch=[tail, tail, VMEM((6 * EX * TALL, NZ), f32), work, work],
-        aliases={0: 0, 1: 1}, limit=20,
-    )
+    work = [VMEM((6 * EX * TALL, NZ), f32), VMEM((3 * SIZE, NZ), f32), VMEM((3 * SIZE, NZ), f32)]
+    *state, dots = call(
+        inner_kernel, (ext,) * 8 + (shape(3, 8, NZ),),
+        [VMEM] * 6, (load, free, ylo, yhi, young, inverse),
+        scratch=work, aliases={0: 0, 1: 1},
+        cost=pl.CostEstimate(flops=60000000, transcendentals=0, bytes_accessed=9000000),
+    )
+    *state, dots = call(
+        outer_kernel, (ext,) * 8 + (shape(1, NZ),),
+        [VMEM] * 13, (*state, xlo, xhi, young, inverse, dots),
+        scratch=work, aliases={i: i for i in range(8)},
+    )
+    z, y = state[2], state[3]
     parts = lax.all_to_all(
         jnp.broadcast_to(dots, (nx * ny, NZ)), ("gx", "gy"), 0, 0, tiled=True
     )

time: 67.1 us -> 61.4 us (0.915)
  waiting for transfers between devices: 3.85 us -> 0.01 us
  blocking collectives: 31.4 us -> 29.3 us
  starting transfers between devices: 10.5 us -> 11.4 us
    ppermute x1, waiting for transfers between devices: 3.16 us -> 0.01 us  [per_device(): xhi = lax.ppermute(xlo_send, 'gx', down_x)]
    all_to_all x1, blocking collectives: 31.4 us -> 29.3 us  [per_device(): lax.all_to_all(jnp.broadcast_to(dots, (nx * ny, NZ)), ('gx', 'gy'), 0, 0,...]
    ppermute x1, starting transfers between devices: 1.92 us -> 2.64 us  [per_device(): yhi = lax.ppermute(ylo_send, 'gy', down_y)]
    ppermute x1, waiting for transfers between devices: 0.68 us -> 0.01 us  [per_device(): yhi = lax.ppermute(ylo_send, 'gy', down_y)]
    pallas_call x6 -> x7, Pallas kernels: 19.2 us -> 18.6 us  [call(): pl.pallas_call(kernel, out_shape=out_shape, in_specs=[spec(s) for s in in...]
  transfers between devices with their start and end apart: 4 -> 4, of which waited for: 2 -> 0; matrix products, arithmetic and copies ran while one was open for 0% -> 0% of each run, Pallas kernels for 7% -> 16%
where the time goes in v4:
time: 61.4 us; the launch traced here: 61 us
  blocking collectives  29.3 us (48%)
  Pallas kernels  18.6 us (30%)
  starting transfers between devices  11.4 us (19%)
  between operations  1.46 us (2%)
    all_to_all x1, blocking collectives, per_device(): lax.all_to_all(jnp.broadcast_to(dots, (nx * ny, NZ)), ('gx', 'gy'), 0, 0,...  29.3 us
    pallas_call x7, Pallas kernels, call(): pl.pallas_call(kernel, out_shape=out_shape, in_specs=[spec(s) for s in in...  18.6 us
    ppermute x1, starting transfers between devices, per_device(): ylo = lax.ppermute(yhi_send, 'gy', up_y)  4.38 us
    ppermute x1, starting transfers between devices, per_device(): xlo = lax.ppermute(xhi_send, 'gx', up_x)  3.08 us
    ppermute x1, starting transfers between devices, per_device(): yhi = lax.ppermute(ylo_send, 'gy', down_y)  2.64 us
    ppermute x1, starting transfers between devices, per_device(): xhi = lax.ppermute(xlo_send, 'gx', down_x)  1.29 us
  transfers between devices with their start and end apart: 4, of which 0 were waited for; matrix products, arithmetic and copies ran while one was open for 0% of the time, Pallas kernels for 16%

profile of v4, /device:TPU:1, one launch (start us, length us, event | category | flops | bytes accessed | tf_op | source)
XLA Modules:
  0.0 61.0 jit_solution(18295650100963141178)
XLA Ops:
  0.6 0.0 copy-start.3
  0.6 0.0 copy-start.2
  0.7 0.0 copy-start
  0.7 0.0 copy-start.1
  0.7 0.1 pad_add_fusion.ids
  0.8 2.6 %shard_map.104 = (f32[2880,128]{1,0:T(8,128)S(1)}, f32[2880,128]{1,0:T(8,128)S(1)}, f32[144,128]{1,0:T(8,128)S(1)}, f32[144,128]{1,0:T(8,128)S(1)}) custom-call(s32[2]{0:T(128)S(1)} %pad_add_fusion.ids, s32[3,512]{1,0:T(4,128)} %bitcast.16, f32[3,512]{1,0:T(4,128)} %forces.1, f32[1536,128]{1,0:T(8,128)} %bitcast.13, s32[1536,128]{1,0:T(8,128)} %bitcast.14), custom_call_target="tpu_custom_call" | custom-call | flops 400000 | bytes 2400000 | tf_op jit(solution)/shard_map/pallas_call | solution.py:45
  3.3 4.4 %collective-permute-start = (f32[144,128]{1,0:T(8,128)S(1)}, f32[144,128]{1,0:T(8,128)S(1)}, u32[]{:S(2)}, u32[]{:S(2)}) collective-permute-start(f32[144,128]{1,0:T(8,128)S(1)} %get-tuple-element.25), channel_id=1, source_target_pairs={{0,1},{1,2},{2,3},{3,4},{4,5},{5,6},{6,7},{8,9},{9,10},{10,11},{11... | collective-permute-start | bytes 221192 | tf_op jit(solution)/shard_map/ppermute | solution.py:640
  7.7 2.6 %collective-permute-start.1 = (f32[144,128]{1,0:T(8,128)S(1)}, f32[144,128]{1,0:T(8,128)S(1)}, u32[]{:S(2)}, u32[]{:S(2)}) collective-permute-start(f32[144,128]{1,0:T(8,128)S(1)} %get-tuple-element.26), channel_id=1, source_target_pairs={{1,0},{2,1},{3,2},{4,3},{5,4},{6,5},{7,6},{9,8},{10,9},{11,10},{12... | collective-permute-start | bytes 221192 | tf_op jit(solution)/shard_map/ppermute | solution.py:641
  11.0 0.0 copy-done.3
  11.0 0.0 copy-done.2
  11.0 0.0 copy-done
  11.0 0.0 copy-done.1
  11.1 2.4 %shard_map.105.coarse = f32[6,16,128]{2,1,0:T(8,128)S(1)} custom-call(s32[2]{0:T(128)S(1)} %pad_add_fusion.ids, f32[3,64]{1,0:T(4,128)S(1)} %copy-done.1, f32[3,128,128]{2,1,0:T(8,128)S(1)} %copy-done, f32[3,128]{1,0:T(4,128)S(1)} %copy-done.2, f32[1,128]{1,0:T(1,128)S(1)} %bitcast.12, f32[1]{0:T(128)S(6)} %copy.31.bout), custom_call_target="tpu_custom_call" | custom-call | flops 1500000000 | bytes 300000 | tf_op jit(solution)/shard_map/pallas_call | solution.py:45
  13.4 0.0 collective-permute-done.ylo
  13.4 0.0 collective-permute-done.1.yhi
  13.4 0.1 shard_map.108
  13.5 3.1 %collective-permute-start.2 = (f32[360,128]{1,0:T(8,128)S(1)}, f32[360,128]{1,0:T(8,128)S(1)}, u32[]{:S(2)}, u32[]{:S(2)}) collective-permute-start(f32[360,128]{1,0:T(8,128)S(1)} %get-tuple-element.37), channel_id=1, source_target_pairs={{0,8},{8,16},{16,24},{24,32},{32,40},{40,48},{48,56},{56,64},{64,7... | collective-permute-start | bytes 552968 | tf_op jit(solution)/shard_map/ppermute | solution.py:654
  16.6 1.3 %collective-permute-start.3 = (f32[360,128]{1,0:T(8,128)S(1)}, f32[360,128]{1,0:T(8,128)S(1)}, u32[]{:S(2)}, u32[]{:S(2)}) collective-permute-start(f32[360,128]{1,0:T(8,128)S(1)} %get-tuple-element.38), channel_id=1, source_target_pairs={{8,0},{16,8},{24,16},{32,24},{40,32},{48,40},{56,48},{64,56},{72,6... | collective-permute-start | bytes 552968 | tf_op jit(solution)/shard_map/ppermute | solution.py:655
  17.9 2.0 %shard_map.106 = (f32[960,128]{1,0:T(8,128)S(1)}, f32[960,128]{1,0:T(8,128)S(1)}, f32[512,128]{1,0:T(8,128)}) custom-call(s32[2]{0:T(128)S(1)} %pad_add_fusion.ids, f32[6,16,128]{2,1,0:T(8,128)S(1)} %shard_map.105.coarse), custom_call_target="tpu_custom_call" | custom-call | flops 8000000 | bytes 1300000 | tf_op jit(solution)/shard_map/pallas_call | solution.py:45
  19.9 5.1 %shard_map.107 = (f32[2880,128]{1,0:T(8,128)S(1)}, f32[2880,128]{1,0:T(8,128)S(1)}, f32[2880,128]{1,0:T(8,128)S(1)}, f32[2880,128]{1,0:T(8,128)S(1)}, f32[2880,1...) custom-call(f32[2880,128]{1,0:T(8,128)S(1)} %get-tuple-element.23.lo, ...), custom_call_target="tpu_custom_call", output_to_operand_aliasing={{0}: (0, {}), {1}: (1, {})} | custom-call | flops 60000000 | bytes 9000000 | tf_op jit(solution)/shard_map/pallas_call | solution.py:45
  25.0 0.0 collective-permute-done.2.xlo
  25.0 0.0 collective-permute-done.3.xhi
  25.0 5.4 %shard_map.109 = (f32[2880,128]{1,0:T(8,128)S(1)}, f32[2880,128]{1,0:T(8,128)S(1)}, f32[2880,128]{1,0:T(8,128)S(1)}, f32[2880,128]{1,0:T(8,128)S(1)}, f32[2880,1...) custom-call(f32[2880,128]{1,0:T(8,128)S(1)} %get-tuple-element.29.lo, ...), custom_call_target="tpu_custom_call", output_to_operand_aliasing={{0}: (0, {}), {1}: (1, {}), {2}: (2, {}), {3}: (3, {}), {4}... | custom-call | tf_op jit(solution)/shard_map/pallas_call | solution.py:45
  30.5 0.1 broadcast_in_dim.2
  30.5 29.3 %all_to_all.8 = f32[256,1,128]{2,1,0:T(1,128)S(1)} all-to-all(f32[256,1,128]{2,1,0:T(1,128)S(1)} %broadcast_in_dim.2), channel_id=1, replica_groups=mesh['gx'=32,'gy'=8] {'gx','gy'}, dimensions={0} | all-to-all | bytes 262144 | tf_op jit(solution)/shard_map/all_to_all | solution.py:676
  59.9 1.1 %shard_map.110 = f32[1536,128]{1,0:T(8,128)} custom-call(f32[256,128]{1,0:T(8,128)S(1)} %bitcast.10, f32[2880,128]{1,0:T(8,128)S(1)} %get-tuple-element.41.z, f32[2880,128]{1,0:T(8,128)S(1)} %get-tuple-element.42.y), custom_call_target="tpu_custom_call" | custom-call | tf_op jit(solution)/shard_map/pallas_call | solution.py:45
Async XLA Ops:
  0.6 10.4 %copy-start.3 = (f32[128]{0:T(128)S(1)}, f32[128]{0:T(128)}, u32[]{:S(2)}) copy-start(f32[128]{0:T(128)} %param.16) | copy-start | bytes 1540
  0.6 10.4 %copy-start.2 = (f32[3,128]{1,0:T(4,128)S(1)}, f32[3,128]{1,0:T(4,128)}, u32[]{:S(2)}) copy-start(f32[3,128]{1,0:T(4,128)} %biases.1) | copy-start | bytes 4612
  0.7 10.4 %copy-start = (f32[3,128,128]{2,1,0:T(8,128)S(1)}, f32[3,128,128]{2,1,0:T(8,128)}, u32[]{:S(2)}) copy-start(f32[3,128,128]{2,1,0:T(8,128)} %weights.1) | copy-start | bytes 589828
  0.7 10.4 %copy-start.1 = (f32[3,64]{1,0:T(4,128)S(1)}, f32[3,64]{1,0:T(4,128)}, u32[]{:S(2)}) copy-start(f32[3,64]{1,0:T(4,128)} %freq.1) | copy-start | bytes 2308
  3.3 10.1 %collective-permute-start = (f32[144,128]{1,0:T(8,128)S(1)}, f32[144,128]{1,0:T(8,128)S(1)}, u32[]{:S(2)}, u32[]{:S(2)}) collective-permute-start(f32[144,128]{1,0:T(8,128)S(1)} %get-tuple-element.25), channel_id=1, source_target_pairs={{0,1},{1,2},{2,3},{3,4},{4,5},{5,6},{6,7},{8,9},{9,10},{10,11},{11... | collective-permute-start | bytes 221192 | tf_op jit(solution)/shard_map/ppermute | solution.py:640
  7.7 5.7 %collective-permute-start.1 = (f32[144,128]{1,0:T(8,128)S(1)}, f32[144,128]{1,0:T(8,128)S(1)}, u32[]{:S(2)}, u32[]{:S(2)}) collective-permute-start(f32[144,128]{1,0:T(8,128)S(1)} %get-tuple-element.26), channel_id=1, source_target_pairs={{1,0},{2,1},{3,2},{4,3},{5,4},{6,5},{7,6},{9,8},{10,9},{11,10},{12... | collective-permute-start | bytes 221192 | tf_op jit(solution)/shard_map/ppermute | solution.py:641
  13.5 11.5 %collective-permute-start.2 = (f32[360,128]{1,0:T(8,128)S(1)}, f32[360,128]{1,0:T(8,128)S(1)}, u32[]{:S(2)}, u32[]{:S(2)}) collective-permute-start(f32[360,128]{1,0:T(8,128)S(1)} %get-tuple-element.37), channel_id=1, source_target_pairs={{0,8},{8,16},{16,24},{24,32},{32,40},{40,48},{48,56},{56,64},{64,7... | collective-permute-start | bytes 552968 | tf_op jit(solution)/shard_map/ppermute | solution.py:654
  16.6 8.4 %collective-permute-start.3 = (f32[360,128]{1,0:T(8,128)S(1)}, f32[360,128]{1,0:T(8,128)S(1)}, u32[]{:S(2)}, u32[]{:S(2)}) collective-permute-start(f32[360,128]{1,0:T(8,128)S(1)} %get-tuple-element.38), channel_id=1, source_target_pairs={{8,0},{16,8},{24,16},{32,24},{40,32},{48,40},{56,48},{64,56},{72,6... | collective-permute-start | bytes 552968 | tf_op jit(solution)/shard_map/ppermute | solution.py:655

commit v5 on v4

--- a/solution.py
+++ b/solution.py
@@ -54,14 +54,18 @@
     )(*args)
 
 
+def place():
+    return lax.axis_index("gx"), lax.axis_index("gy")
+
+
 def shape(*dims):
     return jax.ShapeDtypeStruct(dims, f32)
 
 
 def pack_kernel(
-    ids, nodes, forces, body, fixed,
+    nodes, forces, body, fixed,
     load, free, lo_out, hi_out,
-    body_v, fixed_v, nodes_v, nodes_s, forces_s, sem,
+    body_v, fixed_v, nodes_v, nodes_s, forces_s, found, sem,
 ):
     part = NX * NY
     copies = [
@@ -88,6 +92,7 @@
 
     lax.fori_loop(CF, CF + NX, clear, 0, unroll=2)
 
+    ids = place()
     start_x = ids[0] * NX
     start_y = ids[1] * NY
     for copy in copies[:3]:
@@ -98,23 +103,30 @@
     index = lax.broadcasted_iota(jnp.int32, (1, LOADS), 1)
     todo = jnp.where(mine, index, LOADS)
     lane = lax.broadcasted_iota(jnp.int32, (1, NZ), 1)
-    first = jnp.min(todo)
+
+    def more(state):
+        return state[0] < LOADS
+
+    def collect(state):
+        p, count = state
+        found[count] = p
+        return jnp.min(jnp.where(todo > p, todo, LOADS)), count + 1
+
+    _, count = lax.while_loop(more, collect, (jnp.min(todo), 0))
     for copy in copies[3:]:
         copy.wait()
 
-    def more(p):
-        return p < LOADS
-
-    def add_one(p):
+    def add_one(i, carry):
+        p = found[i]
         x = nodes_s[0, p] - start_x
         y = nodes_s[1, p] - start_y
         hit = lane == nodes_s[2, p]
         for c in range(3):
             row = pl.ds((c * NX + x) * NY + y, 1)
             body_v[row, :] = body_v[row, :] + jnp.where(hit, forces_s[c, p], 0.0)
-        return jnp.min(jnp.where(todo > p, todo, LOADS))
-
-    lax.while_loop(more, add_one, first)
+        return carry
+
+    lax.fori_loop(0, count, add_one, 0)
 
     def mask(x, carry):
         for c in range(3):
@@ -183,7 +195,8 @@
 GROUP = 3
 
 
-def mlp_kernel(ids, freq, weights, biases, wout, bout, coarse, axy, bxy, w2):
+def mlp_kernel(freq, weights, biases, wout, bout, coarse, axy, bxy, w2):
+    ids = place()
     cx0 = ids[0] * CX - 1
     cy0 = ids[1] * CY - 1
     f = freq[...]
@@ -238,7 +251,7 @@
                 cell = (k * GY + j) * CZ
                 line = jnp.sum(jnp.where(pick, h[cell : cell + CZ, :], 0.0), axis=0, keepdims=True)
                 logits = jnp.where(row16 == (j + 15) % 16, line, logits)
-            coarse[GROUP * i + k] = 1.0 / (1.0 + jnp.exp(-(logits + bout[0])))
+            coarse[GROUP * i + k] = 1.0 / (1.0 + jnp.exp(-(logits + bout[...])))
         return carry
 
     lax.fori_loop(0, GX // GROUP, body, 0)
@@ -248,7 +261,8 @@
 SCALE = MU / 16.0
 
 
-def density_kernel(ids, coarse, young, inverse, density, density_v, sem):
+def density_kernel(coarse, young, inverse, density, density_v, sem):
+    ids = place()
     lane = lax.broadcasted_iota(jnp.int32, (16, NZ), 1)
     not_last, not_first = lane < NZ - 1, lane > 0
     row16 = lax.broadcasted_iota(jnp.int32, (16, NZ), 0)
@@ -532,12 +546,12 @@
         stages.prepare(first, x)
         return carry
 
-    lax.fori_loop(CF, LAST + 1, prepare, 0, unroll=2)
+    lax.fori_loop(CF, LAST + 1, prepare, 0, unroll=4)
     clear_row_past(first, LAST + 1)
     clear_edges(above)
     operator_pass(zsum, zdiff, young, above, minus, plus, CF, LAST, 7)
     dots = lax.fori_loop(
-        CF + 1, LAST, lambda x, d: stages.finish_one(second, x, d), [jnp.zeros((8, NZ), f32)] * 3, unroll=2
+        CF + 1, LAST, lambda x, d: stages.finish_one(second, x, d), [jnp.zeros((8, NZ), f32)] * 3, unroll=7
     )
     for k, d in enumerate(dots):
         dots_out[k] = d
@@ -573,7 +587,7 @@
         dots = stages.finish_one(second, x, dots)
 
     operator_pass(zsum2, zdiff2, young, above, minus, plus, CF - 1, LAST + 1, 8)
-    dots = dots + lax.fori_loop(CF, LAST + 1, stages.finish_two, [jnp.zeros((8, NZ), f32)], unroll=2)
+    dots = dots + lax.fori_loop(CF, LAST + 1, stages.finish_two, [jnp.zeros((8, NZ), f32)], unroll=4)
     one = lax.broadcasted_iota(jnp.int32, (1, NZ), 1)
     line = jnp.zeros((1, NZ), f32)
     for k, d in enumerate(dots):
@@ -617,8 +631,7 @@
     body_force, fixed_dofs, load_nodes, load_forces, frequencies,
     hidden_weights, hidden_biases, output_weights, output_bias,
 ):
-    bx, by = lax.axis_index("gx"), lax.axis_index("gy")
-    ids = jnp.stack([bx, by]).astype(jnp.int32)
+    bx, by = place()
     rows = 3 * NX * NY
     body = body_force.reshape(rows, NZ)
     fixed = fixed_dofs.reshape(rows, NZ)
@@ -627,23 +640,26 @@
     ext = shape(3 * SIZE, NZ)
     load, free, ylo_send, yhi_send = call(
         pack_kernel, (ext, ext, strip, strip),
-        [SMEM] + [pltpu.HBM] * 4, (ids, nodes, load_forces, body, fixed),
+        [pltpu.HBM] * 4, (nodes, load_forces, body, fixed),
         scratch=[VMEM((rows, NZ), f32), VMEM((rows, NZ), jnp.int32), VMEM((3, LOADS), jnp.int32),
-                 SMEM((3, LOADS), jnp.int32), SMEM((3, LOADS), f32), pltpu.SemaphoreType.DMA((9,))],
+                 SMEM((3, LOADS), jnp.int32), SMEM((3, LOADS), f32), SMEM((LOADS,), jnp.int32), pltpu.SemaphoreType.DMA((9,))],
         cost=pl.CostEstimate(flops=400000, transcendentals=0, bytes_accessed=2400000),
     )
     ny, nx = lax.axis_size("gy"), lax.axis_size("gx")
-    up_y = [(i, i + 1) for i in range(ny - 1)]
-    down_y = [(i + 1, i) for i in range(ny - 1)]
-    up_x = [(i, i + 1) for i in range(nx - 1)]
-    down_x = [(i + 1, i) for i in range(nx - 1)]
-    ylo = lax.ppermute(yhi_send, "gy", up_y)
-    yhi = lax.ppermute(ylo_send, "gy", down_y)
+    def swap(lo_send, hi_send, axis, count, place):
+        even = place % 2 == 0
+        one = [(i, i ^ 1) for i in range(count)]
+        two = [(i, j) for i in range(1, count - 1) for j in (i + 1 if i % 2 else i - 1,)]
+        a = lax.ppermute(jnp.where(even, hi_send, lo_send), axis, one)
+        b = lax.ppermute(jnp.where(even, lo_send, hi_send), axis, two)
+        return jnp.where(even, b, a), jnp.where(even, a, b)
+
+    ylo, yhi = swap(ylo_send, yhi_send, "gy", ny, by)
 
     coarse = call(
         mlp_kernel, shape(GX, 16, 128),
-        [SMEM, VMEM, VMEM, VMEM, VMEM, SMEM],
-        (ids, frequencies, hidden_weights, hidden_biases, output_weights.reshape(1, 128), output_bias),
+        [VMEM] * 5,
+        (frequencies, hidden_weights, hidden_biases, output_weights.reshape(1, 128), output_bias.reshape(1, 1)),
         scratch=[VMEM((16 * GX, 128), f32), VMEM((16 * GX, 128), f32), VMEM((4, 256, 256), jnp.bfloat16)],
         cost=pl.CostEstimate(flops=1500000000, transcendentals=800000, bytes_accessed=300000),
     )
@@ -651,11 +667,10 @@
     xlo_send, xhi_send = call(
         planes_kernel, (plane, plane), [VMEM] * 5, (load, free, ylo, yhi, coarse),
     )
-    xlo = lax.ppermute(xhi_send, "gx", up_x)
-    xhi = lax.ppermute(xlo_send, "gx", down_x)
+    xlo, xhi = swap(xlo_send, xhi_send, "gx", nx, bx)
     young, inverse, density = call(
         density_kernel, (shape(SIZE, NZ), shape(SIZE, NZ), shape(NX * NY, NZ)),
-        [SMEM, VMEM], (ids, coarse),
+        [VMEM], (coarse,),
         scratch=[VMEM((NX * NY, NZ), f32), pltpu.SemaphoreType.DMA],
         out_spaces=(VMEM, VMEM, pltpu.HBM),
         cost=pl.CostEstimate(flops=8000000, transcendentals=0, bytes_accessed=1300000),

time: 61.4 us -> 55 us (0.90)
  starting transfers between devices: 11.4 us -> 5.67 us
  Pallas kernels: 18.6 us -> 16.3 us
  blocking collectives: 29.3 us -> 30.4 us
  waiting for transfers between devices: 0.01 us -> 0.99 us
    ppermute x4, starting transfers between devices: 11.4 us -> 5.67 us  [the longest x2 2.88 us: swap(): a = lax.ppermute(jnp.where(even, hi_send, lo_send), axis, one)]
    pallas_call x7, Pallas kernels: 18.6 us -> 16.3 us  [call(): pl.pallas_call(kernel, out_shape=out_shape, in_specs=[spec(s) for s in in...]
    all_to_all x1, blocking collectives: 29.3 us -> 30.4 us  [per_device(): lax.all_to_all(jnp.broadcast_to(dots, (nx * ny, NZ)), ('gx', 'gy'), 0, 0,...]
    ppermute x4, waiting for transfers between devices: 0.01 us -> 0.99 us  [the longest x2 0.99 us: swap(): b = lax.ppermute(jnp.where(even, lo_send, hi_send), axis, two)]
  transfers between devices with their start and end apart: 4 -> 4, of which waited for: 0 -> 1; matrix products, arithmetic and copies ran while one was open for 0% -> 0% of each run, Pallas kernels for 16% -> 14%
where the time goes in v5:
time: 55 us; the launch traced here: 54.9 us
  blocking collectives  30.4 us (55%)
  Pallas kernels  16.3 us (30%)
  starting transfers between devices  5.67 us (10%)
  between operations  1.48 us (3%)
  waiting for transfers between devices  0.99 us (2%)
    all_to_all x1, blocking collectives, per_device(): lax.all_to_all(jnp.broadcast_to(dots, (nx * ny, NZ)), ('gx', 'gy'), 0, 0,...  30.4 us
    pallas_call x7, Pallas kernels, call(): pl.pallas_call(kernel, out_shape=out_shape, in_specs=[spec(s) for s in in...  16.3 us
    ppermute x2, starting transfers between devices, swap(): a = lax.ppermute(jnp.where(even, hi_send, lo_send), axis, one)  2.88 us
    ppermute x2, starting transfers between devices, swap(): b = lax.ppermute(jnp.where(even, lo_send, hi_send), axis, two)  2.79 us
  transfers between devices with their start and end apart: 4, of which 1 were waited for; matrix products, arithmetic and copies ran while one was open for 0% of the time, Pallas kernels for 14%

profile of v5, /device:TPU:1, one launch (start us, length us, event | category | flops | bytes accessed | tf_op | source)
XLA Modules:
  0.0 54.9 jit_solution(6102773178996437241)
XLA Ops:
  0.6 0.0 copy-start.3
  0.6 0.0 copy-start.2
  0.7 0.0 copy-start
  0.7 0.0 copy-start.1
  0.7 2.4 %shard_map.104 = (f32[2880,128]{1,0:T(8,128)S(1)}, f32[2880,128]{1,0:T(8,128)S(1)}, f32[144,128]{1,0:T(8,128)S(1)}, f32[144,128]{1,0:T(8,128)S(1)}) custom-call(s32[3,512]{1,0:T(4,128)} %bitcast.16, f32[3,512]{1,0:T(4,128)} %forces.1, f32[1536,128]{1,0:T(8,128)} %bitcast.13, s32[1536,128]{1,0:T(8,128)} %bitcast.14), custom_call_target="tpu_custom_call" | custom-call | flops 400000 | bytes 2400000 | tf_op jit(solution)/shard_map/pallas_call | solution.py:45
  3.1 2.6 %collective-permute-start.1 = (f32[144,128]{1,0:T(8,128)S(1)}, f32[144,128]{1,0:T(8,128)S(1)}, u32[]{:S(2)}, u32[]{:S(2)}) collective-permute-start(f32[144,128]{1,0:T(8,128)S(1)} %get-tuple-element.50), channel_id=1, source_target_pairs={{0,1},{1,0},{2,3},{3,2},{4,5},{5,4},{6,7},{7,6},{8,9},{9,8},{10,11... | collective-permute-start | bytes 221192 | tf_op jit(solution)/shard_map/ppermute | solution.py:653
  5.7 2.1 %collective-permute-start = (f32[144,128]{1,0:T(8,128)S(1)}, f32[144,128]{1,0:T(8,128)S(1)}, u32[]{:S(2)}, u32[]{:S(2)}) collective-permute-start(f32[144,128]{1,0:T(8,128)S(1)} %get-tuple-element.51), channel_id=1, source_target_pairs={{1,2},{2,1},{3,4},{4,3},{5,6},{6,5},{9,10},{10,9},{11,12},{12,11},... | collective-permute-start | bytes 221192 | tf_op jit(solution)/shard_map/ppermute | solution.py:654
  8.5 0.0 copy-done.3
  8.5 0.0 copy-done.2
  8.5 0.0 copy-done
  8.5 0.0 copy-done.1
  8.5 1.8 %shard_map.105.coarse = f32[6,16,128]{2,1,0:T(8,128)S(1)} custom-call(f32[3,64]{1,0:T(4,128)S(1)} %copy-done.1, f32[3,128,128]{2,1,0:T(8,128)S(1)} %copy-done, f32[3,128]{1,0:T(4,128)S(1)} %copy-done.2, f32[1,128]{1,0:T(1,128)S(1)} %bitcast.12, f32[1,1]{1,0:T(1,128)} %bitcast.9.bout), custom_call_target="tpu_custom_call" | custom-call | flops 1500000000 | bytes 300000 | tf_op jit(solution)/shard_map/pallas_call | solution.py:45
  10.4 0.0 collective-permute-done.1
  10.4 1.0 %collective-permute-done = f32[144,128]{1,0:T(8,128)S(1)} collective-permute-done((f32[144,128]{1,0:T(8,128)S(1)}, f32[144,128]{1,0:T(8,128)S(1)}, u32[]{:S(2)}, u32[]{:S(2)}) %collective-permute-start) | collective-permute-done | bytes 73760 | tf_op jit(solution)/shard_map/ppermute | solution.py:654
  11.4 0.1 shard_map.108
  11.5 0.3 collective-permute-start.3
  11.8 0.7 %collective-permute-start.2 = (f32[360,128]{1,0:T(8,128)S(1)}, f32[360,128]{1,0:T(8,128)S(1)}, u32[]{:S(2)}, u32[]{:S(2)}) collective-permute-start(f32[360,128]{1,0:T(8,128)S(1)} %get-tuple-element.47), channel_id=1, source_target_pairs={{8,16},{16,8},{24,32},{32,24},{40,48},{48,40},{56,64},{64,56},{72,... | collective-permute-start | bytes 552968 | tf_op jit(solution)/shard_map/ppermute | solution.py:654
  12.5 1.5 %shard_map.106 = (f32[960,128]{1,0:T(8,128)S(1)}, f32[960,128]{1,0:T(8,128)S(1)}, f32[512,128]{1,0:T(8,128)}) custom-call(f32[6,16,128]{2,1,0:T(8,128)S(1)} %shard_map.105.coarse), custom_call_target="tpu_custom_call" | custom-call | flops 8000000 | bytes 1300000 | tf_op jit(solution)/shard_map/pallas_call | solution.py:45
  13.9 4.3 %shard_map.107 = (f32[2880,128]{1,0:T(8,128)S(1)}, f32[2880,128]{1,0:T(8,128)S(1)}, f32[2880,128]{1,0:T(8,128)S(1)}, f32[2880,128]{1,0:T(8,128)S(1)}, f32[2880,1...) custom-call(f32[2880,128]{1,0:T(8,128)S(1)} %get-tuple-element.23.lo, ...), custom_call_target="tpu_custom_call", output_to_operand_aliasing={{0}: (0, {}), {1}: (1, {})} | custom-call | flops 60000000 | bytes 9000000 | tf_op jit(solution)/shard_map/pallas_call | solution.py:45
  18.3 0.0 collective-permute-done.3
  18.3 0.0 collective-permute-done.2
  18.3 5.1 %shard_map.109 = (f32[2880,128]{1,0:T(8,128)S(1)}, f32[2880,128]{1,0:T(8,128)S(1)}, f32[2880,128]{1,0:T(8,128)S(1)}, f32[2880,128]{1,0:T(8,128)S(1)}, f32[2880,1...) custom-call(f32[2880,128]{1,0:T(8,128)S(1)} %get-tuple-element.29.lo, ...), custom_call_target="tpu_custom_call", output_to_operand_aliasing={{0}: (0, {}), {1}: (1, {}), {2}: (2, {}), {3}: (3, {}), {4}... | custom-call | tf_op jit(solution)/shard_map/pallas_call | solution.py:45
  23.4 0.1 broadcast_in_dim.2
  23.5 30.4 %all_to_all.8 = f32[256,1,128]{2,1,0:T(1,128)S(1)} all-to-all(f32[256,1,128]{2,1,0:T(1,128)S(1)} %broadcast_in_dim.2), channel_id=1, replica_groups=mesh['gx'=32,'gy'=8] {'gx','gy'}, dimensions={0} | all-to-all | bytes 262144 | tf_op jit(solution)/shard_map/all_to_all | solution.py:691
  53.9 1.1 %shard_map.110 = f32[1536,128]{1,0:T(8,128)} custom-call(f32[256,128]{1,0:T(8,128)S(1)} %bitcast.10, f32[2880,128]{1,0:T(8,128)S(1)} %get-tuple-element.41.z, f32[2880,128]{1,0:T(8,128)S(1)} %get-tuple-element.42.y), custom_call_target="tpu_custom_call" | custom-call | tf_op jit(solution)/shard_map/pallas_call | solution.py:45
  (4 shorter events, 0.1 us)
Async XLA Ops:
  0.6 7.9 %copy-start.3 = (f32[128]{0:T(128)S(1)}, f32[128]{0:T(128)}, u32[]{:S(2)}) copy-start(f32[128]{0:T(128)} %param.16) | copy-start | bytes 1540
  0.6 7.9 %copy-start.2 = (f32[3,128]{1,0:T(4,128)S(1)}, f32[3,128]{1,0:T(4,128)}, u32[]{:S(2)}) copy-start(f32[3,128]{1,0:T(4,128)} %biases.1) | copy-start | bytes 4612
  0.7 7.9 %copy-start = (f32[3,128,128]{2,1,0:T(8,128)S(1)}, f32[3,128,128]{2,1,0:T(8,128)}, u32[]{:S(2)}) copy-start(f32[3,128,128]{2,1,0:T(8,128)} %weights.1) | copy-start | bytes 589828
  0.7 7.9 %copy-start.1 = (f32[3,64]{1,0:T(4,128)S(1)}, f32[3,64]{1,0:T(4,128)}, u32[]{:S(2)}) copy-start(f32[3,64]{1,0:T(4,128)} %freq.1) | copy-start | bytes 2308
  3.1 7.2 %collective-permute-start.1 = (f32[144,128]{1,0:T(8,128)S(1)}, f32[144,128]{1,0:T(8,128)S(1)}, u32[]{:S(2)}, u32[]{:S(2)}) collective-permute-start(f32[144,128]{1,0:T(8,128)S(1)} %get-tuple-element.50), channel_id=1, source_target_pairs={{0,1},{1,0},{2,3},{3,2},{4,5},{5,4},{6,7},{7,6},{8,9},{9,8},{10,11... | collective-permute-start | bytes 221192 | tf_op jit(solution)/shard_map/ppermute | solution.py:653
  5.7 5.7 %collective-permute-start = (f32[144,128]{1,0:T(8,128)S(1)}, f32[144,128]{1,0:T(8,128)S(1)}, u32[]{:S(2)}, u32[]{:S(2)}) collective-permute-start(f32[144,128]{1,0:T(8,128)S(1)} %get-tuple-element.51), channel_id=1, source_target_pairs={{1,2},{2,1},{3,4},{4,3},{5,6},{6,5},{9,10},{10,9},{11,12},{12,11},... | collective-permute-start | bytes 221192 | tf_op jit(solution)/shard_map/ppermute | solution.py:654
  11.5 6.8 %collective-permute-start.3 = (f32[360,128]{1,0:T(8,128)S(1)}, f32[360,128]{1,0:T(8,128)S(1)}, u32[]{:S(2)}, u32[]{:S(2)}) collective-permute-start(f32[360,128]{1,0:T(8,128)S(1)} %get-tuple-element.46), channel_id=1, source_target_pairs={{0,8},{8,0},{16,24},{24,16},{32,40},{40,32},{48,56},{56,48},{64,72... | collective-permute-start | bytes 552968 | tf_op jit(solution)/shard_map/ppermute | solution.py:653
  11.8 6.5 %collective-permute-start.2 = (f32[360,128]{1,0:T(8,128)S(1)}, f32[360,128]{1,0:T(8,128)S(1)}, u32[]{:S(2)}, u32[]{:S(2)}) collective-permute-start(f32[360,128]{1,0:T(8,128)S(1)} %get-tuple-element.47), channel_id=1, source_target_pairs={{8,16},{16,8},{24,32},{32,24},{40,48},{48,40},{56,64},{64,56},{72,... | collective-permute-start | bytes 552968 | tf_op jit(solution)/shard_map/ppermute | solution.py:654

commit v6 on v5

--- a/solution.py
+++ b/solution.py
@@ -104,40 +104,42 @@
     todo = jnp.where(mine, index, LOADS)
     lane = lax.broadcasted_iota(jnp.int32, (1, NZ), 1)
 
+    todos = [todo[:, k * 128 : (k + 1) * 128] for k in range(LOADS // 128)]
+
     def more(state):
-        return state[0] < LOADS
+        *heads, _ = state
+        return functools.reduce(jnp.minimum, heads) < LOADS
 
     def collect(state):
-        p, count = state
-        found[count] = p
-        return jnp.min(jnp.where(todo > p, todo, LOADS)), count + 1
-
-    _, count = lax.while_loop(more, collect, (jnp.min(todo), 0))
-    for copy in copies[3:]:
-        copy.wait()
-
-    def add_one(i, carry):
-        p = found[i]
-        x = nodes_s[0, p] - start_x
-        y = nodes_s[1, p] - start_y
-        hit = lane == nodes_s[2, p]
-        for c in range(3):
-            row = pl.ds((c * NX + x) * NY + y, 1)
+        *heads, count = state
+        for p in heads:
+            found[count] = p
+            count = count + jnp.where(p < LOADS, 1, 0)
+        return (*(jnp.min(jnp.where(t > p, t, LOADS)) for t, p in zip(todos, heads)), count)
+
+    *_, count = lax.while_loop(more, collect, (*(jnp.min(t) for t in todos), 0))
+    for c in range(3):
+        for copy in copies[3 + 2 * c : 5 + 2 * c]:
+            copy.wait()
+
+        def add_one(i, carry, c=c):
+            p = found[i]
+            row = pl.ds((c * NX + nodes_s[0, p] - start_x) * NY + nodes_s[1, p] - start_y, 1)
+            hit = lane == nodes_s[2, p]
             body_v[row, :] = body_v[row, :] + jnp.where(hit, forces_s[c, p], 0.0)
-        return carry
-
-    lax.fori_loop(0, count, add_one, 0)
-
-    def mask(x, carry):
-        for c in range(3):
+            return carry
+
+        lax.fori_loop(0, count, add_one, 0)
+
+        def mask(x, carry, c=c):
             src = pl.ds(pl.multiple_of((c * NX + x) * NY, NY), NY)
             dst = pl.ds(c * SIZE + (x + CF) * EY + CF, NY)
             ok = fixed_v[src, :] == 0
             load[dst, :] = jnp.where(ok, body_v[src, :], 0.0)
             free[dst, :] = jnp.where(ok, 1.0, 0.0)
-        return carry
-
-    lax.fori_loop(0, NX, mask, 0, unroll=2)
+            return carry
+
+        lax.fori_loop(0, NX, mask, 0, unroll=4)
     for c in range(3):
         base = c * SIZE + CF * EY + CF
         for j in range(2):
@@ -553,6 +555,9 @@
     dots = lax.fori_loop(
         CF + 1, LAST, lambda x, d: stages.finish_one(second, x, d), [jnp.zeros((8, NZ), f32)] * 3, unroll=7
     )
+    clear_row_past(second, LAST)
+    operator_pass(zsum2, zdiff2, young, above, minus, plus, CF + 1, LAST - 1, 6)
+    dots = dots + lax.fori_loop(CF + 2, LAST - 1, stages.finish_two, [jnp.zeros((8, NZ), f32)], unroll=4)
     for k, d in enumerate(dots):
         dots_out[k] = d
 
@@ -586,8 +591,12 @@
     for x in (CF, LAST):
         dots = stages.finish_one(second, x, dots)
 
-    operator_pass(zsum2, zdiff2, young, above, minus, plus, CF - 1, LAST + 1, 8)
-    dots = dots + lax.fori_loop(CF, LAST + 1, stages.finish_two, [jnp.zeros((8, NZ), f32)], unroll=4)
+    operator_pass(zsum2, zdiff2, young, above, minus, plus, CF - 1, CF + 2, 2)
+    operator_pass(zsum2, zdiff2, young, above, minus, plus, LAST - 2, LAST + 1, 2)
+    last = [dots_in[3]]
+    for x in (CF, CF + 1, LAST - 1, LAST):
+        last = stages.finish_two(x, last)
+    dots = dots + last
     one = lax.broadcasted_iota(jnp.int32, (1, NZ), 1)
     line = jnp.zeros((1, NZ), f32)
     for k, d in enumerate(dots):
@@ -611,16 +620,19 @@
     c1 = jnp.broadcast_to(alpha + alpha1 * (1.0 + beta), (8, NZ))[0:1, :]
     c2 = jnp.broadcast_to(-(alpha * alpha1), (8, NZ))[0:1, :]
     copies = []
-    for c in range(3):
+    half = NX // 2
+    for k in range(6):
+        c, begin = k // 2, (k % 2) * half
+
         def body(x, carry, c=c):
             src = pl.ds(c * SIZE + (x + CF) * EY + CF, NY)
             to = pl.ds(pl.multiple_of((c * NX + x) * NY, NY), NY)
             out_v[to, :] = c1 * z[src, :] + c2 * y[src, :]
             return carry
 
-        lax.fori_loop(0, NX, body, 0, unroll=4)
-        rows = pl.ds(c * NX * NY, NX * NY)
-        copy = pltpu.make_async_copy(out_v.at[rows, :], out.at[rows, :], sem.at[c])
+        lax.fori_loop(begin, begin + half, body, 0, unroll=4)
+        rows = pl.ds(k * half * NY, half * NY)
+        copy = pltpu.make_async_copy(out_v.at[rows, :], out.at[rows, :], sem.at[k])
         copy.start()
         copies.append(copy)
     for copy in copies:
@@ -642,7 +654,7 @@
         pack_kernel, (ext, ext, strip, strip),
         [pltpu.HBM] * 4, (nodes, load_forces, body, fixed),
         scratch=[VMEM((rows, NZ), f32), VMEM((rows, NZ), jnp.int32), VMEM((3, LOADS), jnp.int32),
-                 SMEM((3, LOADS), jnp.int32), SMEM((3, LOADS), f32), SMEM((LOADS,), jnp.int32), pltpu.SemaphoreType.DMA((9,))],
+                 SMEM((3, LOADS), jnp.int32), SMEM((3, LOADS), f32), SMEM((LOADS + 8,), jnp.int32), pltpu.SemaphoreType.DMA((9,))],
         cost=pl.CostEstimate(flops=400000, transcendentals=0, bytes_accessed=2400000),
     )
     ny, nx = lax.axis_size("gy"), lax.axis_size("gx")
@@ -677,7 +689,7 @@
     )
     work = [VMEM((6 * EX * TALL, NZ), f32), VMEM((3 * SIZE, NZ), f32), VMEM((3 * SIZE, NZ), f32)]
     *state, dots = call(
-        inner_kernel, (ext,) * 8 + (shape(3, 8, NZ),),
+        inner_kernel, (ext,) * 8 + (shape(QUANTITIES, 8, NZ),),
         [VMEM] * 6, (load, free, ylo, yhi, young, inverse),
         scratch=work, aliases={0: 0, 1: 1},
         cost=pl.CostEstimate(flops=60000000, transcendentals=0, bytes_accessed=9000000),
@@ -693,7 +705,7 @@
     )
     out = call(
         final_kernel, shape(rows, NZ), [VMEM] * 3, (parts, z, y),
-        scratch=[VMEM((rows, NZ), f32), pltpu.SemaphoreType.DMA((3,))], out_spaces=pltpu.HBM,
+        scratch=[VMEM((rows, NZ), f32), pltpu.SemaphoreType.DMA((6,))], out_spaces=pltpu.HBM,
     )
     return out.reshape(3, NX, NY, NZ), density.reshape(NX, NY, NZ)
 

time: 55 us -> 53.6 us (0.975)
  blocking collectives: 30.4 us -> 28.9 us
    all_to_all x1, blocking collectives: 30.4 us -> 28.9 us  [per_device(): lax.all_to_all(jnp.broadcast_to(dots, (nx * ny, NZ)), ('gx', 'gy'), 0, 0,...]
  transfers between devices with their start and end apart: 4 -> 4, of which waited for: 1 -> 1; matrix products, arithmetic and copies ran while one was open for 0% -> 0% of each run, Pallas kernels for 14% -> 20%
where the time goes in v6:
time: 53.6 us; the launch traced here: 53.3 us
  blocking collectives  28.9 us (54%)
  Pallas kernels  16.2 us (30%)
  starting transfers between devices  5.39 us (10%)
  between operations  1.49 us (3%)
  waiting for transfers between devices  1.21 us (2%)
    all_to_all x1, blocking collectives, per_device(): lax.all_to_all(jnp.broadcast_to(dots, (nx * ny, NZ)), ('gx', 'gy'), 0, 0,...  28.9 us
    pallas_call x7, Pallas kernels, call(): pl.pallas_call(kernel, out_shape=out_shape, in_specs=[spec(s) for s in in...  16.2 us
    ppermute x2, starting transfers between devices, swap(): a = lax.ppermute(jnp.where(even, hi_send, lo_send), axis, one)  2.81 us
    ppermute x2, starting transfers between devices, swap(): b = lax.ppermute(jnp.where(even, lo_send, hi_send), axis, two)  2.58 us
    ppermute x2, waiting for transfers between devices, swap(): b = lax.ppermute(jnp.where(even, lo_send, hi_send), axis, two)  1.21 us
  transfers between devices with their start and end apart: 4, of which 1 were waited for; matrix products, arithmetic and copies ran while one was open for 0% of the time, Pallas kernels for 20%

profile of v6, /device:TPU:1, one launch (start us, length us, event | category | flops | bytes accessed | tf_op | source)
XLA Modules:
  0.0 53.3 jit_solution(9120881267895034988)
XLA Ops:
  0.6 0.0 copy-start.3
  0.6 0.0 copy-start.2
  0.7 0.0 copy-start
  0.7 0.0 copy-start.1
  0.7 2.4 %shard_map.104 = (f32[2880,128]{1,0:T(8,128)S(1)}, f32[2880,128]{1,0:T(8,128)S(1)}, f32[144,128]{1,0:T(8,128)S(1)}, f32[144,128]{1,0:T(8,128)S(1)}) custom-call(s32[3,512]{1,0:T(4,128)} %bitcast.16, f32[3,512]{1,0:T(4,128)} %forces.1, f32[1536,128]{1,0:T(8,128)} %bitcast.13, s32[1536,128]{1,0:T(8,128)} %bitcast.14), custom_call_target="tpu_custom_call" | custom-call | flops 400000 | bytes 2400000 | tf_op jit(solution)/shard_map/pallas_call | solution.py:45
  3.1 2.7 %collective-permute-start.1 = (f32[144,128]{1,0:T(8,128)S(1)}, f32[144,128]{1,0:T(8,128)S(1)}, u32[]{:S(2)}, u32[]{:S(2)}) collective-permute-start(f32[144,128]{1,0:T(8,128)S(1)} %get-tuple-element.50), channel_id=1, source_target_pairs={{0,1},{1,0},{2,3},{3,2},{4,5},{5,4},{6,7},{7,6},{8,9},{9,8},{10,11... | collective-permute-start | bytes 221192 | tf_op jit(solution)/shard_map/ppermute | solution.py:665
  5.8 1.9 %collective-permute-start = (f32[144,128]{1,0:T(8,128)S(1)}, f32[144,128]{1,0:T(8,128)S(1)}, u32[]{:S(2)}, u32[]{:S(2)}) collective-permute-start(f32[144,128]{1,0:T(8,128)S(1)} %get-tuple-element.51), channel_id=1, source_target_pairs={{1,2},{2,1},{3,4},{4,3},{5,6},{6,5},{9,10},{10,9},{11,12},{12,11},... | collective-permute-start | bytes 221192 | tf_op jit(solution)/shard_map/ppermute | solution.py:666
  8.4 0.0 copy-done.3
  8.4 0.0 copy-done.2
  8.4 0.0 copy-done
  8.4 0.0 copy-done.1
  8.4 1.8 %shard_map.105.coarse = f32[6,16,128]{2,1,0:T(8,128)S(1)} custom-call(f32[3,64]{1,0:T(4,128)S(1)} %copy-done.1, f32[3,128,128]{2,1,0:T(8,128)S(1)} %copy-done, f32[3,128]{1,0:T(4,128)S(1)} %copy-done.2, f32[1,128]{1,0:T(1,128)S(1)} %bitcast.12, f32[1,1]{1,0:T(1,128)} %bitcast.9.bout), custom_call_target="tpu_custom_call" | custom-call | flops 1500000000 | bytes 300000 | tf_op jit(solution)/shard_map/pallas_call | solution.py:45
  10.3 0.0 collective-permute-done.1
  10.3 1.2 %collective-permute-done = f32[144,128]{1,0:T(8,128)S(1)} collective-permute-done((f32[144,128]{1,0:T(8,128)S(1)}, f32[144,128]{1,0:T(8,128)S(1)}, u32[]{:S(2)}, u32[]{:S(2)}) %collective-permute-start) | collective-permute-done | bytes 73760 | tf_op jit(solution)/shard_map/ppermute | solution.py:666
  11.5 0.1 shard_map.108
  11.6 0.1 collective-permute-start.3
  11.7 0.7 %collective-permute-start.2 = (f32[360,128]{1,0:T(8,128)S(1)}, f32[360,128]{1,0:T(8,128)S(1)}, u32[]{:S(2)}, u32[]{:S(2)}) collective-permute-start(f32[360,128]{1,0:T(8,128)S(1)} %get-tuple-element.47), channel_id=1, source_target_pairs={{8,16},{16,8},{24,32},{32,24},{40,48},{48,40},{56,64},{64,56},{72,... | collective-permute-start | bytes 552968 | tf_op jit(solution)/shard_map/ppermute | solution.py:666
  12.4 1.5 %shard_map.106 = (f32[960,128]{1,0:T(8,128)S(1)}, f32[960,128]{1,0:T(8,128)S(1)}, f32[512,128]{1,0:T(8,128)}) custom-call(f32[6,16,128]{2,1,0:T(8,128)S(1)} %shard_map.105.coarse), custom_call_target="tpu_custom_call" | custom-call | flops 8000000 | bytes 1300000 | tf_op jit(solution)/shard_map/pallas_call | solution.py:45
  13.9 7.2 %shard_map.107 = (f32[2880,128]{1,0:T(8,128)S(1)}, f32[2880,128]{1,0:T(8,128)S(1)}, f32[2880,128]{1,0:T(8,128)S(1)}, f32[2880,128]{1,0:T(8,128)S(1)}, f32[2880,1...) custom-call(f32[2880,128]{1,0:T(8,128)S(1)} %get-tuple-element.23.lo, ...), custom_call_target="tpu_custom_call", output_to_operand_aliasing={{0}: (0, {}), {1}: (1, {})} | custom-call | flops 60000000 | bytes 9000000 | tf_op jit(solution)/shard_map/pallas_call | solution.py:45
  21.1 0.0 collective-permute-done.3
  21.1 0.0 collective-permute-done.2
  21.1 2.1 %shard_map.109 = (f32[2880,128]{1,0:T(8,128)S(1)}, f32[2880,128]{1,0:T(8,128)S(1)}, f32[2880,128]{1,0:T(8,128)S(1)}, f32[2880,128]{1,0:T(8,128)S(1)}, f32[2880,1...) custom-call(f32[2880,128]{1,0:T(8,128)S(1)} %get-tuple-element.29.lo, ...), custom_call_target="tpu_custom_call", output_to_operand_aliasing={{0}: (0, {}), {1}: (1, {}), {2}: (2, {}), {3}: (3, {}), {4}... | custom-call | tf_op jit(solution)/shard_map/pallas_call | solution.py:45
  23.3 0.1 broadcast_in_dim.2
  23.4 28.9 %all_to_all.8 = f32[256,1,128]{2,1,0:T(1,128)S(1)} all-to-all(f32[256,1,128]{2,1,0:T(1,128)S(1)} %broadcast_in_dim.2), channel_id=1, replica_groups=mesh['gx'=32,'gy'=8] {'gx','gy'}, dimensions={0} | all-to-all | bytes 262144 | tf_op jit(solution)/shard_map/all_to_all | solution.py:703
  52.2 1.1 %shard_map.110 = f32[1536,128]{1,0:T(8,128)} custom-call(f32[256,128]{1,0:T(8,128)S(1)} %bitcast.10, f32[2880,128]{1,0:T(8,128)S(1)} %get-tuple-element.41.z, f32[2880,128]{1,0:T(8,128)S(1)} %get-tuple-element.42.y), custom_call_target="tpu_custom_call" | custom-call | tf_op jit(solution)/shard_map/pallas_call | solution.py:45
  (4 shorter events, 0.1 us)
Async XLA Ops:
  0.6 7.8 %copy-start.3 = (f32[128]{0:T(128)S(1)}, f32[128]{0:T(128)}, u32[]{:S(2)}) copy-start(f32[128]{0:T(128)} %param.16) | copy-start | bytes 1540
  0.6 7.8 %copy-start.2 = (f32[3,128]{1,0:T(4,128)S(1)}, f32[3,128]{1,0:T(4,128)}, u32[]{:S(2)}) copy-start(f32[3,128]{1,0:T(4,128)} %biases.1) | copy-start | bytes 4612
  0.7 7.8 %copy-start = (f32[3,128,128]{2,1,0:T(8,128)S(1)}, f32[3,128,128]{2,1,0:T(8,128)}, u32[]{:S(2)}) copy-start(f32[3,128,128]{2,1,0:T(8,128)} %weights.1) | copy-start | bytes 589828
  0.7 7.8 %copy-start.1 = (f32[3,64]{1,0:T(4,128)S(1)}, f32[3,64]{1,0:T(4,128)}, u32[]{:S(2)}) copy-start(f32[3,64]{1,0:T(4,128)} %freq.1) | copy-start | bytes 2308
  3.1 7.2 %collective-permute-start.1 = (f32[144,128]{1,0:T(8,128)S(1)}, f32[144,128]{1,0:T(8,128)S(1)}, u32[]{:S(2)}, u32[]{:S(2)}) collective-permute-start(f32[144,128]{1,0:T(8,128)S(1)} %get-tuple-element.50), channel_id=1, source_target_pairs={{0,1},{1,0},{2,3},{3,2},{4,5},{5,4},{6,7},{7,6},{8,9},{9,8},{10,11... | collective-permute-start | bytes 221192 | tf_op jit(solution)/shard_map/ppermute | solution.py:665
  5.8 5.7 %collective-permute-start = (f32[144,128]{1,0:T(8,128)S(1)}, f32[144,128]{1,0:T(8,128)S(1)}, u32[]{:S(2)}, u32[]{:S(2)}) collective-permute-start(f32[144,128]{1,0:T(8,128)S(1)} %get-tuple-element.51), channel_id=1, source_target_pairs={{1,2},{2,1},{3,4},{4,3},{5,6},{6,5},{9,10},{10,9},{11,12},{12,11},... | collective-permute-start | bytes 221192 | tf_op jit(solution)/shard_map/ppermute | solution.py:666
  11.6 9.5 %collective-permute-start.3 = (f32[360,128]{1,0:T(8,128)S(1)}, f32[360,128]{1,0:T(8,128)S(1)}, u32[]{:S(2)}, u32[]{:S(2)}) collective-permute-start(f32[360,128]{1,0:T(8,128)S(1)} %get-tuple-element.46), channel_id=1, source_target_pairs={{0,8},{8,0},{16,24},{24,16},{32,40},{40,32},{48,56},{56,48},{64,72... | collective-permute-start | bytes 552968 | tf_op jit(solution)/shard_map/ppermute | solution.py:665
  11.7 9.4 %collective-permute-start.2 = (f32[360,128]{1,0:T(8,128)S(1)}, f32[360,128]{1,0:T(8,128)S(1)}, u32[]{:S(2)}, u32[]{:S(2)}) collective-permute-start(f32[360,128]{1,0:T(8,128)S(1)} %get-tuple-element.47), channel_id=1, source_target_pairs={{8,16},{16,8},{24,32},{32,24},{40,48},{48,40},{56,64},{64,56},{72,... | collective-permute-start | bytes 552968 | tf_op jit(solution)/shard_map/ppermute | solution.py:666

commit v7 on v6

--- a/solution.py
+++ b/solution.py
@@ -661,9 +661,10 @@
     def swap(lo_send, hi_send, axis, count, place):
         even = place % 2 == 0
         one = [(i, i ^ 1) for i in range(count)]
-        two = [(i, j) for i in range(1, count - 1) for j in (i + 1 if i % 2 else i - 1,)]
+        two = [(i, (i + 1 if i % 2 else i - 1) % count) for i in range(count)]
         a = lax.ppermute(jnp.where(even, hi_send, lo_send), axis, one)
         b = lax.ppermute(jnp.where(even, lo_send, hi_send), axis, two)
+        b = jnp.where((place == 0) | (place == count - 1), 0.0, b)
         return jnp.where(even, b, a), jnp.where(even, a, b)
 
     ylo, yhi = swap(ylo_send, yhi_send, "gy", ny, by)

time: 53.6 us -> 51.9 us (0.968)
  blocking collectives: 28.9 us -> 20.5 us
  starting transfers between devices: 5.39 us -> 11.7 us
  other arithmetic: 0.09 us -> 2.33 us
  waiting for transfers between devices: 1.21 us -> 0.01 us
  Pallas kernels: 16.2 us -> 15.6 us
    all_to_all x1, blocking collectives: 28.9 us -> 20.5 us  [per_device(): lax.all_to_all(jnp.broadcast_to(dots, (nx * ny, NZ)), ('gx', 'gy'), 0, 0,...]
    ppermute x2, starting transfers between devices: 2.58 us -> 10.7 us  [swap(): b = lax.ppermute(jnp.where(even, lo_send, hi_send), axis, two)]
    ppermute x2, starting transfers between devices: 2.81 us -> 1 us  [swap(): a = lax.ppermute(jnp.where(even, hi_send, lo_send), axis, one)]
    select_n x2, other arithmetic: 0.04 us -> 1.35 us  [swap(): b = lax.ppermute(jnp.where(even, lo_send, hi_send), axis, two)]
    ppermute x2, waiting for transfers between devices: 1.21 us -> 0.01 us  [swap(): b = lax.ppermute(jnp.where(even, lo_send, hi_send), axis, two)]
    select_n x2, other arithmetic: 0.04 us -> 0.98 us  [swap(): return (jnp.where(even, b, a), jnp.where(even, a, b))]
    pallas_call x7, Pallas kernels: 16.2 us -> 15.6 us  [call(): pl.pallas_call(kernel, out_shape=out_shape, in_specs=[spec(s) for s in in...]
  transfers between devices with their start and end apart: 4 -> 4, of which waited for: 1 -> 0; matrix products, arithmetic and copies ran while one was open for 0% -> 0% of each run, Pallas kernels for 20% -> 20%
where the time goes in v7:
time: 51.9 us; the launch traced here: 51.7 us
  blocking collectives  20.5 us (39%)
  Pallas kernels  15.6 us (30%)
  starting transfers between devices  11.7 us (23%)
  other arithmetic  2.33 us (4%)
  between operations  1.46 us (3%)
    all_to_all x1, blocking collectives, per_device(): lax.all_to_all(jnp.broadcast_to(dots, (nx * ny, NZ)), ('gx', 'gy'), 0, 0,...  20.5 us
    pallas_call x7, Pallas kernels, call(): pl.pallas_call(kernel, out_shape=out_shape, in_specs=[spec(s) for s in in...  15.6 us
    ppermute x2, starting transfers between devices, swap(): b = lax.ppermute(jnp.where(even, lo_send, hi_send), axis, two)  10.7 us
    select_n x2, other arithmetic, swap(): b = lax.ppermute(jnp.where(even, lo_send, hi_send), axis, two)  1.35 us
  transfers between devices with their start and end apart: 4, of which 0 were waited for; matrix products, arithmetic and copies ran while one was open for 0% of the time, Pallas kernels for 20%

profile of v7, /device:TPU:1, one launch (start us, length us, event | category | flops | bytes accessed | tf_op | source)
XLA Modules:
  0.0 51.7 jit_solution(4380949741361687357)
XLA Ops:
  0.6 0.0 copy-start.3
  0.6 0.0 copy-start.2
  0.7 0.0 copy-start
  0.7 0.0 copy-start.1
  0.7 1.9 %shard_map.104 = (f32[2880,128]{1,0:T(8,128)S(1)}, f32[2880,128]{1,0:T(8,128)S(1)}, f32[144,128]{1,0:T(8,128)S(1)}, f32[144,128]{1,0:T(8,128)S(1)}) custom-call(s32[3,512]{1,0:T(4,128)} %bitcast.16, f32[3,512]{1,0:T(4,128)} %forces.1, f32[1536,128]{1,0:T(8,128)} %bitcast.13, s32[1536,128]{1,0:T(8,128)} %bitcast.14), custom_call_target="tpu_custom_call" | custom-call | flops 400000 | bytes 2400000 | tf_op jit(solution)/shard_map/pallas_call | solution.py:45
  2.6 0.6 %broadcast_select_fusion.3 = (f32[144,128]{1,0:T(8,128)}, f32[144,128]{1,0:T(8,128)S(1)}) fusion(f32[144,128]{1,0:T(8,128)S(1)} %get-tuple-element.25, f32[144,128]{1,0:T(8,128)S(1)} %get-tuple-element.26, pred[]{:T(512)S(6)} %eq.21), kind=kLoop, calls=%fused_computation.7 | loop fusion | flops 36864 | bytes 294913 | tf_op jit(solution)/shard_map/jit(_where)/select_n | solution.py:666
  3.2 2.7 %collective-permute-start = (f32[144,128]{1,0:T(8,128)}, f32[144,128]{1,0:T(8,128)S(1)}, u32[]{:S(2)}, u32[]{:S(2)}) collective-permute-start(f32[144,128]{1,0:T(8,128)} %get-tuple-element.50), channel_id=1, source_target_pairs={{0,7},{1,2},{2,1},{3,4},{4,3},{5,6},{6,5},{7,0},{8,15},{9,10},{10,... | collective-permute-start | bytes 221192 | tf_op jit(solution)/shard_map/ppermute | solution.py:666
  5.9 1.0 %collective-permute-start.1 = (f32[144,128]{1,0:T(8,128)S(1)}, f32[144,128]{1,0:T(8,128)S(1)}, u32[]{:S(2)}, u32[]{:S(2)}) collective-permute-start(f32[144,128]{1,0:T(8,128)S(1)} %get-tuple-element.51), channel_id=1, source_target_pairs={{0,1},{1,0},{2,3},{3,2},{4,5},{5,4},{6,7},{7,6},{8,9},{9,8},{10,11... | collective-permute-start | bytes 221192 | tf_op jit(solution)/shard_map/ppermute | solution.py:665
  7.5 0.0 copy-done.3
  7.5 0.0 copy-done.2
  7.6 0.0 copy-done
  7.6 0.0 copy-done.1
  7.6 1.8 %shard_map.105.coarse = f32[6,16,128]{2,1,0:T(8,128)S(1)} custom-call(f32[3,64]{1,0:T(4,128)S(1)} %copy-done.1, f32[3,128,128]{2,1,0:T(8,128)S(1)} %copy-done, f32[3,128]{1,0:T(4,128)S(1)} %copy-done.2, f32[1,128]{1,0:T(1,128)S(1)} %bitcast.12, f32[1,1]{1,0:T(1,128)} %bitcast.9.bout), custom_call_target="tpu_custom_call" | custom-call | flops 1500000000 | bytes 300000 | tf_op jit(solution)/shard_map/pallas_call | solution.py:45
  9.4 0.0 collective-permute-done
  9.4 0.0 collective-permute-done.1
  9.4 0.1 shard_map.108
  9.5 0.7 %broadcast_select_fusion.1 = (f32[360,128]{1,0:T(8,128)}, f32[360,128]{1,0:T(8,128)S(1)}) fusion(f32[360,128]{1,0:T(8,128)S(1)} %get-tuple-element.37, f32[360,128]{1,0:T(8,128)S(1)} %get-tuple-element.38, pred[]{:T(512)S(6)} %eq.24), kind=kLoop, calls=%fused_computation.3 | loop fusion | flops 92160 | bytes 737281 | tf_op jit(solution)/shard_map/jit(_where)/select_n | solution.py:666
  10.2 8.0 %collective-permute-start.2 = (f32[360,128]{1,0:T(8,128)}, f32[360,128]{1,0:T(8,128)S(1)}, u32[]{:S(2)}, u32[]{:S(2)}) collective-permute-start(f32[360,128]{1,0:T(8,128)} %get-tuple-element.46), channel_id=1, source_target_pairs={{0,248},{8,16},{16,8},{24,32},{32,24},{40,48},{48,40},{56,64},{64,... | collective-permute-start | bytes 552968 | tf_op jit(solution)/shard_map/ppermute | solution.py:666
  18.2 0.0 collective-permute-start.3
  18.2 1.5 %shard_map.106 = (f32[960,128]{1,0:T(8,128)S(1)}, f32[960,128]{1,0:T(8,128)S(1)}, f32[512,128]{1,0:T(8,128)}) custom-call(f32[6,16,128]{2,1,0:T(8,128)S(1)} %shard_map.105.coarse), custom_call_target="tpu_custom_call" | custom-call | flops 8000000 | bytes 1300000 | tf_op jit(solution)/shard_map/pallas_call | solution.py:45
  19.7 7.2 %shard_map.107 = (f32[2880,128]{1,0:T(8,128)S(1)}, f32[2880,128]{1,0:T(8,128)S(1)}, f32[2880,128]{1,0:T(8,128)S(1)}, f32[2880,128]{1,0:T(8,128)S(1)}, f32[2880,1...) custom-call(f32[2880,128]{1,0:T(8,128)S(1)} %get-tuple-element.23.lo, ...), custom_call_target="tpu_custom_call", output_to_operand_aliasing={{0}: (0, {}), {1}: (1, {})} | custom-call | flops 60000000 | bytes 9000000 | tf_op jit(solution)/shard_map/pallas_call | solution.py:45
  26.9 0.0 collective-permute-done.2
  26.9 0.0 collective-permute-done.3
  27.0 1.0 %select_select_fusion = (f32[360,128]{1,0:T(8,128)S(1)}, f32[360,128]{1,0:T(8,128)S(1)}) fusion(f32[360,128]{1,0:T(8,128)} %collective-permute-done.3, f32[360,128]{1,0:T(8,128)S(1)} %collective-permute-done.2, pred[]{:T(512)S(6)} %or.7, pred[]{:T(512)S(6)} %eq.24), kind=kLoop, calls=%fused_computation | loop fusion | flops 138240 | bytes 737282 | tf_op jit(solution)/shard_map/jit(_where)/select_n | solution.py:668
  27.9 2.1 %shard_map.109 = (f32[2880,128]{1,0:T(8,128)S(1)}, f32[2880,128]{1,0:T(8,128)S(1)}, f32[2880,128]{1,0:T(8,128)S(1)}, f32[2880,128]{1,0:T(8,128)S(1)}, f32[2880,1...) custom-call(f32[2880,128]{1,0:T(8,128)S(1)} %get-tuple-element.29.lo, ...), custom_call_target="tpu_custom_call", output_to_operand_aliasing={{0}: (0, {}), {1}: (1, {}), {2}: (2, {}), {3}: (3, {}), {4}... | custom-call | tf_op jit(solution)/shard_map/pallas_call | solution.py:45
  30.1 0.1 broadcast_in_dim.15
  30.1 20.5 %all_to_all.8 = f32[256,1,128]{2,1,0:T(1,128)S(1)} all-to-all(f32[256,1,128]{2,1,0:T(1,128)S(1)} %broadcast_in_dim.15), channel_id=1, replica_groups=mesh['gx'=32,'gy'=8] {'gx','gy'}, dimensions={0} | all-to-all | bytes 262144 | tf_op jit(solution)/shard_map/all_to_all | solution.py:704
  50.6 1.1 %shard_map.110 = f32[1536,128]{1,0:T(8,128)} custom-call(f32[256,128]{1,0:T(8,128)S(1)} %bitcast.10, f32[2880,128]{1,0:T(8,128)S(1)} %get-tuple-element.41.z, f32[2880,128]{1,0:T(8,128)S(1)} %get-tuple-element.42.y), custom_call_target="tpu_custom_call" | custom-call | tf_op jit(solution)/shard_map/pallas_call | solution.py:45
  (1 shorter events, 0.0 us)
Async XLA Ops:
  0.6 6.9 %copy-start.3 = (f32[128]{0:T(128)S(1)}, f32[128]{0:T(128)}, u32[]{:S(2)}) copy-start(f32[128]{0:T(128)} %param.16) | copy-start | bytes 1540
  0.6 6.9 %copy-start.2 = (f32[3,128]{1,0:T(4,128)S(1)}, f32[3,128]{1,0:T(4,128)}, u32[]{:S(2)}) copy-start(f32[3,128]{1,0:T(4,128)} %biases.1) | copy-start | bytes 4612
  0.7 6.9 %copy-start = (f32[3,128,128]{2,1,0:T(8,128)S(1)}, f32[3,128,128]{2,1,0:T(8,128)}, u32[]{:S(2)}) copy-start(f32[3,128,128]{2,1,0:T(8,128)} %weights.1) | copy-start | bytes 589828
  0.7 6.9 %copy-start.1 = (f32[3,64]{1,0:T(4,128)S(1)}, f32[3,64]{1,0:T(4,128)}, u32[]{:S(2)}) copy-start(f32[3,64]{1,0:T(4,128)} %freq.1) | copy-start | bytes 2308
  3.2 6.2 %collective-permute-start = (f32[144,128]{1,0:T(8,128)}, f32[144,128]{1,0:T(8,128)S(1)}, u32[]{:S(2)}, u32[]{:S(2)}) collective-permute-start(f32[144,128]{1,0:T(8,128)} %get-tuple-element.50), channel_id=1, source_target_pairs={{0,7},{1,2},{2,1},{3,4},{4,3},{5,6},{6,5},{7,0},{8,15},{9,10},{10,... | collective-permute-start | bytes 221192 | tf_op jit(solution)/shard_map/ppermute | solution.py:666
  5.9 3.5 %collective-permute-start.1 = (f32[144,128]{1,0:T(8,128)S(1)}, f32[144,128]{1,0:T(8,128)S(1)}, u32[]{:S(2)}, u32[]{:S(2)}) collective-permute-start(f32[144,128]{1,0:T(8,128)S(1)} %get-tuple-element.51), channel_id=1, source_target_pairs={{0,1},{1,0},{2,3},{3,2},{4,5},{5,4},{6,7},{7,6},{8,9},{9,8},{10,11... | collective-permute-start | bytes 221192 | tf_op jit(solution)/shard_map/ppermute | solution.py:665
  10.2 16.7 %collective-permute-start.2 = (f32[360,128]{1,0:T(8,128)}, f32[360,128]{1,0:T(8,128)S(1)}, u32[]{:S(2)}, u32[]{:S(2)}) collective-permute-start(f32[360,128]{1,0:T(8,128)} %get-tuple-element.46), channel_id=1, source_target_pairs={{0,248},{8,16},{16,8},{24,32},{32,24},{40,48},{48,40},{56,64},{64,... | collective-permute-start | bytes 552968 | tf_op jit(solution)/shard_map/ppermute | solution.py:666
  18.2 8.7 %collective-permute-start.3 = (f32[360,128]{1,0:T(8,128)S(1)}, f32[360,128]{1,0:T(8,128)}, u32[]{:S(2)}, u32[]{:S(2)}) collective-permute-start(f32[360,128]{1,0:T(8,128)S(1)} %get-tuple-element.47), channel_id=1, source_target_pairs={{0,8},{8,0},{16,24},{24,16},{32,40},{40,32},{48,56},{56,48},{64,72... | collective-permute-start | bytes 552968 | tf_op jit(solution)/shard_map/ppermute | solution.py:665

commit v8 on v7

--- a/solution.py
+++ b/solution.py
@@ -58,13 +58,25 @@
     return lax.axis_index("gx"), lax.axis_index("gy")
 
 
+def in_pairs(position, action, a, b):
+    even = (position & 1) == 0
+
+    @pl.when(even)
+    def _():
+        action(b, a)
+
+    @pl.when(jnp.logical_not(even))
+    def _():
+        action(a, b)
+
+
 def shape(*dims):
     return jax.ShapeDtypeStruct(dims, f32)
 
 
 def pack_kernel(
     nodes, forces, body, fixed,
-    load, free, lo_out, hi_out,
+    load, free, a_out, b_out,
     body_v, fixed_v, nodes_v, nodes_s, forces_s, found, sem,
 ):
     part = NX * NY
@@ -140,35 +152,42 @@
             return carry
 
         lax.fori_loop(0, NX, mask, 0, unroll=4)
-    for c in range(3):
-        base = c * SIZE + CF * EY + CF
-        for j in range(2):
-            to = pl.ds((c * 2 + j) * NX, NX)
-            lo_out[to, :] = load[pl.ds(base + j, NX, stride=EY), :]
-            hi_out[to, :] = load[pl.ds(base + NY - 2 + j, NX, stride=EY), :]
-        to = pl.ds((6 + c) * NX, NX)
-        lo_out[to, :] = free[pl.ds(base, NX, stride=EY), :]
-        hi_out[to, :] = free[pl.ds(base + NY - 1, NX, stride=EY), :]
-
-
-def planes_kernel(load, free, ylo, yhi, coarse, lo_out, hi_out):
+    def strips(lo_out, hi_out):
+        for c in range(3):
+            base = c * SIZE + CF * EY + CF
+            for j in range(2):
+                to = pl.ds((c * 2 + j) * NX, NX)
+                lo_out[to, :] = load[pl.ds(base + j, NX, stride=EY), :]
+                hi_out[to, :] = load[pl.ds(base + NY - 2 + j, NX, stride=EY), :]
+            to = pl.ds((6 + c) * NX, NX)
+            lo_out[to, :] = free[pl.ds(base, NX, stride=EY), :]
+            hi_out[to, :] = free[pl.ds(base + NY - 1, NX, stride=EY), :]
+
+    in_pairs(ids[1], strips, a_out, b_out)
+
+
+def planes_kernel(load, free, ylo, yhi, coarse, a_out, b_out):
     del coarse
-    for out, first in ((lo_out, CF), (hi_out, CF + NX - 2)):
-        for c in range(3):
-            for j in range(2):
-                x = first + j
-                base = (c * 2 + j) * EY
-                out[pl.ds(base, EY), :] = load[pl.ds(c * SIZE + x * EY, EY), :]
-                for k in range(2):
-                    at = pl.ds((c * 2 + k) * NX + x - CF, 1)
-                    out[pl.ds(base + 2 + k, 1), :] = ylo[at, :]
-                    out[pl.ds(base + 36 + k, 1), :] = yhi[at, :]
-            x = CF if first == CF else CF + NX - 1
-            base = (6 + c) * EY
-            out[pl.ds(base, EY), :] = free[pl.ds(c * SIZE + x * EY, EY), :]
-            at = pl.ds((6 + c) * NX + x - CF, 1)
-            out[pl.ds(base + 3, 1), :] = ylo[at, :]
-            out[pl.ds(base + 36, 1), :] = yhi[at, :]
+
+    def planes(lo_out, hi_out):
+        for out, first in ((lo_out, CF), (hi_out, CF + NX - 2)):
+            for c in range(3):
+                for j in range(2):
+                    x = first + j
+                    base = (c * 2 + j) * EY
+                    out[pl.ds(base, EY), :] = load[pl.ds(c * SIZE + x * EY, EY), :]
+                    for k in range(2):
+                        at = pl.ds((c * 2 + k) * NX + x - CF, 1)
+                        out[pl.ds(base + 2 + k, 1), :] = ylo[at, :]
+                        out[pl.ds(base + 36 + k, 1), :] = yhi[at, :]
+                x = CF if first == CF else CF + NX - 1
+                base = (6 + c) * EY
+                out[pl.ds(base, EY), :] = free[pl.ds(c * SIZE + x * EY, EY), :]
+                at = pl.ds((6 + c) * NX + x - CF, 1)
+                out[pl.ds(base + 3, 1), :] = ylo[at, :]
+                out[pl.ds(base + 36, 1), :] = yhi[at, :]
+
+    in_pairs(place()[0], planes, a_out, b_out)
 
 
 def split2(v):
@@ -564,17 +583,30 @@
 
 def outer_kernel(
     load_in, free_in, field_in, scaled_in, zsum_in, zdiff_in, zsum2_in, zdiff2_in,
-    xlo, xhi, young, inverse, dots_in,
+    xa, xb, young, inverse, dots_in,
     load, free, field, scaled, zsum, zdiff, zsum2, zdiff2, dots_out,
     above, minus, plus,
 ):
     del load_in, free_in, field_in, scaled_in, zsum_in, zdiff_in, zsum2_in, zdiff2_in
-    for c in range(3):
-        for k in range(2):
-            for plane, x in ((xlo, 2 + k), (xhi, LAST + 1 + k)):
-                load[pl.ds(c * SIZE + x * EY, EY), :] = plane[pl.ds((c * 2 + k) * EY, EY), :]
-        for plane, x in ((xlo, 3), (xhi, LAST + 1)):
-            free[pl.ds(c * SIZE + x * EY, EY), :] = plane[pl.ds((6 + c) * EY, EY), :]
+    bx = place()[0]
+
+    def insert(xlo, xhi):
+        for c in range(3):
+            for plane, x, k, ok in (
+                (xlo, 2, 0, bx > 0),
+                (xlo, 3, 1, bx > 0),
+                (xhi, LAST + 1, 0, bx < TOTAL_X // NX - 1),
+                (xhi, LAST + 2, 1, bx < TOTAL_X // NX - 1),
+            ):
+                load[pl.ds(c * SIZE + x * EY, EY), :] = jnp.where(
+                    ok, plane[pl.ds((c * 2 + k) * EY, EY), :], 0.0
+                )
+                if x in (3, LAST + 1):
+                    free[pl.ds(c * SIZE + x * EY, EY), :] = jnp.where(
+                        ok, plane[pl.ds((6 + c) * EY, EY), :], 0.0
+                    )
+
+    in_pairs(bx, insert, xa, xb)
     stages = Stages(load, free, inverse, field, scaled, minus, plus)
     first, second = (zsum, zdiff), (zsum2, zdiff2)
     for start in (2, LAST + 1):
@@ -650,7 +682,7 @@
     nodes = load_nodes.T
     strip = shape(9 * NX, NZ)
     ext = shape(3 * SIZE, NZ)
-    load, free, ylo_send, yhi_send = call(
+    load, free, ya_send, yb_send = call(
         pack_kernel, (ext, ext, strip, strip),
         [pltpu.HBM] * 4, (nodes, load_forces, body, fixed),
         scratch=[VMEM((rows, NZ), f32), VMEM((rows, NZ), jnp.int32), VMEM((3, LOADS), jnp.int32),
@@ -658,16 +690,14 @@
         cost=pl.CostEstimate(flops=400000, transcendentals=0, bytes_accessed=2400000),
     )
     ny, nx = lax.axis_size("gy"), lax.axis_size("gx")
-    def swap(lo_send, hi_send, axis, count, place):
-        even = place % 2 == 0
+    def swap(a_send, b_send, axis, count):
         one = [(i, i ^ 1) for i in range(count)]
         two = [(i, (i + 1 if i % 2 else i - 1) % count) for i in range(count)]
-        a = lax.ppermute(jnp.where(even, hi_send, lo_send), axis, one)
-        b = lax.ppermute(jnp.where(even, lo_send, hi_send), axis, two)
-        b = jnp.where((place == 0) | (place == count - 1), 0.0, b)
-        return jnp.where(even, b, a), jnp.where(even, a, b)
-
-    ylo, yhi = swap(ylo_send, yhi_send, "gy", ny, by)
+        return lax.ppermute(a_send, axis, one), lax.ppermute(b_send, axis, two)
+
+    ya, yb = swap(ya_send, yb_send, "gy", ny)
+    yb = jnp.where((by == 0) | (by == ny - 1), 0.0, yb)
+    ylo, yhi = jnp.where(by % 2 == 0, yb, ya), jnp.where(by % 2 == 0, ya, yb)
 
     coarse = call(
         mlp_kernel, shape(GX, 16, 128),
@@ -677,10 +707,10 @@
         cost=pl.CostEstimate(flops=1500000000, transcendentals=800000, bytes_accessed=300000),
     )
     plane = shape(9 * EY, NZ)
-    xlo_send, xhi_send = call(
+    xa_send, xb_send = call(
         planes_kernel, (plane, plane), [VMEM] * 5, (load, free, ylo, yhi, coarse),
     )
-    xlo, xhi = swap(xlo_send, xhi_send, "gx", nx, bx)
+    xa, xb = swap(xa_send, xb_send, "gx", nx)
     young, inverse, density = call(
         density_kernel, (shape(SIZE, NZ), shape(SIZE, NZ), shape(NX * NY, NZ)),
         [VMEM], (coarse,),
@@ -697,7 +727,7 @@
     )
     *state, dots = call(
         outer_kernel, (ext,) * 8 + (shape(1, NZ),),
-        [VMEM] * 13, (*state, xlo, xhi, young, inverse, dots),
+        [VMEM] * 13, (*state, xa, xb, young, inverse, dots),
         scratch=work, aliases={i: i for i in range(8)},
     )
     z, y = state[2], state[3]

time: 51.9 us -> 49.7 us (0.958)
  other arithmetic: 2.33 us -> 0.02 us
  starting transfers between devices: 11.7 us -> 12.4 us
  blocking collectives: 20.5 us -> 19.9 us
    select_n x4 -> x1, other arithmetic: 2.33 us -> 0.02 us  [per_device(): ylo, yhi = (jnp.where(by % 2 == 0, yb, ya), jnp.where(by % 2 == 0, ya, yb))]
    ppermute x4, starting transfers between devices: 11.7 us -> 12.4 us  [swap(): return (lax.ppermute(a_send, axis, one), lax.ppermute(b_send, axis, two))]
    all_to_all x1, blocking collectives: 20.5 us -> 19.9 us  [per_device(): lax.all_to_all(jnp.broadcast_to(dots, (nx * ny, NZ)), ('gx', 'gy'), 0, 0,...]
  transfers between devices with their start and end apart: 4 -> 4, of which waited for: 0 -> 0; matrix products, arithmetic and copies ran while one was open for 0% -> 0% of each run, Pallas kernels for 20% -> 21%
where the time goes in v8:
time: 49.7 us; the launch traced here: 49.6 us
  blocking collectives  19.9 us (40%)
  Pallas kernels  15.7 us (32%)
  starting transfers between devices  12.4 us (25%)
  between operations  1.44 us (3%)
    all_to_all x1, blocking collectives, per_device(): lax.all_to_all(jnp.broadcast_to(dots, (nx * ny, NZ)), ('gx', 'gy'), 0, 0,...  19.9 us
    pallas_call x7, Pallas kernels, call(): pl.pallas_call(kernel, out_shape=out_shape, in_specs=[spec(s) for s in in...  15.7 us
    ppermute x4, starting transfers between devices, swap(): return (lax.ppermute(a_send, axis, one), lax.ppermute(b_send, axis, two))  12.4 us
  transfers between devices with their start and end apart: 4, of which 0 were waited for; matrix products, arithmetic and copies ran while one was open for 0% of the time, Pallas kernels for 21%

profile of v8, /device:TPU:1, one launch (start us, length us, event | category | flops | bytes accessed | tf_op | source)
XLA Modules:
  0.0 49.6 jit_solution(9902687958770088201)
XLA Ops:
  0.6 0.0 copy-start.3
  0.6 0.0 copy-start.2
  0.7 0.0 copy-start
  0.7 0.0 copy-start.1
  0.7 1.9 %shard_map.104 = (f32[2880,128]{1,0:T(8,128)S(1)}, f32[2880,128]{1,0:T(8,128)S(1)}, f32[144,128]{1,0:T(8,128)S(1)}, f32[144,128]{1,0:T(8,128)S(1)}) custom-call(s32[3,512]{1,0:T(4,128)} %bitcast.16, f32[3,512]{1,0:T(4,128)} %forces.1, f32[1536,128]{1,0:T(8,128)} %bitcast.13, s32[1536,128]{1,0:T(8,128)} %bitcast.14), custom_call_target="tpu_custom_call" | custom-call | flops 400000 | bytes 2400000 | tf_op jit(solution)/shard_map/pallas_call | solution.py:45
  2.5 2.5 %collective-permute-start = (f32[144,128]{1,0:T(8,128)S(1)}, f32[144,128]{1,0:T(8,128)S(1)}, u32[]{:S(2)}, u32[]{:S(2)}) collective-permute-start(f32[144,128]{1,0:T(8,128)S(1)} %get-tuple-element.25), channel_id=1, source_target_pairs={{0,7},{1,2},{2,1},{3,4},{4,3},{5,6},{6,5},{7,0},{8,15},{9,10},{10,... | collective-permute-start | bytes 221192 | tf_op jit(solution)/shard_map/ppermute | solution.py:696
  5.0 1.9 %collective-permute-start.1 = (f32[144,128]{1,0:T(8,128)S(1)}, f32[144,128]{1,0:T(8,128)S(1)}, u32[]{:S(2)}, u32[]{:S(2)}) collective-permute-start(f32[144,128]{1,0:T(8,128)S(1)} %get-tuple-element.26), channel_id=1, source_target_pairs={{0,1},{1,0},{2,3},{3,2},{4,5},{5,4},{6,7},{7,6},{8,9},{9,8},{10,11... | collective-permute-start | bytes 221192 | tf_op jit(solution)/shard_map/ppermute | solution.py:696
  7.6 0.0 copy-done.3
  7.6 0.0 copy-done.2
  7.6 0.0 copy-done
  7.6 0.0 copy-done.1
  7.6 1.8 %shard_map.105.coarse = f32[6,16,128]{2,1,0:T(8,128)S(1)} custom-call(f32[3,64]{1,0:T(4,128)S(1)} %copy-done.1, f32[3,128,128]{2,1,0:T(8,128)S(1)} %copy-done, f32[3,128]{1,0:T(4,128)S(1)} %copy-done.2, f32[1,128]{1,0:T(1,128)S(1)} %bitcast.12, f32[1,1]{1,0:T(1,128)} %bitcast.9.bout), custom_call_target="tpu_custom_call" | custom-call | flops 1500000000 | bytes 300000 | tf_op jit(solution)/shard_map/pallas_call | solution.py:45
  9.4 0.0 collective-permute-done
  9.4 0.0 collective-permute-done.1
  9.5 0.1 shard_map.108
  9.5 0.9 %collective-permute-start.2 = (f32[360,128]{1,0:T(8,128)S(1)}, f32[360,128]{1,0:T(8,128)S(1)}, u32[]{:S(2)}, u32[]{:S(2)}) collective-permute-start(f32[360,128]{1,0:T(8,128)S(1)} %get-tuple-element.37), channel_id=1, source_target_pairs={{0,8},{8,0},{16,24},{24,16},{32,40},{40,32},{48,56},{56,48},{64,72... | collective-permute-start | bytes 552968 | tf_op jit(solution)/shard_map/ppermute | solution.py:696
  10.5 7.1 %collective-permute-start.3 = (f32[360,128]{1,0:T(8,128)S(1)}, f32[360,128]{1,0:T(8,128)S(1)}, u32[]{:S(2)}, u32[]{:S(2)}) collective-permute-start(f32[360,128]{1,0:T(8,128)S(1)} %get-tuple-element.38), channel_id=1, source_target_pairs={{0,248},{8,16},{16,8},{24,32},{32,24},{40,48},{48,40},{56,64},{64,... | collective-permute-start | bytes 552968 | tf_op jit(solution)/shard_map/ppermute | solution.py:696
  17.6 1.5 %shard_map.106 = (f32[960,128]{1,0:T(8,128)S(1)}, f32[960,128]{1,0:T(8,128)S(1)}, f32[512,128]{1,0:T(8,128)}) custom-call(f32[6,16,128]{2,1,0:T(8,128)S(1)} %shard_map.105.coarse), custom_call_target="tpu_custom_call" | custom-call | flops 8000000 | bytes 1300000 | tf_op jit(solution)/shard_map/pallas_call | solution.py:45
  19.1 7.2 %shard_map.107 = (f32[2880,128]{1,0:T(8,128)S(1)}, f32[2880,128]{1,0:T(8,128)S(1)}, f32[2880,128]{1,0:T(8,128)S(1)}, f32[2880,128]{1,0:T(8,128)S(1)}, f32[2880,1...) custom-call(f32[2880,128]{1,0:T(8,128)S(1)} %get-tuple-element.23.lo, ...), custom_call_target="tpu_custom_call", output_to_operand_aliasing={{0}: (0, {}), {1}: (1, {})} | custom-call | flops 60000000 | bytes 9000000 | tf_op jit(solution)/shard_map/pallas_call | solution.py:45
  26.3 0.0 collective-permute-done.2.xa
  26.3 0.0 collective-permute-done.3.xb
  26.3 2.2 %shard_map.109 = (f32[2880,128]{1,0:T(8,128)S(1)}, f32[2880,128]{1,0:T(8,128)S(1)}, f32[2880,128]{1,0:T(8,128)S(1)}, f32[2880,128]{1,0:T(8,128)S(1)}, f32[2880,1...) custom-call(f32[2880,128]{1,0:T(8,128)S(1)} %get-tuple-element.29.lo, ...), custom_call_target="tpu_custom_call", output_to_operand_aliasing={{0}: (0, {}), {1}: (1, {}), {2}: (2, {}), {3}: (3, {}), {4}... | custom-call | tf_op jit(solution)/shard_map/pallas_call | solution.py:45
  28.5 0.1 broadcast_in_dim.10
  28.6 19.9 %all_to_all.8 = f32[256,1,128]{2,1,0:T(1,128)S(1)} all-to-all(f32[256,1,128]{2,1,0:T(1,128)S(1)} %broadcast_in_dim.10), channel_id=1, replica_groups=mesh['gx'=32,'gy'=8] {'gx','gy'}, dimensions={0} | all-to-all | bytes 262144 | tf_op jit(solution)/shard_map/all_to_all | solution.py:734
  48.5 1.1 %shard_map.110 = f32[1536,128]{1,0:T(8,128)} custom-call(f32[256,128]{1,0:T(8,128)S(1)} %bitcast.10, f32[2880,128]{1,0:T(8,128)S(1)} %get-tuple-element.41.z, f32[2880,128]{1,0:T(8,128)S(1)} %get-tuple-element.42.y), custom_call_target="tpu_custom_call" | custom-call | tf_op jit(solution)/shard_map/pallas_call | solution.py:45
  (1 shorter events, 0.0 us)
Async XLA Ops:
  0.6 6.9 %copy-start.3 = (f32[128]{0:T(128)S(1)}, f32[128]{0:T(128)}, u32[]{:S(2)}) copy-start(f32[128]{0:T(128)} %param.16) | copy-start | bytes 1540
  0.6 6.9 %copy-start.2 = (f32[3,128]{1,0:T(4,128)S(1)}, f32[3,128]{1,0:T(4,128)}, u32[]{:S(2)}) copy-start(f32[3,128]{1,0:T(4,128)} %biases.1) | copy-start | bytes 4612
  0.7 6.9 %copy-start = (f32[3,128,128]{2,1,0:T(8,128)S(1)}, f32[3,128,128]{2,1,0:T(8,128)}, u32[]{:S(2)}) copy-start(f32[3,128,128]{2,1,0:T(8,128)} %weights.1) | copy-start | bytes 589828
  0.7 6.9 %copy-start.1 = (f32[3,64]{1,0:T(4,128)S(1)}, f32[3,64]{1,0:T(4,128)}, u32[]{:S(2)}) copy-start(f32[3,64]{1,0:T(4,128)} %freq.1) | copy-start | bytes 2308
  2.5 6.9 %collective-permute-start = (f32[144,128]{1,0:T(8,128)S(1)}, f32[144,128]{1,0:T(8,128)S(1)}, u32[]{:S(2)}, u32[]{:S(2)}) collective-permute-start(f32[144,128]{1,0:T(8,128)S(1)} %get-tuple-element.25), channel_id=1, source_target_pairs={{0,7},{1,2},{2,1},{3,4},{4,3},{5,6},{6,5},{7,0},{8,15},{9,10},{10,... | collective-permute-start | bytes 221192 | tf_op jit(solution)/shard_map/ppermute | solution.py:696
  5.0 4.4 %collective-permute-start.1 = (f32[144,128]{1,0:T(8,128)S(1)}, f32[144,128]{1,0:T(8,128)S(1)}, u32[]{:S(2)}, u32[]{:S(2)}) collective-permute-start(f32[144,128]{1,0:T(8,128)S(1)} %get-tuple-element.26), channel_id=1, source_target_pairs={{0,1},{1,0},{2,3},{3,2},{4,5},{5,4},{6,7},{7,6},{8,9},{9,8},{10,11... | collective-permute-start | bytes 221192 | tf_op jit(solution)/shard_map/ppermute | solution.py:696
  9.5 16.8 %collective-permute-start.2 = (f32[360,128]{1,0:T(8,128)S(1)}, f32[360,128]{1,0:T(8,128)S(1)}, u32[]{:S(2)}, u32[]{:S(2)}) collective-permute-start(f32[360,128]{1,0:T(8,128)S(1)} %get-tuple-element.37), channel_id=1, source_target_pairs={{0,8},{8,0},{16,24},{24,16},{32,40},{40,32},{48,56},{56,48},{64,72... | collective-permute-start | bytes 552968 | tf_op jit(solution)/shard_map/ppermute | solution.py:696
  10.5 15.8 %collective-permute-start.3 = (f32[360,128]{1,0:T(8,128)S(1)}, f32[360,128]{1,0:T(8,128)S(1)}, u32[]{:S(2)}, u32[]{:S(2)}) collective-permute-start(f32[360,128]{1,0:T(8,128)S(1)} %get-tuple-element.38), channel_id=1, source_target_pairs={{0,248},{8,16},{16,8},{24,32},{32,24},{40,48},{48,40},{56,64},{64,... | collective-permute-start | bytes 552968 | tf_op jit(solution)/shard_map/ppermute | solution.py:696

commit v9 on v8

--- a/solution.py
+++ b/solution.py
@@ -570,12 +570,12 @@
     lax.fori_loop(CF, LAST + 1, prepare, 0, unroll=4)
     clear_row_past(first, LAST + 1)
     clear_edges(above)
-    operator_pass(zsum, zdiff, young, above, minus, plus, CF, LAST, 7)
+    operator_pass(zsum, zdiff, young, above, minus, plus, CF, LAST, 14)
     dots = lax.fori_loop(
         CF + 1, LAST, lambda x, d: stages.finish_one(second, x, d), [jnp.zeros((8, NZ), f32)] * 3, unroll=7
     )
     clear_row_past(second, LAST)
-    operator_pass(zsum2, zdiff2, young, above, minus, plus, CF + 1, LAST - 1, 6)
+    operator_pass(zsum2, zdiff2, young, above, minus, plus, CF + 1, LAST - 1, 12)
     dots = dots + lax.fori_loop(CF + 2, LAST - 1, stages.finish_two, [jnp.zeros((8, NZ), f32)], unroll=4)
     for k, d in enumerate(dots):
         dots_out[k] = d

time: 49.7 us -> 48.4 us (0.974)
  Pallas kernels: 15.7 us -> 13.9 us
  blocking collectives: 19.9 us -> 20.7 us
    pallas_call x7, Pallas kernels: 15.7 us -> 13.9 us  [call(): pl.pallas_call(kernel, out_shape=out_shape, in_specs=[spec(s) for s in in...]
    all_to_all x1, blocking collectives: 19.9 us -> 20.7 us  [per_device(): lax.all_to_all(jnp.broadcast_to(dots, (nx * ny, NZ)), ('gx', 'gy'), 0, 0,...]
  transfers between devices with their start and end apart: 4 -> 4, of which waited for: 0 -> 0; matrix products, arithmetic and copies ran while one was open for 0% -> 0% of each run, Pallas kernels for 21% -> 18%
where the time goes in v9:
time: 48.4 us; the launch traced here: 48.1 us
  blocking collectives  20.7 us (43%)
  Pallas kernels  13.9 us (29%)
  starting transfers between devices  12 us (25%)
  between operations  1.44 us (3%)
    all_to_all x1, blocking collectives, per_device(): lax.all_to_all(jnp.broadcast_to(dots, (nx * ny, NZ)), ('gx', 'gy'), 0, 0,...  20.7 us
    pallas_call x7, Pallas kernels, call(): pl.pallas_call(kernel, out_shape=out_shape, in_specs=[spec(s) for s in in...  13.9 us
    ppermute x4, starting transfers between devices, swap(): return (lax.ppermute(a_send, axis, one), lax.ppermute(b_send, axis, two))  12 us
  transfers between devices with their start and end apart: 4, of which 0 were waited for; matrix products, arithmetic and copies ran while one was open for 0% of the time, Pallas kernels for 18%

profile of v9, /device:TPU:1, one launch (start us, length us, event | category | flops | bytes accessed | tf_op | source)
XLA Modules:
  0.0 48.1 jit_solution(891349829229895343)
XLA Ops:
  0.6 0.0 copy-start.3
  0.6 0.0 copy-start.2
  0.7 0.0 copy-start
  0.7 0.0 copy-start.1
  0.7 2.1 %shard_map.104 = (f32[2880,128]{1,0:T(8,128)S(1)}, f32[2880,128]{1,0:T(8,128)S(1)}, f32[144,128]{1,0:T(8,128)S(1)}, f32[144,128]{1,0:T(8,128)S(1)}) custom-call(s32[3,512]{1,0:T(4,128)} %bitcast.16, f32[3,512]{1,0:T(4,128)} %forces.1, f32[1536,128]{1,0:T(8,128)} %bitcast.13, s32[1536,128]{1,0:T(8,128)} %bitcast.14), custom_call_target="tpu_custom_call" | custom-call | flops 400000 | bytes 2400000 | tf_op jit(solution)/shard_map/pallas_call | solution.py:45
  2.8 2.5 %collective-permute-start = (f32[144,128]{1,0:T(8,128)S(1)}, f32[144,128]{1,0:T(8,128)S(1)}, u32[]{:S(2)}, u32[]{:S(2)}) collective-permute-start(f32[144,128]{1,0:T(8,128)S(1)} %get-tuple-element.25), channel_id=1, source_target_pairs={{0,7},{1,2},{2,1},{3,4},{4,3},{5,6},{6,5},{7,0},{8,15},{9,10},{10,... | collective-permute-start | bytes 221192 | tf_op jit(solution)/shard_map/ppermute | solution.py:696
  5.3 1.4 %collective-permute-start.1 = (f32[144,128]{1,0:T(8,128)S(1)}, f32[144,128]{1,0:T(8,128)S(1)}, u32[]{:S(2)}, u32[]{:S(2)}) collective-permute-start(f32[144,128]{1,0:T(8,128)S(1)} %get-tuple-element.26), channel_id=1, source_target_pairs={{0,1},{1,0},{2,3},{3,2},{4,5},{5,4},{6,7},{7,6},{8,9},{9,8},{10,11... | collective-permute-start | bytes 221192 | tf_op jit(solution)/shard_map/ppermute | solution.py:696
  7.3 0.0 copy-done.3
  7.3 0.0 copy-done.2
  7.3 0.0 copy-done
  7.3 0.0 copy-done.1
  7.3 1.8 %shard_map.105.coarse = f32[6,16,128]{2,1,0:T(8,128)S(1)} custom-call(f32[3,64]{1,0:T(4,128)S(1)} %copy-done.1, f32[3,128,128]{2,1,0:T(8,128)S(1)} %copy-done, f32[3,128]{1,0:T(4,128)S(1)} %copy-done.2, f32[1,128]{1,0:T(1,128)S(1)} %bitcast.12, f32[1,1]{1,0:T(1,128)} %bitcast.9.bout), custom_call_target="tpu_custom_call" | custom-call | flops 1500000000 | bytes 300000 | tf_op jit(solution)/shard_map/pallas_call | solution.py:45
  9.2 0.0 collective-permute-done
  9.2 0.0 collective-permute-done.1
  9.2 0.1 shard_map.108
  9.3 1.2 %collective-permute-start.2 = (f32[360,128]{1,0:T(8,128)S(1)}, f32[360,128]{1,0:T(8,128)S(1)}, u32[]{:S(2)}, u32[]{:S(2)}) collective-permute-start(f32[360,128]{1,0:T(8,128)S(1)} %get-tuple-element.37), channel_id=1, source_target_pairs={{0,8},{8,0},{16,24},{24,16},{32,40},{40,32},{48,56},{56,48},{64,72... | collective-permute-start | bytes 552968 | tf_op jit(solution)/shard_map/ppermute | solution.py:696
  10.5 6.9 %collective-permute-start.3 = (f32[360,128]{1,0:T(8,128)S(1)}, f32[360,128]{1,0:T(8,128)S(1)}, u32[]{:S(2)}, u32[]{:S(2)}) collective-permute-start(f32[360,128]{1,0:T(8,128)S(1)} %get-tuple-element.38), channel_id=1, source_target_pairs={{0,248},{8,16},{16,8},{24,32},{32,24},{40,48},{48,40},{56,64},{64,... | collective-permute-start | bytes 552968 | tf_op jit(solution)/shard_map/ppermute | solution.py:696
  17.4 1.5 %shard_map.106 = (f32[960,128]{1,0:T(8,128)S(1)}, f32[960,128]{1,0:T(8,128)S(1)}, f32[512,128]{1,0:T(8,128)}) custom-call(f32[6,16,128]{2,1,0:T(8,128)S(1)} %shard_map.105.coarse), custom_call_target="tpu_custom_call" | custom-call | flops 8000000 | bytes 1300000 | tf_op jit(solution)/shard_map/pallas_call | solution.py:45
  18.9 5.1 %shard_map.107 = (f32[2880,128]{1,0:T(8,128)S(1)}, f32[2880,128]{1,0:T(8,128)S(1)}, f32[2880,128]{1,0:T(8,128)S(1)}, f32[2880,128]{1,0:T(8,128)S(1)}, f32[2880,1...) custom-call(f32[2880,128]{1,0:T(8,128)S(1)} %get-tuple-element.23.lo, ...), custom_call_target="tpu_custom_call", output_to_operand_aliasing={{0}: (0, {}), {1}: (1, {})} | custom-call | flops 60000000 | bytes 9000000 | tf_op jit(solution)/shard_map/pallas_call | solution.py:45
  24.0 0.0 collective-permute-done.2.xa
  24.1 0.0 collective-permute-done.3.xb
  24.1 2.2 %shard_map.109 = (f32[2880,128]{1,0:T(8,128)S(1)}, f32[2880,128]{1,0:T(8,128)S(1)}, f32[2880,128]{1,0:T(8,128)S(1)}, f32[2880,128]{1,0:T(8,128)S(1)}, f32[2880,1...) custom-call(f32[2880,128]{1,0:T(8,128)S(1)} %get-tuple-element.29.lo, ...), custom_call_target="tpu_custom_call", output_to_operand_aliasing={{0}: (0, {}), {1}: (1, {}), {2}: (2, {}), {3}: (3, {}), {4}... | custom-call | tf_op jit(solution)/shard_map/pallas_call | solution.py:45
  26.3 0.1 broadcast_in_dim.10
  26.3 20.7 %all_to_all.8 = f32[256,1,128]{2,1,0:T(1,128)S(1)} all-to-all(f32[256,1,128]{2,1,0:T(1,128)S(1)} %broadcast_in_dim.10), channel_id=1, replica_groups=mesh['gx'=32,'gy'=8] {'gx','gy'}, dimensions={0} | all-to-all | bytes 262144 | tf_op jit(solution)/shard_map/all_to_all | solution.py:734
  47.1 1.1 %shard_map.110 = f32[1536,128]{1,0:T(8,128)} custom-call(f32[256,128]{1,0:T(8,128)S(1)} %bitcast.10, f32[2880,128]{1,0:T(8,128)S(1)} %get-tuple-element.41.z, f32[2880,128]{1,0:T(8,128)S(1)} %get-tuple-element.42.y), custom_call_target="tpu_custom_call" | custom-call | tf_op jit(solution)/shard_map/pallas_call | solution.py:45
  (1 shorter events, 0.0 us)
Async XLA Ops:
  0.6 6.7 %copy-start.3 = (f32[128]{0:T(128)S(1)}, f32[128]{0:T(128)}, u32[]{:S(2)}) copy-start(f32[128]{0:T(128)} %param.16) | copy-start | bytes 1540
  0.6 6.7 %copy-start.2 = (f32[3,128]{1,0:T(4,128)S(1)}, f32[3,128]{1,0:T(4,128)}, u32[]{:S(2)}) copy-start(f32[3,128]{1,0:T(4,128)} %biases.1) | copy-start | bytes 4612
  0.7 6.7 %copy-start = (f32[3,128,128]{2,1,0:T(8,128)S(1)}, f32[3,128,128]{2,1,0:T(8,128)}, u32[]{:S(2)}) copy-start(f32[3,128,128]{2,1,0:T(8,128)} %weights.1) | copy-start | bytes 589828
  0.7 6.7 %copy-start.1 = (f32[3,64]{1,0:T(4,128)S(1)}, f32[3,64]{1,0:T(4,128)}, u32[]{:S(2)}) copy-start(f32[3,64]{1,0:T(4,128)} %freq.1) | copy-start | bytes 2308
  2.8 6.4 %collective-permute-start = (f32[144,128]{1,0:T(8,128)S(1)}, f32[144,128]{1,0:T(8,128)S(1)}, u32[]{:S(2)}, u32[]{:S(2)}) collective-permute-start(f32[144,128]{1,0:T(8,128)S(1)} %get-tuple-element.25), channel_id=1, source_target_pairs={{0,7},{1,2},{2,1},{3,4},{4,3},{5,6},{6,5},{7,0},{8,15},{9,10},{10,... | collective-permute-start | bytes 221192 | tf_op jit(solution)/shard_map/ppermute | solution.py:696
  5.3 3.9 %collective-permute-start.1 = (f32[144,128]{1,0:T(8,128)S(1)}, f32[144,128]{1,0:T(8,128)S(1)}, u32[]{:S(2)}, u32[]{:S(2)}) collective-permute-start(f32[144,128]{1,0:T(8,128)S(1)} %get-tuple-element.26), channel_id=1, source_target_pairs={{0,1},{1,0},{2,3},{3,2},{4,5},{5,4},{6,7},{7,6},{8,9},{9,8},{10,11... | collective-permute-start | bytes 221192 | tf_op jit(solution)/shard_map/ppermute | solution.py:696
  9.3 14.8 %collective-permute-start.2 = (f32[360,128]{1,0:T(8,128)S(1)}, f32[360,128]{1,0:T(8,128)S(1)}, u32[]{:S(2)}, u32[]{:S(2)}) collective-permute-start(f32[360,128]{1,0:T(8,128)S(1)} %get-tuple-element.37), channel_id=1, source_target_pairs={{0,8},{8,0},{16,24},{24,16},{32,40},{40,32},{48,56},{56,48},{64,72... | collective-permute-start | bytes 552968 | tf_op jit(solution)/shard_map/ppermute | solution.py:696
  10.5 13.5 %collective-permute-start.3 = (f32[360,128]{1,0:T(8,128)S(1)}, f32[360,128]{1,0:T(8,128)S(1)}, u32[]{:S(2)}, u32[]{:S(2)}) collective-permute-start(f32[360,128]{1,0:T(8,128)S(1)} %get-tuple-element.38), channel_id=1, source_target_pairs={{0,248},{8,16},{16,8},{24,32},{32,24},{40,48},{48,40},{56,64},{64,... | collective-permute-start | bytes 552968 | tf_op jit(solution)/shard_map/ppermute | solution.py:696
